TPU v7x, 32 devices: a whole 2x2x4 slice. The times are simulated.
32 devices in a mesh: param: 4 (over y, x), ex: 8 (over z, core).
Axes of the slice: x: 2, y: 2, z: 4, core: 2. Of those that a mesh axis runs over, the one named last changes fastest.
Arguments:
- activations: bfloat16 [64, 32, 4096], P('ex', None, 'param'), may hold values from -24 to 24
- output_gradients: bfloat16 [2, 64, 32, 4096], P(None, 'ex', None, 'param'), may hold values from -24 to 24
- down_projection_weight: bfloat16 [2, 16, 4096], P(None, None, 'param'), may hold values from -0.09375 to 0.09375
- adapter_up: bfloat16 [2, 4096, 16], P(None, 'param'), may hold values from -0.09375 to 0.09375
- projection: bfloat16 [262144, 4096], P(('param', 'ex')), may hold values from -0.111328125 to 0.111328125
- domains: int32 [64], P('ex'), may hold values from 0 to 3
- target_ids: int32 [256], P('param'), may hold values from 0 to 63
Outputs:
- scores: float32 [256, 64], P('param', 'ex')
- domain_scores: float32 [256, 4], P('param')
All inputs are finite; a program needn't handle non-finite values.
Results may differ from a plain program's by a relative error of at most 0.0059.
Values may be sent and summed in bfloat16 or wider, within the bound.
No kernel may reach another device: no remote copies, remote signals or barrier semaphores. Data moves between devices by JAX's collectives and lax.ppermute only.
A program may use at most 192 MiB of HBM per device.

v0:
```python
import math

import jax
import jax.numpy as jnp
from jax import lax
from jax.sharding import PartitionSpec as P

K = 4096
DOMAINS = 4


def inner_rows(left, right):
    return lax.dot_general(
        left,
        right,
        (((0,), (0,)), ((), ())),
        precision=lax.Precision.HIGHEST,
        preferred_element_type=jnp.float32,
    )


def local(
    activations,
    output_gradients,
    down_projection_weight,
    adapter_up,
    projection,
    domains,
    target_ids,
):
    single_float = jnp.float32
    ex_rows = activations.shape[0]
    adapter_rank_size = down_projection_weight.shape[1]
    up_terms = jnp.einsum(
        "ansd,adr->ansr", output_gradients, adapter_up, preferred_element_type=single_float
    )
    down_terms = jnp.einsum(
        "nsd,ard->ansr", activations, down_projection_weight, preferred_element_type=single_float
    )
    partial_low = jnp.concatenate([up_terms[0], up_terms[1], down_terms[0], down_terms[1]], axis=-1)
    rank_factor = lax.psum(partial_low, "param").astype(jnp.bfloat16)
    first = jnp.einsum(
        "erb,ery->eby",
        activations,
        rank_factor[..., : 2 * adapter_rank_size],
        preferred_element_type=single_float,
    )
    second = jnp.einsum(
        "fai,fav->fiv",
        output_gradients[0],
        rank_factor[..., 2 * adapter_rank_size : 3 * adapter_rank_size],
        preferred_element_type=single_float,
    )
    third = jnp.einsum(
        "fai,fav->fiv",
        output_gradients[1],
        rank_factor[..., 3 * adapter_rank_size :],
        preferred_element_type=single_float,
    )
    grads = jnp.concatenate([first, second, third], axis=-1).astype(jnp.bfloat16)
    grads = grads.reshape(ex_rows, grads.shape[1] * grads.shape[2])
    column_indices = lax.all_to_all(grads, "ex", split_axis=1, concat_axis=0, tiled=True)
    features = lax.psum_scatter(
        lax.dot_general(
            projection,
            column_indices,
            (((0,), (1,)), ((), ())),
            preferred_element_type=single_float,
        ),
        ("param", "ex"),
        scatter_dimension=0,
        tiled=True,
    )
    totals = lax.psum(jnp.sum(features * features, axis=0), ("param", "ex"))
    unit_rows = features * lax.rsqrt(totals + 1e-06)[None, :]
    gram = lax.psum(inner_rows(unit_rows, unit_rows), ("param", "ex"))
    example_count = gram.shape[0]
    kernel = gram + 0.25 * jnp.eye(example_count, dtype=single_float)
    lower = jnp.linalg.cholesky(kernel)
    first_row = lax.axis_index("ex") * ex_rows
    picks = (
        jnp.arange(example_count, dtype=jnp.int32)[:, None]
        == first_row + jnp.arange(ex_rows, dtype=jnp.int32)[None, :]
    ).astype(single_float)
    inverse_cols = jax.scipy.linalg.cho_solve((lower, True), picks)
    cross = jnp.take(gram, target_ids, axis=0)
    selfmask = target_ids[:, None] == jnp.arange(example_count, dtype=jnp.int32)[None, :]
    cross = jnp.where(selfmask, jnp.zeros_like(cross), cross)
    scores = math.sqrt(K) * jnp.dot(
        cross, inverse_cols, precision=lax.Precision.HIGHEST, preferred_element_type=single_float
    )
    indicator_matrix = (domains[:, None] == jnp.arange(DOMAINS, dtype=jnp.int32)[None, :]).astype(
        single_float
    )
    domain_partial_sums = jnp.dot(
        scores,
        indicator_matrix,
        precision=lax.Precision.HIGHEST,
        preferred_element_type=single_float,
    )
    domain_scores = lax.psum(domain_partial_sums, "ex") / math.sqrt(example_count / DOMAINS)
    return (scores, domain_scores)


def solution(mesh):
    in_specs = (
        P("ex", None, "param"),
        P(None, "ex", None, "param"),
        P(None, None, "param"),
        P(None, "param", None),
        P(("param", "ex"), None),
        P("ex"),
        P("param"),
    )
    out_specs = (P("param", "ex"), P("param", None))
    return jax.shard_map(local, mesh=mesh, in_specs=in_specs, out_specs=out_specs, check_vma=False)
```

profile of v0, /device:TPU:0, one launch (start us, length us, event | category | flops | bytes accessed | tf_op | source)
XLA Modules:
  0.0 345.9 jit_solution(10288716785213548179)
XLA Ops:
  7.2 0.0 copy-start
  7.2 0.0 copy-start.1
  7.2 0.0 reduce-scatter.2.cloned.1.call-start
  7.2 1.0 copy-done
  8.2 1.3 convolution_bitcast_fusion.1
  9.6 2.0 fusion.11
  11.7 22.6 %psum.28 = bf16[8,32,64]{1,2,0:T(8,128)(2,1)S(1)} all-reduce(f32[8,32,64]{1,2,0:T(8,128)S(1)} %pad_maximum_fusion.1), channel_id=1, replica_groups=mesh['param'=4,'ex'=8] {'param'}, use_global_device_ids=true, to_apply=%region_0.0 | all-reduce | flops 16384 | bytes 98304 | tf_op jit(solution)/shard_map/psum | solution.py:41
  34.3 0.3 fusion
  34.6 0.0 copy-done.1
  34.6 0.2 fusion.1
  34.8 0.2 fusion.2
  35.0 1.1 pad_maximum_fusion
  36.1 2.0 copy.13
  38.2 2.5 convert_element_type.13
  40.7 1.8 copy.14
  42.5 31.3 %all_to_all.16 = bf16[8,8,8192]{2,0,1:T(8,128)(2,1)S(1)} all-to-all(bf16[8,8,8192]{2,0,1:T(8,128)(2,1)S(1)} %copy.14), channel_id=1, replica_groups=mesh['param'=4,'ex'=8] {'ex'}, dimensions={1} | all-to-all | bytes 2097152 | tf_op jit(solution)/shard_map/all_to_all | solution.py:62
  73.7 0.0 copy-start.2
  73.7 0.0 copy-start.3
  73.7 24.4 %convolution_bitcast_fusion = f32[4096,64]{0,1:T(8,128)} fusion(bf16[8192,4096]{1,0:T(8,128)(2,1)} %param.11, bf16[8,8,8192]{2,0,1:T(8,128)(2,1)S(1)} %all_to_all.16), kind=kOutput, calls=%fused_computation.1 | convolution fusion | flops 4294967296 | bytes 69206016 | tf_op jit(solution)/shard_map/dot_general | solution.py:64
  98.1 0.0 reduce-scatter.2.cloned.1.call-update
  98.2 0.0 copy-done.2
  98.2 132.3 %reduce-scatter.2.cloned.1.call-done = f32[128,64]{0,1:T(8,128)} async-done(((f32[4096,64]{0,1:T(8,128)}), f32[128,64]{0,1:T(8,128)}) %reduce-scatter.2.cloned.1.call-update) | async-done | bytes 32784 | tf_op jit(solution)/shard_map/reduce_scatter | solution.py:63
  230.5 0.9 multiply_reduce_fusion
  231.3 36.9 %psum.29 = f32[64]{0:T(128)S(1)} all-reduce(f32[64]{0:T(128)S(1)} %multiply_reduce_fusion), channel_id=1, replica_groups=mesh['param'=4,'ex'=8] {'param','ex'}, use_global_device_ids=true, to_apply=%region_3.0 | all-reduce | flops 64 | bytes 512 | tf_op jit(solution)/shard_map/psum | solution.py:74
  268.2 1.1 fusion.23
  269.3 41.6 %psum.30 = f32[64,64]{1,0:T(8,128)S(1)} all-reduce(f32[64,64]{1,0:T(8,128)S(1)} %fusion.23), channel_id=1, replica_groups=mesh['param'=4,'ex'=8] {'param','ex'}, use_global_device_ids=true, to_apply=%region_4.0 | all-reduce | flops 4096 | bytes 32768 | tf_op jit(solution)/shard_map/psum | solution.py:76
  310.9 0.1 copy.15
  311.0 5.8 %cholesky.15 = f32[64,64]{1,0:T(8,128)S(1)} custom-call(f32[64,64]{1,0:T(8,128)S(1)} %fusion.20), custom_call_target="Cholesky" | custom-call | tf_op jit(solution)/shard_map/jit(cholesky)/cholesky | solution.py:79
  316.9 0.6 compare_reduce_fusion
  317.5 0.7 fusion.13
  318.2 4.9 %custom-call.10 = f32[1,64,64]{1,2,0:T(8,128)S(1)} custom-call(f32[1,64,64]{2,1,0:T(8,128)S(1)} %fusion.13), custom_call_target="InvertDiagBlocksLowerTriangular" | custom-call | tf_op jit(solution)/shard_map/jit(_cho_solve)/triangular_solve | solution.py:85
  323.1 0.2 fusion.18
  323.3 0.2 fusion.16
  323.5 0.6 gather_fusion
  324.1 0.2 convolution_multiply_fusion
  324.3 0.0 copy-done.3
  324.3 0.0 copy-start.4
  324.3 0.3 fusion.31
  324.6 13.9 %psum.31 = f32[64,4]{0,1:T(4,128)S(1)} all-reduce(f32[64,4]{0,1:T(4,128)S(1)} %fusion.31), channel_id=1, replica_groups=mesh['param'=4,'ex'=8] {'ex'}, use_global_device_ids=true, to_apply=%region_7.8 | all-reduce | flops 256 | bytes 2048 | tf_op jit(solution)/shard_map/psum | solution.py:101
  338.4 0.6 broadcast_multiply_fusion
  339.0 0.0 copy-done.4
  (10 shorter events, 0.1 us)
Async XLA Ops:
  7.2 1.0 copy-start
  7.2 27.4 %copy-start.1 = (bf16[2,8,32,1024]{3,2,1,0:T(8,128)(2,1)S(1)}, bf16[2,8,32,1024]{3,2,1,0:T(8,128)(2,1)}, u32[]{:S(2)}) copy-start(bf16[2,8,32,1024]{3,2,1,0:T(8,128)(2,1)} %param.8) | copy-start | bytes 3145732
  7.2 223.3 %reduce-scatter.2.cloned.1.call-start = ((), (), s32[]{:S(2)}) async-start(), calls=%async_computation.2 | async-start | bytes 1081344 | tf_op jit(solution)/shard_map/reduce_scatter | solution.py:63
  73.7 24.4 %copy-start.2 = (s32[64]{0:T(128)S(1)}, s32[64]{0:T(128)}, u32[]{:S(2)}) copy-start(s32[64]{0:T(128)} %param.13) | copy-start | bytes 772
  73.7 250.6 %copy-start.3 = (s32[8]{0:T(128)S(1)}, s32[8]{0:T(128)}, u32[]{:S(2)}) copy-start(s32[8]{0:T(128)} %param.12) | copy-start | bytes 100
  324.3 14.7 %copy-start.4 = (f32[64,8]{0,1:T(8,128)}, f32[64,8]{0,1:T(8,128)S(1)}, u32[]{:S(2)}) copy-start(f32[64,8]{0,1:T(8,128)S(1)} %convolution_multiply_fusion) | copy-start | bytes 6148
Sparse Core Ops, SparseCore 0:
  98.3 132.1 reduce-scatter.1
where the time goes:
time: 346 us
  blocking collectives  146 us (42%)
  waiting for transfers between devices  132 us (38%)
  matrix products  30.4 us (9%)
  other arithmetic  14.7 us (4%)
  between operations  14.2 us (4%)
  local copies, waits for them, and re-layouts  8.06 us (2%)
    reduce_scatter x1, waiting for transfers between devices, local(): lax.psum_scatter(lax.dot_general(projection, column_indices, (((0,), (1,)...  132 us
    psum x1, blocking collectives, local(): gram = lax.psum(inner_rows(unit_rows, unit_rows), ('param', 'ex'))  41.6 us
    psum x1, blocking collectives, local(): totals = lax.psum(jnp.sum(features * features, axis=0), ('param', 'ex'))  36.9 us
    all_to_all x1, blocking collectives, local(): lax.all_to_all(grads, 'ex', split_axis=1, concat_axis=0, tiled=True)  31.3 us
    dot_general x1, matrix products, local(): lax.dot_general(projection, column_indices, (((0,), (1,)), ((), ())), pre...  24.4 us
    psum x1, blocking collectives, local(): rank_factor = lax.psum(partial_low, 'param').astype(jnp.bfloat16)  22.6 us
    psum x1, blocking collectives, local(): lax.psum(domain_partial_sums, 'ex') / math.sqrt(example_count / DOMAINS)  13.9 us
  transfers between devices with their start and end apart: 1, of which 1 were waited for; matrix products, arithmetic and copies ran while one was open for 0% of the time, Pallas kernels for 0%

commit v1 on v0

v1 whole, which is shorter than its diff:
```python
import math

import jax
import jax.numpy as jnp
from jax import lax
from jax.sharding import PartitionSpec as P

K = 4096
DOMAINS = 4
EVERY = ("param", "ex")


def exact_dot(left, right, dims):
    return lax.dot_general(
        left, right, (dims, ((), ())), precision=lax.Precision.HIGHEST, preferred_element_type=jnp.float32
    )


def swap(blocks, axes):
    return lax.all_to_all(blocks, axes, split_axis=0, concat_axis=0, tiled=True)


def local(
    activations,
    output_gradients,
    down_projection_weight,
    adapter_up,
    projection,
    domains,
    target_ids,
):
    single_float = jnp.float32
    ex_rows = activations.shape[0]
    rank = down_projection_weight.shape[1]
    ex_size = lax.axis_size("ex")
    devices = lax.axis_size("param") * ex_size
    example_count = ex_rows * ex_size

    up_terms = jnp.einsum(
        "ansd,adr->ansr", output_gradients, adapter_up, preferred_element_type=single_float
    )
    down_terms = jnp.einsum(
        "nsd,ard->ansr", activations, down_projection_weight, preferred_element_type=single_float
    )
    partial_low = jnp.concatenate([up_terms[0], up_terms[1], down_terms[0], down_terms[1]], axis=-1)
    low = jnp.sum(lax.all_gather(partial_low, "param"), axis=0).astype(jnp.bfloat16)

    first = jnp.einsum(
        "erb,ery->eby", activations, low[..., : 2 * rank], preferred_element_type=single_float
    )
    second = jnp.einsum(
        "fai,fav->fiv",
        output_gradients[0],
        low[..., 2 * rank : 3 * rank],
        preferred_element_type=single_float,
    )
    third = jnp.einsum(
        "fai,fav->fiv", output_gradients[1], low[..., 3 * rank :], preferred_element_type=single_float
    )
    grads = jnp.concatenate([first, second, third], axis=-1).astype(jnp.bfloat16)
    grads = grads.reshape(ex_rows, grads.shape[1] * grads.shape[2])
    grads = lax.all_to_all(grads, "ex", split_axis=1, concat_axis=0, tiled=True)

    partial_features = jnp.dot(grads, projection, preferred_element_type=single_float)
    blocks = partial_features.astype(jnp.bfloat16).reshape(example_count, devices, K // devices)
    features = jnp.sum(swap(blocks.transpose(1, 0, 2), EVERY).astype(single_float).reshape(
        devices, example_count, K // devices), axis=0)

    raw_gram = exact_dot(features, features, ((1,), (1,)))
    rows = example_count // devices
    raw_rows = jnp.sum(swap(raw_gram, EVERY).reshape(devices, rows, example_count), axis=0)
    domain_row = jnp.pad(domains.astype(single_float), (0, example_count - ex_rows))
    piece = jnp.concatenate([raw_rows, domain_row[None]], axis=0)
    pieces = swap(jnp.broadcast_to(piece[None], (devices, rows + 1, example_count)), EVERY)
    raw_gram = pieces[:, :rows].reshape(example_count, example_count)
    all_domains = pieces[:ex_size, rows, :ex_rows].reshape(example_count).astype(jnp.int32)

    eye = jnp.eye(example_count, dtype=single_float)
    inverse_norm = lax.rsqrt(jnp.sum(raw_gram * eye, axis=0) + 1e-06)
    gram = raw_gram * inverse_norm[:, None] * inverse_norm[None, :]
    lower = jnp.linalg.cholesky(gram + 0.25 * eye)
    inverse = jax.scipy.linalg.cho_solve((lower, True), eye)
    cross = jnp.take(gram, target_ids, axis=0)
    selfmask = target_ids[:, None] == jnp.arange(example_count, dtype=jnp.int32)[None, :]
    cross = jnp.where(selfmask, jnp.zeros_like(cross), cross)
    scores = math.sqrt(K) * exact_dot(cross, inverse, ((1,), (0,)))
    indicator = (all_domains[:, None] == jnp.arange(DOMAINS, dtype=jnp.int32)[None, :]).astype(single_float)
    domain_scores = exact_dot(scores, indicator, ((1,), (0,))) / math.sqrt(example_count / DOMAINS)
    first_row = lax.axis_index("ex") * ex_rows
    return (lax.dynamic_slice_in_dim(scores, first_row, ex_rows, axis=1), domain_scores)


def solution(mesh):
    in_specs = (
        P("ex", None, "param"),
        P(None, "ex", None, "param"),
        P(None, None, "param"),
        P(None, "param", None),
        P(("param", "ex"), None),
        P("ex"),
        P("param"),
    )
    out_specs = (P("param", "ex"), P("param", None))
    return jax.shard_map(local, mesh=mesh, in_specs=in_specs, out_specs=out_specs, check_vma=False)
```

time: 346 us -> 139 us (0.40)
  blocking collectives: 146 us -> 42.9 us
  waiting for transfers between devices: 132 us -> 30.6 us
  between operations: 14.2 us -> 0.93 us
  starting transfers between devices: 0.04 us -> 7.73 us
  local copies, waits for them, and re-layouts: 8.06 us -> 12 us
    reduce_scatter x1 -> x0, waiting for transfers between devices: 132 us -> none  [local(): lax.psum_scatter(lax.dot_general(projection, column_indices, (((0,), (1,)...]
    psum x4 -> x0, blocking collectives: 115 us -> none  [the longest x1 41.6 us: local(): gram = lax.psum(inner_rows(unit_rows, unit_rows), ('param', 'ex'))]
    all_to_all x0 -> x3, waiting for transfers between devices: none -> 30.6 us  [swap(): return lax.all_to_all(blocks, axes, split_axis=0, concat_axis=0, tiled=True)]
    all_gather x0 -> x1, blocking collectives: none -> 11.6 us  [local(): lax.all_gather(partial_low, 'param')]
    all_to_all x0 -> x3, starting transfers between devices: none -> 7.73 us  [swap(): return lax.all_to_all(blocks, axes, split_axis=0, concat_axis=0, tiled=True)]
  transfers between devices with their start and end apart: 1 -> 3, of which waited for: 1 -> 3; matrix products, arithmetic and copies ran while one was open for 0% -> 0% of each run, Pallas kernels for 0% -> 0%
where the time goes in v1:
time: 139 us; the launch traced here: 138 us
  blocking collectives  42.9 us (31%)
  waiting for transfers between devices  30.6 us (22%)
  matrix products  29.2 us (21%)
  other arithmetic  15.1 us (11%)
  local copies, waits for them, and re-layouts  12 us (9%)
  starting transfers between devices  7.73 us (6%)
    all_to_all x1, blocking collectives, local(): grads = lax.all_to_all(grads, 'ex', split_axis=1, concat_axis=0, tiled=True)  31.3 us
    all_to_all x3, waiting for transfers between devices, swap(): return lax.all_to_all(blocks, axes, split_axis=0, concat_axis=0, tiled=True)  30.6 us
    dot_general x1, matrix products, local(): jnp.dot(grads, projection, preferred_element_type=single_float)  23.4 us
    all_gather x1, blocking collectives, local(): lax.all_gather(partial_low, 'param')  11.6 us
    all_to_all x3, starting transfers between devices, swap(): return lax.all_to_all(blocks, axes, split_axis=0, concat_axis=0, tiled=True)  7.73 us
    another operation x3, other arithmetic, local(): lower = jnp.linalg.cholesky(gram + 0.25 * eye)  6.52 us
    another operation x2, other arithmetic, local(): inverse = jax.scipy.linalg.cho_solve((lower, True), eye)  5.55 us
    convert_element_type x2, local copies, waits for them, and re-layouts, local(): jnp.concatenate([first, second, third], axis=-1).astype(jnp.bfloat16)  4.31 us
  transfers between devices with their start and end apart: 3, of which 3 were waited for; matrix products, arithmetic and copies ran while one was open for 0% of the time, Pallas kernels for 0%

profile of v1, /device:TPU:0, one launch (start us, length us, event | category | flops | bytes accessed | tf_op | source)
XLA Modules:
  0.0 138.5 jit_solution(5921641653240655357)
XLA Ops:
  0.6 0.0 copy-start
  0.6 1.0 copy-done
  1.7 1.3 convolution_bitcast_fusion
  3.0 2.0 %fusion.12 = f32[2,8,32,16]{2,3,1,0:T(8,128)S(1)} fusion(bf16[2,8,32,1024]{3,2,1,0:T(8,128)(2,1)} %param.8, bf16[2,1024,16]{1,2,0:T(8,128)(2,1)} %param.10), kind=kOutput, calls=%fused_computation.28 | convolution fusion | flops 16777216 | bytes 1146880 | tf_op jit(solution)/shard_map/ansd,adr->ansr/dot_general | solution.py:39
  5.1 0.1 copy.23
  5.2 11.6 %all-gather = f32[32,32,64]{2,1,0:T(8,128)S(1)} all-gather(f32[8,32,64]{2,1,0:T(8,128)S(1)} %copy.23), channel_id=2, replica_groups=mesh['param'=4,'ex'=8] {'param'}, dimensions={0}, use_global_device_ids=true | all-gather | bytes 327680 | tf_op jit(solution)/shard_map/all_gather | solution.py:46
  16.9 0.1 copy.24
  17.1 0.3 fusion
  17.3 0.2 fusion.2
  17.6 0.2 fusion.3
  17.8 1.1 pad_maximum_fusion
  18.9 2.0 %copy.25 = bf16[8,1024,64]{2,1,0:T(8,128)(2,1)S(1)} copy(bf16[8,1024,64]{1,2,0:T(8,128)(2,1)} %pad_maximum_fusion) | data formatting | bytes 2097152 | tf_op jit(solution)/shard_map/concatenate | solution.py:60
  20.9 2.5 %convert_element_type.33 = bf16[8,8,8192]{2,1,0:T(8,128)(2,1)} reshape(bf16[8,1024,64]{2,1,0:T(8,128)(2,1)S(1)} %copy.25) | data formatting | bytes 2097152 | tf_op jit(solution)/shard_map/convert_element_type | solution.py:60
  23.4 1.8 %copy.26 = bf16[8,8,8192]{2,0,1:T(8,128)(2,1)S(1)} copy(bf16[8,8,8192]{2,1,0:T(8,128)(2,1)} %convert_element_type.33) | data formatting | bytes 2097152 | tf_op jit(solution)/shard_map/convert_element_type | solution.py:60
  25.2 31.3 %all_to_all.32 = bf16[8,8,8192]{2,0,1:T(8,128)(2,1)S(1)} all-to-all(bf16[8,8,8192]{2,0,1:T(8,128)(2,1)S(1)} %copy.26), channel_id=1, replica_groups=mesh['param'=4,'ex'=8] {'ex'}, dimensions={1} | all-to-all | bytes 2097152 | tf_op jit(solution)/shard_map/all_to_all | solution.py:62
  56.5 23.4 %fusion.1 = bf16[8,32,8,128]{3,2,1,0:T(8,128)(2,1)S(1)} fusion(bf16[8192,4096]{1,0:T(8,128)(2,1)} %param.11, bf16[8,8,8192]{2,0,1:T(8,128)(2,1)S(1)} %all_to_all.32), kind=kOutput, calls=%fused_computation.4 | convolution fusion | flops 4295229440 | bytes 68681728 | tf_op jit(solution)/shard_map/dot_general | solution.py:64
  79.9 0.0 copy-start.2
  79.9 0.0 copy-start.3
  79.9 0.9 copy.37
  80.9 2.6 %all-to-all-start.1 = ((bf16[32,64,128]{2,1,0:T(8,128)(2,1)}), bf16[32,64,128]{2,1,0:T(8,128)(2,1)S(1)}, u32[]{:S(2)}, u32[]{:S(2)}) async-start(bf16[32,64,128]{2,1,0:T(8,128)(2,1)} %bitcast.72), calls=%async_computation.1 | async-start | bytes 1048576 | tf_op jit(solution)/shard_map/all_to_all | solution.py:20
  83.6 16.3 %all-to-all-done.1 = bf16[32,64,128]{2,1,0:T(8,128)(2,1)S(1)} async-done(((bf16[32,64,128]{2,1,0:T(8,128)(2,1)}), bf16[32,64,128]{2,1,0:T(8,128)(2,1)S(1)}, u32[]{:S(2)}, u32[]{:S(2)}) %all-to-all-start.1) | async-done | bytes 524320 | tf_op jit(solution)/shard_map/all_to_all | solution.py:20
  99.8 0.1 convert_reduce_fusion
  99.9 0.2 fusion.23
  100.1 0.7 reshape.89
  100.8 2.6 %all-to-all-start.2 = ((f32[32,1,128]{2,1,0:T(1,128)}), f32[32,1,128]{2,1,0:T(1,128)S(1)}, u32[]{:S(2)}, u32[]{:S(2)}) async-start(f32[32,1,128]{2,1,0:T(1,128)} %reshape.89), calls=%async_computation.2 | async-start | bytes 32768 | tf_op jit(solution)/shard_map/all_to_all | solution.py:20
  103.4 7.1 %all-to-all-done.2 = f32[32,1,128]{2,1,0:T(1,128)S(1)} async-done(((f32[32,1,128]{2,1,0:T(1,128)}), f32[32,1,128]{2,1,0:T(1,128)S(1)}, u32[]{:S(2)}, u32[]{:S(2)}) %all-to-all-start.2) | async-done | bytes 16416 | tf_op jit(solution)/shard_map/all_to_all | solution.py:20
  110.5 0.5 broadcast.108
  111.1 0.7 reduce.12
  111.8 0.1 reshape.90
  111.9 0.7 reshape.91
  112.6 2.6 %all-to-all-start.3 = ((f32[32,1,192]{2,1,0:T(1,128)}), f32[32,1,192]{2,1,0:T(1,128)S(1)}, u32[]{:S(2)}, u32[]{:S(2)}) async-start(f32[32,1,192]{2,1,0:T(1,128)} %reshape.91), calls=%async_computation.3 | async-start | bytes 65536 | tf_op jit(solution)/shard_map/all_to_all | solution.py:20
  115.2 7.2 %all-to-all-done.3 = f32[32,1,192]{2,1,0:T(1,128)S(1)} async-done(((f32[32,1,192]{2,1,0:T(1,128)}), f32[32,1,192]{2,1,0:T(1,128)S(1)}, u32[]{:S(2)}, u32[]{:S(2)}) %all-to-all-start.3) | async-done | bytes 24608 | tf_op jit(solution)/shard_map/all_to_all | solution.py:20
  122.4 0.7 reduce.13
  123.2 0.1 reshape.92
  123.3 0.1 fusion.36
  123.4 0.1 select_add_fusion
  123.5 0.1 copy.30
  123.6 5.8 %cholesky.16 = f32[64,64]{1,0:T(8,128)S(1)} custom-call(f32[64,64]{1,0:T(8,128)S(1)} %fusion.22), custom_call_target="Cholesky" | custom-call | tf_op jit(solution)/shard_map/jit(cholesky)/cholesky | solution.py:81
  129.5 0.6 compare_reduce_fusion
  130.1 0.7 fusion.14
  130.8 4.9 %custom-call.10 = f32[1,64,64]{1,2,0:T(8,128)S(1)} custom-call(f32[1,64,64]{2,1,0:T(8,128)S(1)} %fusion.14), custom_call_target="InvertDiagBlocksLowerTriangular" | custom-call | tf_op jit(solution)/shard_map/jit(_cho_solve)/triangular_solve | solution.py:82
  135.7 0.2 fusion.20
  135.9 0.2 fusion.18
  136.1 0.6 gather_fusion
  136.7 0.1 convert_element_type.38
  136.8 0.3 convolution_multiply_fusion
  137.0 0.8 convolution_multiply_fusion.1
  137.9 0.6 constant_dynamic-slice_fusion
  (21 shorter events, 0.3 us)
Async XLA Ops:
  0.6 1.0 copy-start
  5.0 12.3 %copy-start.1 = (bf16[2,8,32,1024]{3,2,1,0:T(8,128)(2,1)S(1)}, bf16[2,8,32,1024]{3,2,1,0:T(8,128)(2,1)}, u32[]{:S(2)}) copy-start(bf16[2,8,32,1024]{3,2,1,0:T(8,128)(2,1)} %param.8) | copy-start | bytes 3145732
  79.9 3.6 %copy-start.2 = (s32[8]{0:T(128)S(1)}, s32[8]{0:T(128)}, u32[]{:S(2)}) copy-start(s32[8]{0:T(128)} %param.12) | copy-start | bytes 100
  79.9 3.6 %copy-start.3 = (s32[64]{0:T(128)S(1)}, s32[64]{0:T(128)}, u32[]{:S(2)}) copy-start(s32[64]{0:T(128)} %param.13) | copy-start | bytes 772
  80.9 19.0 %all-to-all-start.1 = ((bf16[32,64,128]{2,1,0:T(8,128)(2,1)}), bf16[32,64,128]{2,1,0:T(8,128)(2,1)S(1)}, u32[]{:S(2)}, u32[]{:S(2)}) async-start(bf16[32,64,128]{2,1,0:T(8,128)(2,1)} %bitcast.72), calls=%async_computation.1 | async-start | bytes 1048576 | tf_op jit(solution)/shard_map/all_to_all | solution.py:20
  100.8 9.7 %all-to-all-start.2 = ((f32[32,1,128]{2,1,0:T(1,128)}), f32[32,1,128]{2,1,0:T(1,128)S(1)}, u32[]{:S(2)}, u32[]{:S(2)}) async-start(f32[32,1,128]{2,1,0:T(1,128)} %reshape.89), calls=%async_computation.2 | async-start | bytes 32768 | tf_op jit(solution)/shard_map/all_to_all | solution.py:20
  112.6 9.8 %all-to-all-start.3 = ((f32[32,1,192]{2,1,0:T(1,128)}), f32[32,1,192]{2,1,0:T(1,128)S(1)}, u32[]{:S(2)}, u32[]{:S(2)}) async-start(f32[32,1,192]{2,1,0:T(1,128)} %reshape.91), calls=%async_computation.3 | async-start | bytes 65536 | tf_op jit(solution)/shard_map/all_to_all | solution.py:20

commit v2 on v1

--- a/solution.py
+++ b/solution.py
@@ -1,12 +1,16 @@
+import functools
 import math
 
 import jax
 import jax.numpy as jnp
 from jax import lax
+from jax.experimental import pallas as pl
+from jax.experimental.pallas import tpu as pltpu
 from jax.sharding import PartitionSpec as P
 
 K = 4096
 DOMAINS = 4
+HALF = 32
 EVERY = ("param", "ex")
 
 
@@ -18,6 +22,108 @@
 
 def swap(blocks, axes):
     return lax.all_to_all(blocks, axes, split_axis=0, concat_axis=0, tiled=True)
+
+
+def packs(example_count):
+    return example_count == 2 * HALF
+
+
+def packed_gram_kernel(blocks_ref, row_ref, out_ref):
+    features = jnp.sum(blocks_ref[...].astype(jnp.float32), axis=0)
+    gram = exact_dot(features, features, ((1,), (1,)))
+    upper, across, under = gram[:HALF, :HALF], gram[:HALF, HALF:], gram[HALF:, HALF:]
+    rows = lax.broadcasted_iota(jnp.int32, (HALF, HALF), 0)
+    cols = lax.broadcasted_iota(jnp.int32, (HALF, HALF), 1)
+    mixed = jnp.where(rows <= cols, upper, under)
+    quarter = HALF // 2
+    body = jnp.concatenate([across[:quarter], across[quarter:], mixed[:quarter], mixed[quarter:]], axis=1)
+    diagonal = jnp.sum(jnp.where(rows == cols, under, 0.0), axis=0, keepdims=True)
+    last = row_ref[...] + jnp.concatenate([diagonal, jnp.zeros((1, 128 - HALF), jnp.float32)], axis=1)
+    piece = jnp.concatenate([body, jnp.broadcast_to(last, (8, 128))], axis=0)
+    out_ref[...] = jnp.broadcast_to(piece[None], out_ref.shape)
+
+
+def packed_gram(blocks, row):
+    return pl.pallas_call(
+        packed_gram_kernel,
+        out_shape=jax.ShapeDtypeStruct((blocks.shape[0], HALF // 2 + 8, 128), jnp.float32),
+        name="packed_gram",
+    )(blocks, row)
+
+
+def unpack(total):
+    quarter = HALF // 2
+    rows = lax.broadcasted_iota(jnp.int32, (HALF, HALF), 0)
+    cols = lax.broadcasted_iota(jnp.int32, (HALF, HALF), 1)
+    body = total[:quarter]
+    across = jnp.concatenate([body[:, :HALF], body[:, HALF : 2 * HALF]], axis=0)
+    mixed = jnp.concatenate([body[:, 2 * HALF : 3 * HALF], body[:, 3 * HALF :]], axis=0)
+    turned = mixed.T
+    upper = jnp.where(rows <= cols, mixed, turned)
+    diagonal = jnp.broadcast_to(total[quarter : quarter + 1, :HALF], (HALF, HALF))
+    under = jnp.where(rows == cols, diagonal, jnp.where(rows > cols, mixed, turned))
+    gram = jnp.concatenate(
+        [jnp.concatenate([upper, across], axis=1), jnp.concatenate([across.T, under], axis=1)], axis=0
+    )
+    return gram, total[quarter : quarter + 1, HALF : 3 * HALF]
+
+
+def solve_kernel(count, slot_ref, pieces_ref, ids_ref, scores_ref, domain_ref, work_ref):
+    total = jnp.sum(pieces_ref[...], axis=0)
+    if packs(count):
+        raw_gram, all_domains = unpack(total)
+    else:
+        raw_gram, all_domains = total[:count], total[count : count + 1]
+    rows = lax.broadcasted_iota(jnp.int32, (count, count), 0)
+    cols = lax.broadcasted_iota(jnp.int32, (count, count), 1)
+    on_diagonal = jnp.where(rows == cols, raw_gram, 0.0)
+    gram = raw_gram * lax.rsqrt(jnp.sum(on_diagonal, axis=1, keepdims=True) + 1e-06)
+    gram = gram * lax.rsqrt(jnp.sum(on_diagonal, axis=0, keepdims=True) + 1e-06)
+
+    work_ref[...] = gram + jnp.where(rows == cols, 0.25, 0.0)
+
+    def sweep(k, carry):
+        held = work_ref[...]
+        row = work_ref[pl.ds(k, 1), :]
+        pivot = 1.0 / jnp.sum(jnp.where(cols[:1] == k, row, 0.0), axis=1, keepdims=True)
+        column = jnp.sum(jnp.where(cols == k, held, 0.0), axis=1, keepdims=True)
+        row = jnp.where(cols[:1] == k, -pivot, row * pivot)
+        column = jnp.where(rows[:, :1] == k, -1.0, column)
+        work_ref[...] = jnp.where((cols == k) | (rows == k), 0.0, held) - column * row
+        return carry
+
+    lax.fori_loop(0, count, sweep, 0)
+
+    targets = ids_ref.shape[1]
+    places = lax.broadcasted_iota(jnp.int32, (count, targets), 0)
+    chosen = places == ids_ref[...]
+    cross = exact_dot(gram, jnp.where(chosen, 1.0, 0.0), ((1,), (0,)))
+    cross = jnp.where(chosen, 0.0, cross)
+    scores = exact_dot(work_ref[...], cross, ((1,), (0,))) * -math.sqrt(K)
+    kinds = lax.broadcasted_iota(jnp.int32, (DOMAINS, count), 0).astype(jnp.float32)
+    indicator = jnp.where(kinds == all_domains, 1.0, 0.0)
+    domain_ref[...] = exact_dot(indicator, scores, ((1,), (0,))) / math.sqrt(count / DOMAINS)
+    work_ref[:, :targets] = scores
+    scores_ref[...] = work_ref[pl.ds(pl.multiple_of(slot_ref[0], 8), scores_ref.shape[0]), :targets]
+
+
+def solve(pieces, target_ids, slot, ex_rows, count):
+    targets = target_ids.shape[0]
+    return pl.pallas_call(
+        functools.partial(solve_kernel, count),
+        out_shape=(
+            jax.ShapeDtypeStruct((ex_rows, targets), jnp.float32),
+            jax.ShapeDtypeStruct((DOMAINS, targets), jnp.float32),
+        ),
+        in_specs=[
+            pl.BlockSpec(memory_space=pltpu.SMEM),
+            pl.BlockSpec(memory_space=pltpu.VMEM),
+            pl.BlockSpec(memory_space=pltpu.VMEM),
+        ],
+        out_specs=(pl.BlockSpec(memory_space=pltpu.VMEM), pl.BlockSpec(memory_space=pltpu.VMEM)),
+        scratch_shapes=[pltpu.VMEM((count, count), jnp.float32)],
+        name="solve",
+    )(jnp.reshape(slot, (1,)), pieces, target_ids[None])
 
 
 def local(
@@ -63,31 +169,24 @@
 
     partial_features = jnp.dot(grads, projection, preferred_element_type=single_float)
     blocks = partial_features.astype(jnp.bfloat16).reshape(example_count, devices, K // devices)
-    features = jnp.sum(swap(blocks.transpose(1, 0, 2), EVERY).astype(single_float).reshape(
-        devices, example_count, K // devices), axis=0)
-
-    raw_gram = exact_dot(features, features, ((1,), (1,)))
-    rows = example_count // devices
-    raw_rows = jnp.sum(swap(raw_gram, EVERY).reshape(devices, rows, example_count), axis=0)
-    domain_row = jnp.pad(domains.astype(single_float), (0, example_count - ex_rows))
-    piece = jnp.concatenate([raw_rows, domain_row[None]], axis=0)
-    pieces = swap(jnp.broadcast_to(piece[None], (devices, rows + 1, example_count)), EVERY)
-    raw_gram = pieces[:, :rows].reshape(example_count, example_count)
-    all_domains = pieces[:ex_size, rows, :ex_rows].reshape(example_count).astype(jnp.int32)
-
-    eye = jnp.eye(example_count, dtype=single_float)
-    inverse_norm = lax.rsqrt(jnp.sum(raw_gram * eye, axis=0) + 1e-06)
-    gram = raw_gram * inverse_norm[:, None] * inverse_norm[None, :]
-    lower = jnp.linalg.cholesky(gram + 0.25 * eye)
-    inverse = jax.scipy.linalg.cho_solve((lower, True), eye)
-    cross = jnp.take(gram, target_ids, axis=0)
-    selfmask = target_ids[:, None] == jnp.arange(example_count, dtype=jnp.int32)[None, :]
-    cross = jnp.where(selfmask, jnp.zeros_like(cross), cross)
-    scores = math.sqrt(K) * exact_dot(cross, inverse, ((1,), (0,)))
-    indicator = (all_domains[:, None] == jnp.arange(DOMAINS, dtype=jnp.int32)[None, :]).astype(single_float)
-    domain_scores = exact_dot(scores, indicator, ((1,), (0,))) / math.sqrt(example_count / DOMAINS)
-    first_row = lax.axis_index("ex") * ex_rows
-    return (lax.dynamic_slice_in_dim(scores, first_row, ex_rows, axis=1), domain_scores)
+    arrived = swap(blocks.transpose(1, 0, 2), EVERY)
+
+    slot = lax.axis_index("ex") * ex_rows
+    mine = jnp.where(lax.axis_index("param") == 0, domains, 0).astype(single_float)
+    domain_row = lax.dynamic_update_slice(jnp.zeros((example_count,), single_float), mine, (slot,))
+    if packs(example_count):
+        row = jnp.pad(domain_row, (HALF, 128 - HALF - example_count))[None]
+        pieces = swap(packed_gram(arrived, row), EVERY)
+    else:
+        features = jnp.sum(arrived.astype(single_float), axis=0)
+        gram = exact_dot(features, features, ((1,), (1,)))
+        gram = jnp.concatenate([gram, jnp.broadcast_to(domain_row, (devices, example_count))], axis=0)
+        share = gram.shape[0] // devices
+        summed = jnp.sum(swap(gram, EVERY).reshape(devices, share, example_count), axis=0)
+        pieces = swap(jnp.broadcast_to(summed[None], (devices, share, example_count)), EVERY)
+        pieces = pieces.reshape(1, devices * share, example_count)
+    scores, domain_scores = solve(pieces, target_ids, slot, ex_rows, example_count)
+    return (scores.T, domain_scores.T)
 
 
 def solution(mesh):

time: 139 us -> 129 us (0.928)
  blocking collectives: 42.9 us -> 59.7 us
  waiting for transfers between devices: 30.6 us -> 15.6 us
  other arithmetic: 15.1 us -> 1.26 us
  Pallas kernels: 0 us -> 10.9 us
  starting transfers between devices: 7.73 us -> 2.6 us
  local copies, waits for them, and re-layouts: 12 us -> 9.94 us
  matrix products: 29.2 us -> 27.5 us
    all_to_all x0 -> x1, blocking collectives: none -> 16.8 us  [swap(): return lax.all_to_all(blocks, axes, split_axis=0, concat_axis=0, tiled=True)]
    all_to_all x3 -> x1, waiting for transfers between devices: 30.6 us -> 15.6 us  [swap(): return lax.all_to_all(blocks, axes, split_axis=0, concat_axis=0, tiled=True)]
    another operation x5 -> x0, other arithmetic: 12.1 us -> none  [the longest x3 6.52 us: local(): lower = jnp.linalg.cholesky(gram + 0.25 * eye)]
    pallas_call x0 -> x2, Pallas kernels: none -> 10.9 us  [the longest x1 8.72 us: solve(): pl.pallas_call(functools.partial(solve_kernel, count), out_shape=(jax.Sha...]
    all_to_all x3 -> x1, starting transfers between devices: 7.73 us -> 2.6 us  [swap(): return lax.all_to_all(blocks, axes, split_axis=0, concat_axis=0, tiled=True)]
    all_to_all x2 -> x0, other arithmetic: 1.4 us -> none  [swap(): return lax.all_to_all(blocks, axes, split_axis=0, concat_axis=0, tiled=True)]
  transfers between devices with their start and end apart: 3 -> 1, of which waited for: 3 -> 1; matrix products, arithmetic and copies ran while one was open for 0% -> 1% of each run, Pallas kernels for 0% -> 0%
where the time goes in v2:
time: 129 us; the launch traced here: 128 us
  blocking collectives  59.7 us (46%)
  matrix products  27.5 us (21%)
  waiting for transfers between devices  15.6 us (12%)
  Pallas kernels  10.9 us (8%)
  local copies, waits for them, and re-layouts  9.94 us (8%)
  starting transfers between devices  2.6 us (2%)
    all_to_all x1, blocking collectives, local(): grads = lax.all_to_all(grads, 'ex', split_axis=1, concat_axis=0, tiled=True)  31.3 us
    dot_general x1, matrix products, local(): jnp.dot(grads, projection, preferred_element_type=single_float)  23.4 us
    all_to_all x1, blocking collectives, swap(): return lax.all_to_all(blocks, axes, split_axis=0, concat_axis=0, tiled=True)  16.8 us
    all_to_all x1, waiting for transfers between devices, swap(): return lax.all_to_all(blocks, axes, split_axis=0, concat_axis=0, tiled=True)  15.6 us
    all_gather x1, blocking collectives, local(): lax.all_gather(partial_low, 'param')  11.6 us
    pallas_call x1, Pallas kernels, solve(): pl.pallas_call(functools.partial(solve_kernel, count), out_shape=(jax.Sha...  8.72 us
    convert_element_type x2, local copies, waits for them, and re-layouts, local(): jnp.concatenate([first, second, third], axis=-1).astype(jnp.bfloat16)  4.29 us
    all_to_all x1, starting transfers between devices, swap(): return lax.all_to_all(blocks, axes, split_axis=0, concat_axis=0, tiled=True)  2.6 us
  transfers between devices with their start and end apart: 1, of which 1 were waited for; matrix products, arithmetic and copies ran while one was open for 1% of the time, Pallas kernels for 0%

profile of v2, /device:TPU:0, one launch (start us, length us, event | category | flops | bytes accessed | tf_op | source)
XLA Modules:
  0.0 128.3 jit_solution(7145370207701511826)
XLA Ops:
  0.6 0.0 copy-start
  0.6 1.0 copy-done
  1.7 1.3 %convolution_bitcast_fusion = f32[2,8,32,16]{2,3,1,0:T(8,128)S(1)} fusion(bf16[8,32,1024]{2,1,0:T(8,128)(2,1)S(1)} %copy-done, bf16[2,16,1024]{2,1,0:T(8,128)(2,1)} %param.9), kind=kOutput, calls=%fused_computation.8 | convolution fusion | flops 16777216 | bytes 622592 | tf_op jit(solution)/shard_map/nsd,ard->ansr/dot_general | solution.py:148
  3.0 2.0 %fusion.12 = f32[2,8,32,16]{2,3,1,0:T(8,128)S(1)} fusion(bf16[2,8,32,1024]{3,2,1,0:T(8,128)(2,1)} %param.8, bf16[2,1024,16]{1,2,0:T(8,128)(2,1)} %param.10), kind=kOutput, calls=%fused_computation.24 | convolution fusion | flops 16777216 | bytes 1146880 | tf_op jit(solution)/shard_map/ansd,adr->ansr/dot_general | solution.py:145
  5.0 0.0 copy-start.1
  5.1 0.1 copy.16
  5.2 11.6 %all-gather = f32[32,32,64]{2,1,0:T(8,128)S(1)} all-gather(f32[8,32,64]{2,1,0:T(8,128)S(1)} %copy.16), channel_id=2, replica_groups=mesh['param'=4,'ex'=8] {'param'}, dimensions={0}, use_global_device_ids=true | all-gather | bytes 327680 | tf_op jit(solution)/shard_map/all_gather | solution.py:152
  16.9 0.1 copy.17
  17.1 0.3 fusion
  17.3 0.0 copy-done.1
  17.3 0.2 fusion.2
  17.6 0.2 fusion.3
  17.8 1.1 pad_maximum_fusion
  18.9 2.0 %copy.18 = bf16[8,1024,64]{2,1,0:T(8,128)(2,1)S(1)} copy(bf16[8,1024,64]{1,2,0:T(8,128)(2,1)} %pad_maximum_fusion) | data formatting | bytes 2097152 | tf_op jit(solution)/shard_map/concatenate | solution.py:166
  20.9 2.5 %convert_element_type.18 = bf16[8,8,8192]{2,1,0:T(8,128)(2,1)} reshape(bf16[8,1024,64]{2,1,0:T(8,128)(2,1)S(1)} %copy.18) | data formatting | bytes 2097152 | tf_op jit(solution)/shard_map/convert_element_type | solution.py:166
  23.4 1.8 %copy.19 = bf16[8,8,8192]{2,0,1:T(8,128)(2,1)S(1)} copy(bf16[8,8,8192]{2,1,0:T(8,128)(2,1)} %convert_element_type.18) | data formatting | bytes 2097152 | tf_op jit(solution)/shard_map/convert_element_type | solution.py:166
  25.2 31.3 %all_to_all.26 = bf16[8,8,8192]{2,0,1:T(8,128)(2,1)S(1)} all-to-all(bf16[8,8,8192]{2,0,1:T(8,128)(2,1)S(1)} %copy.19), channel_id=1, replica_groups=mesh['param'=4,'ex'=8] {'ex'}, dimensions={1} | all-to-all | bytes 2097152 | tf_op jit(solution)/shard_map/all_to_all | solution.py:168
  56.5 23.4 %fusion.1 = bf16[8,32,8,128]{3,2,1,0:T(8,128)(2,1)S(1)} fusion(bf16[8192,4096]{1,0:T(8,128)(2,1)} %param.11, bf16[8,8,8192]{2,0,1:T(8,128)(2,1)S(1)} %all_to_all.26), kind=kOutput, calls=%fused_computation.3 | convolution fusion | flops 4295229440 | bytes 68681728 | tf_op jit(solution)/shard_map/dot_general | solution.py:170
  79.9 0.0 copy-start.3
  79.9 0.9 copy.25
  80.8 2.6 %all-to-all-start.1 = ((bf16[32,64,128]{2,1,0:T(8,128)(2,1)}), bf16[32,64,128]{2,1,0:T(8,128)(2,1)S(1)}, u32[]{:S(2)}, u32[]{:S(2)}) async-start(bf16[32,64,128]{2,1,0:T(8,128)(2,1)} %bitcast.57), calls=%async_computation.1 | async-start | bytes 1048576 | tf_op jit(solution)/shard_map/all_to_all | solution.py:24
  83.5 0.0 copy-done.3
  83.5 0.1 fusion.17
  83.6 0.6 pad_bitcast_fusion.row_ref
  84.2 15.6 %all-to-all-done.1.blocks_ref = bf16[32,64,128]{2,1,0:T(8,128)(2,1)S(1)} async-done(((bf16[32,64,128]{2,1,0:T(8,128)(2,1)}), bf16[32,64,128]{2,1,0:T(8,128)(2,1)S(1)}, u32[]{:S(2)}, u32[]{:S(2)}) %all-to-all-start.1) | async-done | bytes 524320 | tf_op jit(solution)/shard_map/all_to_all | solution.py:24
  99.8 0.0 copy-start.2
  99.8 0.8 copy-done.2
  100.6 2.2 %packed_gram.1 = f32[32,24,128]{2,1,0:T(8,128)} custom-call(bf16[32,64,128]{2,1,0:T(8,128)(2,1)} %copy-done.2, f32[1,128]{1,0:T(1,128)} %pad_bitcast_fusion.row_ref), custom_call_target="tpu_custom_call" | custom-call | tf_op jit(solution)/shard_map/packed_gram/pallas_call | solution.py:47
  102.8 16.8 %all_to_all.27.pieces_ref = f32[32,24,128]{2,1,0:T(8,128)} all-to-all(f32[32,24,128]{2,1,0:T(8,128)} %packed_gram.1), channel_id=1, replica_groups=mesh['param'=4,'ex'=8] {'param','ex'}, dimensions={0} | all-to-all | bytes 786432 | tf_op jit(solution)/shard_map/all_to_all | solution.py:24
  119.6 8.7 %solve.1 = (f32[8,64]{1,0:T(8,128)}, f32[4,64]{1,0:T(4,128)}) custom-call(s32[1]{0:T(128)} %bitcast.slot_ref, f32[32,24,128]{2,1,0:T(8,128)} %all_to_all.27.pieces_ref, s32[1,64]{1,0:T(1,128)} %bitcast.59), custom_call_target="tpu_custom_call" | custom-call | tf_op jit(solution)/shard_map/solve/pallas_call | solution.py:112
  (4 shorter events, 0.1 us)
Async XLA Ops:
  0.6 1.0 copy-start
  5.0 12.3 %copy-start.1 = (bf16[2,8,32,1024]{3,2,1,0:T(8,128)(2,1)S(1)}, bf16[2,8,32,1024]{3,2,1,0:T(8,128)(2,1)}, u32[]{:S(2)}) copy-start(bf16[2,8,32,1024]{3,2,1,0:T(8,128)(2,1)} %param.8) | copy-start | bytes 3145732
  79.9 3.6 %copy-start.3 = (s32[8]{0:T(128)S(1)}, s32[8]{0:T(128)}, u32[]{:S(2)}) copy-start(s32[8]{0:T(128)} %param.12) | copy-start | bytes 100
  80.8 19.0 %all-to-all-start.1 = ((bf16[32,64,128]{2,1,0:T(8,128)(2,1)}), bf16[32,64,128]{2,1,0:T(8,128)(2,1)S(1)}, u32[]{:S(2)}, u32[]{:S(2)}) async-start(bf16[32,64,128]{2,1,0:T(8,128)(2,1)} %bitcast.57), calls=%async_computation.1 | async-start | bytes 1048576 | tf_op jit(solution)/shard_map/all_to_all | solution.py:24
  99.8 0.8 copy-start.2

commit v3 on v2

--- a/solution.py
+++ b/solution.py
@@ -11,6 +11,9 @@
 K = 4096
 DOMAINS = 4
 HALF = 32
+EARLY = 9
+BLOCK = 256
+SLOTS = 12
 EVERY = ("param", "ex")
 
 
@@ -22,6 +25,146 @@
 
 def swap(blocks, axes):
     return lax.all_to_all(blocks, axes, split_axis=0, concat_axis=0, tiled=True)
+
+
+def gradient_rows_kernel(early, act_in, out_in, low_ref, first_ref, second_ref, act_ref, out_ref, tall_ref, wide_ref, sems):
+    copies = [pltpu.make_async_copy(act_in, act_ref, sems.at[0]), pltpu.make_async_copy(out_in, out_ref, sems.at[1])]
+    for copy in copies:
+        copy.start()
+    examples, _, channels = act_ref.shape
+    rank = low_ref.shape[3] // 4
+    blocks = first_ref.shape[0]
+    low = low_ref[0]
+    for part in range(1, low_ref.shape[0]):
+        low = low + low_ref[part]
+    low = low.astype(jnp.bfloat16).astype(jnp.float32)
+    for copy in copies:
+        copy.wait()
+    for n in range(examples):
+        twice = jnp.concatenate([low[n], low[n]], axis=1)
+        lane = lax.broadcasted_iota(jnp.int32, twice.shape, 1)
+        column = lax.rem(lane, 4 * rank)
+        factors = jnp.concatenate(
+            [
+                jnp.where(column < 2 * rank, twice, 0.0),
+                jnp.where((column >= 2 * rank) & (column < 3 * rank), twice, 0.0),
+                jnp.where(column >= 3 * rank, twice, 0.0),
+            ],
+            axis=0,
+        ).astype(jnp.bfloat16)
+        tokens = jnp.concatenate([act_ref[n], out_ref[0, n], out_ref[1, n]], axis=0)
+        tall_ref[...] = lax.dot_general(
+            tokens, factors, (((0,), (0,)), ((), ())), preferred_element_type=jnp.float32
+        )
+        even = tall_ref[pl.ds(0, channels // 2, stride=2), :]
+        odd = tall_ref[pl.ds(1, channels // 2, stride=2), :]
+        lane = lax.broadcasted_iota(jnp.int32, even.shape, 1)
+        wide_ref[pl.ds(n, channels // 2, stride=examples), :] = jnp.where(lane < 4 * rank, even, odd)
+    tiles = channels // 2 // blocks
+    for block in range(blocks):
+        for tile in range(tiles):
+            start = (block * tiles + tile) * examples
+            piece = wide_ref[start : start + examples, :].astype(jnp.bfloat16)
+            at = tile * 128
+            if at < early:
+                first_ref[block, :, at : at + 128] = piece
+            else:
+                second_ref[block, :, at - early : at - early + 128] = piece
+
+
+def gradient_rows(activations, output_gradients, low_parts, blocks, early):
+    examples, _, channels = activations.shape
+    columns = low_parts.shape[3]
+    lanes = channels * columns // blocks
+    return pl.pallas_call(
+        functools.partial(gradient_rows_kernel, early),
+        out_shape=(
+            jax.ShapeDtypeStruct((blocks, examples, early), jnp.bfloat16),
+            jax.ShapeDtypeStruct((blocks, examples, lanes - early), jnp.bfloat16),
+        ),
+        in_specs=[
+            pl.BlockSpec(memory_space=pl.ANY),
+            pl.BlockSpec(memory_space=pl.ANY),
+            pl.BlockSpec(memory_space=pltpu.VMEM),
+        ],
+        scratch_shapes=[
+            pltpu.VMEM(activations.shape, activations.dtype),
+            pltpu.VMEM(output_gradients.shape, output_gradients.dtype),
+            pltpu.VMEM((channels, 2 * columns), jnp.float32),
+            pltpu.VMEM((channels // 2 * examples, 2 * columns), jnp.float32),
+            pltpu.SemaphoreType.DMA((2,)),
+        ],
+        compiler_params=pltpu.CompilerParams(vmem_limit_bytes=24 << 20),
+        name="gradient_rows",
+    )(activations, output_gradients, low_parts)
+
+
+def partial_features_kernel(first_row, has_total, *refs):
+    if has_total:
+        grads_ref, rows_ref, total_ref, out_ref, acc_ref, held_ref, sems = refs
+    else:
+        grads_ref, rows_ref, out_ref, held_ref, sems = refs
+        acc_ref = out_ref
+    slots, block, _ = held_ref.shape
+    count = grads_ref.shape[1]
+    starts = list(range(0, count, block))
+
+    def copy(i):
+        size = min(block, count - starts[i])
+        return pltpu.make_async_copy(
+            rows_ref.at[pl.ds(first_row + starts[i], size)],
+            held_ref.at[i % slots, pl.ds(0, size)],
+            sems.at[i % slots],
+        )
+
+    for i in range(min(slots, len(starts))):
+        copy(i).start()
+    for i, start in enumerate(starts):
+        size = min(block, count - start)
+        copy(i).wait()
+        product = jnp.dot(
+            grads_ref[:, start : start + size], held_ref[i % slots, :size], preferred_element_type=jnp.float32
+        )
+        if i:
+            acc_ref[...] += product
+        elif has_total:
+            acc_ref[...] = total_ref[...] + product
+        else:
+            acc_ref[...] = product
+        if i + slots < len(starts):
+            copy(i + slots).start()
+    if has_total:
+        if len(out_ref.shape) == 3:
+            lanes = out_ref.shape[2]
+            for block in range(out_ref.shape[0]):
+                out_ref[block] = acc_ref[:, block * lanes : (block + 1) * lanes].astype(out_ref.dtype)
+        else:
+            out_ref[...] = acc_ref[...].astype(out_ref.dtype)
+
+
+def partial_features(grads, projection, first_row, total, blocks):
+    examples, count = grads.shape
+    columns = projection.shape[1]
+    in_vmem = pl.BlockSpec(memory_space=pltpu.VMEM)
+    in_specs = [in_vmem, pl.BlockSpec(memory_space=pl.ANY)]
+    scratch = [pltpu.VMEM((SLOTS, BLOCK, columns), projection.dtype), pltpu.SemaphoreType.DMA((SLOTS,))]
+    operands = (grads, projection)
+    out_shape = jax.ShapeDtypeStruct((examples, columns), jnp.float32)
+    if total is not None:
+        operands += (total,)
+        in_specs.append(in_vmem)
+        scratch.insert(0, pltpu.VMEM((examples, columns), jnp.float32))
+        shape = (examples, columns) if columns // blocks % 128 else (blocks, examples, columns // blocks)
+        out_shape = jax.ShapeDtypeStruct(shape, jnp.bfloat16)
+    return pl.pallas_call(
+        functools.partial(partial_features_kernel, first_row, total is not None),
+        out_shape=out_shape,
+        in_specs=in_specs,
+        out_specs=in_vmem,
+        scratch_shapes=scratch,
+        compiler_params=pltpu.CompilerParams(vmem_limit_bytes=40 << 20),
+        name="partial_features",
+    )(*operands)
 
 
 def packs(example_count):
@@ -47,6 +190,7 @@
     return pl.pallas_call(
         packed_gram_kernel,
         out_shape=jax.ShapeDtypeStruct((blocks.shape[0], HALF // 2 + 8, 128), jnp.float32),
+        compiler_params=pltpu.CompilerParams(vmem_limit_bytes=16 << 20),
         name="packed_gram",
     )(blocks, row)
 
@@ -122,6 +266,7 @@
         ],
         out_specs=(pl.BlockSpec(memory_space=pltpu.VMEM), pl.BlockSpec(memory_space=pltpu.VMEM)),
         scratch_shapes=[pltpu.VMEM((count, count), jnp.float32)],
+        compiler_params=pltpu.CompilerParams(vmem_limit_bytes=16 << 20),
         name="solve",
     )(jnp.reshape(slot, (1,)), pieces, target_ids[None])
 
@@ -149,27 +294,17 @@
         "nsd,ard->ansr", activations, down_projection_weight, preferred_element_type=single_float
     )
     partial_low = jnp.concatenate([up_terms[0], up_terms[1], down_terms[0], down_terms[1]], axis=-1)
-    low = jnp.sum(lax.all_gather(partial_low, "param"), axis=0).astype(jnp.bfloat16)
-
-    first = jnp.einsum(
-        "erb,ery->eby", activations, low[..., : 2 * rank], preferred_element_type=single_float
-    )
-    second = jnp.einsum(
-        "fai,fav->fiv",
-        output_gradients[0],
-        low[..., 2 * rank : 3 * rank],
-        preferred_element_type=single_float,
-    )
-    third = jnp.einsum(
-        "fai,fav->fiv", output_gradients[1], low[..., 3 * rank :], preferred_element_type=single_float
-    )
-    grads = jnp.concatenate([first, second, third], axis=-1).astype(jnp.bfloat16)
-    grads = grads.reshape(ex_rows, grads.shape[1] * grads.shape[2])
-    grads = lax.all_to_all(grads, "ex", split_axis=1, concat_axis=0, tiled=True)
-
-    partial_features = jnp.dot(grads, projection, preferred_element_type=single_float)
-    blocks = partial_features.astype(jnp.bfloat16).reshape(example_count, devices, K // devices)
-    arrived = swap(blocks.transpose(1, 0, 2), EVERY)
+    low_parts = lax.all_gather(partial_low, "param")
+
+    row_count = projection.shape[0]
+    early = row_count * EARLY // (16 * 128) * 128
+    wires = gradient_rows(activations, output_gradients, low_parts, ex_size, early)
+    arrived = [swap(wire, "ex").reshape(example_count, wire.shape[2]) for wire in wires]
+    total = partial_features(arrived[0], projection, 0, None, 1)
+    partial_sums = partial_features(arrived[1], projection, early, total, devices)
+    if partial_sums.ndim == 2:
+        partial_sums = partial_sums.reshape(example_count, devices, K // devices).transpose(1, 0, 2)
+    arrived = swap(partial_sums, EVERY)
 
     slot = lax.axis_index("ex") * ex_rows
     mine = jnp.where(lax.axis_index("param") == 0, domains, 0).astype(single_float)

time: 129 us -> 115 us (0.89)
  matrix products: 27.5 us -> 3.57 us
  Pallas kernels: 10.9 us -> 33.9 us
  blocking collectives: 59.7 us -> 48.5 us
  local copies, waits for them, and re-layouts: 9.94 us -> 3.35 us
  starting transfers between devices: 2.6 us -> 7.34 us
  waiting for transfers between devices: 15.6 us -> 17.3 us
    all_to_all x1 -> x0, blocking collectives: 31.3 us -> none  [local(): grads = lax.all_to_all(grads, 'ex', split_axis=1, concat_axis=0, tiled=True)]
    pallas_call x0 -> x3, Pallas kernels: none -> 25.8 us  [the longest x2 23.7 us: partial_features(): pl.pallas_call(functools.partial(partial_features_kernel, first_row, tota...]
    dot_general x4 -> x0, matrix products: 24.1 us -> none  [the longest x1 23.4 us: local(): jnp.dot(grads, projection, preferred_element_type=single_float)]
    all_to_all x1 -> x2, blocking collectives: 16.8 us -> 37 us  [swap(): return lax.all_to_all(blocks, axes, split_axis=0, concat_axis=0, tiled=True)]
    all_to_all x1 -> x2, starting transfers between devices: 2.6 us -> 7.34 us  [swap(): return lax.all_to_all(blocks, axes, split_axis=0, concat_axis=0, tiled=True)]
    convert_element_type x2 -> x0, local copies, waits for them, and re-layouts: 4.29 us -> none  [local(): jnp.concatenate([first, second, third], axis=-1).astype(jnp.bfloat16)]
    concatenate x1 -> x0, local copies, waits for them, and re-layouts: 2.02 us -> none  [local(): jnp.concatenate([first, second, third], axis=-1).astype(jnp.bfloat16)]
    pallas_call x1, Pallas kernels: 2.19 us -> 0.4 us  [packed_gram(): pl.pallas_call(packed_gram_kernel, out_shape=jax.ShapeDtypeStruct((blocks...]
  transfers between devices with their start and end apart: 1 -> 2, of which waited for: 1 -> 2; matrix products, arithmetic and copies ran while one was open for 1% -> 0% of each run, Pallas kernels for 0% -> 11%
where the time goes in v3:
time: 115 us
  blocking collectives  48.5 us (42%)
  Pallas kernels  33.9 us (29%)
  waiting for transfers between devices  17.3 us (15%)
  starting transfers between devices  7.34 us (6%)
  matrix products  3.57 us (3%)
  local copies, waits for them, and re-layouts  3.35 us (3%)
    all_to_all x2, blocking collectives, swap(): return lax.all_to_all(blocks, axes, split_axis=0, concat_axis=0, tiled=True)  37 us
    pallas_call x2, Pallas kernels, partial_features(): pl.pallas_call(functools.partial(partial_features_kernel, first_row, tota...  23.7 us
    all_to_all x2, waiting for transfers between devices, swap(): return lax.all_to_all(blocks, axes, split_axis=0, concat_axis=0, tiled=True)  17.3 us
    all_gather x1, blocking collectives, local(): low_parts = lax.all_gather(partial_low, 'param')  11.5 us
    pallas_call x1, Pallas kernels, solve(): pl.pallas_call(functools.partial(solve_kernel, count), out_shape=(jax.Sha...  7.73 us
    all_to_all x2, starting transfers between devices, swap(): return lax.all_to_all(blocks, axes, split_axis=0, concat_axis=0, tiled=True)  7.34 us
    unnamed x10, local copies, waits for them, and re-layouts  3.12 us
  transfers between devices with their start and end apart: 2, of which 2 were waited for; matrix products, arithmetic and copies ran while one was open for 0% of the time, Pallas kernels for 11%

profile of v3, /device:TPU:0, one launch (start us, length us, event | category | flops | bytes accessed | tf_op | source)
XLA Modules:
  0.0 114.9 jit_solution(2794341509268040512)
XLA Ops:
  0.6 0.0 copy-start
  0.6 0.8 copy-done
  1.5 1.5 %convolution_bitcast_fusion = f32[2,8,32,16]{2,3,1,0:T(8,128)S(1)} fusion(bf16[8,32,1024]{2,1,0:T(8,128)(2,1)} %act_in.1, bf16[2,16,1024]{2,1,0:T(8,128)(2,1)S(1)} %copy-done), kind=kOutput, calls=%fused_computation | convolution fusion | flops 16777216 | bytes 622592 | tf_op jit(solution)/shard_map/nsd,ard->ansr/dot_general | solution.py:293
  3.0 2.0 %fusion.2 = f32[2,8,32,16]{2,3,1,0:T(8,128)S(1)} fusion(bf16[2,8,32,1024]{3,2,1,0:T(8,128)(2,1)} %out_in.1, bf16[2,1024,16]{1,2,0:T(8,128)(2,1)} %param.10), kind=kOutput, calls=%fused_computation.8 | convolution fusion | flops 16777216 | bytes 1146880 | tf_op jit(solution)/shard_map/ansd,adr->ansr/dot_general | solution.py:290
  5.1 0.1 copy.10
  5.2 11.5 %all-gather = f32[32,32,64]{2,1,0:T(8,128)S(1)} all-gather(f32[8,32,64]{2,1,0:T(8,128)S(1)} %copy.10), channel_id=2, replica_groups=mesh['param'=4,'ex'=8] {'param'}, dimensions={0}, use_global_device_ids=true | all-gather | bytes 327680 | tf_op jit(solution)/shard_map/all_gather | solution.py:297
  16.7 0.0 copy-start.1
  16.7 1.2 %copy-done.1 = bf16[2,8,32,1024]{3,2,1,0:T(8,128)(2,1)S(1)} copy-done((bf16[2,8,32,1024]{3,2,1,0:T(8,128)(2,1)S(1)}, bf16[2,8,32,1024]{3,2,1,0:T(8,128)(2,1)}, u32[]{:S(2)}) %copy-start.1) | copy-done | bytes 1048600
  18.0 0.0 copy-start.2
  18.0 1.0 copy-done.2
  19.0 2.1 %gradient_rows.1 = (bf16[8,8,4608]{2,1,0:T(8,128)(2,1)S(1)}, bf16[8,8,3584]{2,1,0:T(8,128)(2,1)}) custom-call(bf16[8,32,1024]{2,1,0:T(8,128)(2,1)S(1)} %copy-done.2, bf16[2,8,32,1024]{3,2,1,0:T(8,128)(2,1)S(1)} %copy-done.1, f32[4,8,32,64]{3,2,1,0:T(8,128)S(1)} %bitcast.34), custom_call_target="tpu_custom_call" | custom-call | tf_op jit(solution)/shard_map/gradient_rows/pallas_call | solution.py:79
  21.1 21.4 %all_to_all.20 = bf16[8,8,4608]{2,1,0:T(8,128)(2,1)S(1)} all-to-all(bf16[8,8,4608]{2,1,0:T(8,128)(2,1)S(1)} %get-tuple-element.7), channel_id=1, replica_groups=mesh['param'=4,'ex'=8] {'ex'}, dimensions={0} | all-to-all | bytes 1179648 | tf_op jit(solution)/shard_map/all_to_all | solution.py:27
  42.5 3.5 %all-to-all-start = ((bf16[8,8,3584]{2,1,0:T(8,128)(2,1)}), bf16[8,8,3584]{2,1,0:T(8,128)(2,1)S(1)}, u32[]{:S(2)}, u32[]{:S(2)}) async-start(bf16[8,8,3584]{2,1,0:T(8,128)(2,1)} %get-tuple-element.6), calls=%async_computation | async-start | bytes 917504 | tf_op jit(solution)/shard_map/all_to_all | solution.py:27
  46.0 0.0 copy-start.4
  46.0 0.0 copy-start.3
  46.1 12.7 %partial_features.2.refs_2_ = f32[64,4096]{1,0:T(8,128)S(1)} custom-call(bf16[64,4608]{1,0:T(8,128)(2,1)S(1)} %bitcast.33, bf16[8192,4096]{1,0:T(8,128)(2,1)} %refs_1_.3), custom_call_target="tpu_custom_call" | custom-call | tf_op jit(solution)/shard_map/partial_features/pallas_call | solution.py:159
  58.7 1.2 %all-to-all-done = bf16[8,8,3584]{2,1,0:T(8,128)(2,1)S(1)} async-done(((bf16[8,8,3584]{2,1,0:T(8,128)(2,1)}), bf16[8,8,3584]{2,1,0:T(8,128)(2,1)S(1)}, u32[]{:S(2)}, u32[]{:S(2)}) %all-to-all-start) | async-done | bytes 458784 | tf_op jit(solution)/shard_map/all_to_all | solution.py:27
  59.9 11.0 %partial_features.3 = bf16[32,64,128]{2,1,0:T(8,128)(2,1)} custom-call(bf16[64,3584]{1,0:T(8,128)(2,1)S(1)} %bitcast.35, bf16[8192,4096]{1,0:T(8,128)(2,1)} %refs_1_.3, f32[64,4096]{1,0:T(8,128)S(1)} %partial_features.2.refs_2_), custom_call_target="tpu_custom_call" | custom-call | tf_op jit(solution)/shard_map/partial_features/pallas_call | solution.py:159
  71.0 3.9 %all-to-all-start.2 = ((bf16[32,64,128]{2,1,0:T(8,128)(2,1)}), bf16[32,64,128]{2,1,0:T(8,128)(2,1)S(1)}, u32[]{:S(2)}, u32[]{:S(2)}) async-start(bf16[32,64,128]{2,1,0:T(8,128)(2,1)} %partial_features.3), calls=%async_computation.2 | async-start | bytes 1048576 | tf_op jit(solution)/shard_map/all_to_all | solution.py:27
  74.9 0.0 copy-done.4
  74.9 0.1 fusion.5
  75.0 0.1 pad_bitcast_fusion.row_ref
  75.0 16.1 %all-to-all-done.2.blocks_ref = bf16[32,64,128]{2,1,0:T(8,128)(2,1)S(1)} async-done(((bf16[32,64,128]{2,1,0:T(8,128)(2,1)}), bf16[32,64,128]{2,1,0:T(8,128)(2,1)S(1)}, u32[]{:S(2)}, u32[]{:S(2)}) %all-to-all-start.2) | async-done | bytes 524320 | tf_op jit(solution)/shard_map/all_to_all | solution.py:27
  91.2 0.4 packed_gram.1
  91.6 15.6 %all_to_all.21.pieces_ref = f32[32,24,128]{2,1,0:T(8,128)S(1)} all-to-all(f32[32,24,128]{2,1,0:T(8,128)S(1)} %packed_gram.1), channel_id=1, replica_groups=mesh['param'=4,'ex'=8] {'param','ex'}, dimensions={0} | all-to-all | bytes 786432 | tf_op jit(solution)/shard_map/all_to_all | solution.py:27
  107.2 0.0 copy-done.3
  107.2 7.7 %solve.1 = (f32[8,64]{1,0:T(8,128)}, f32[4,64]{1,0:T(4,128)}) custom-call(s32[1]{0:T(128)} %bitcast.slot_ref, f32[32,24,128]{2,1,0:T(8,128)S(1)} %all_to_all.21.pieces_ref, s32[1,64]{1,0:T(1,128)S(1)} %bitcast.36), custom_call_target="tpu_custom_call" | custom-call | tf_op jit(solution)/shard_map/solve/pallas_call | solution.py:256
  (3 shorter events, 0.1 us)
Async XLA Ops:
  0.6 0.8 copy-start
  16.7 1.2 %copy-start.1 = (bf16[2,8,32,1024]{3,2,1,0:T(8,128)(2,1)S(1)}, bf16[2,8,32,1024]{3,2,1,0:T(8,128)(2,1)}, u32[]{:S(2)}) copy-start(bf16[2,8,32,1024]{3,2,1,0:T(8,128)(2,1)} %out_in.1) | copy-start | bytes 3145732
  18.0 1.0 copy-start.2
  42.5 17.4 %all-to-all-start = ((bf16[8,8,3584]{2,1,0:T(8,128)(2,1)}), bf16[8,8,3584]{2,1,0:T(8,128)(2,1)S(1)}, u32[]{:S(2)}, u32[]{:S(2)}) async-start(bf16[8,8,3584]{2,1,0:T(8,128)(2,1)} %get-tuple-element.6), calls=%async_computation | async-start | bytes 917504 | tf_op jit(solution)/shard_map/all_to_all | solution.py:27
  46.0 28.8 %copy-start.4 = (s32[8]{0:T(128)S(1)}, s32[8]{0:T(128)}, u32[]{:S(2)}) copy-start(s32[8]{0:T(128)} %param.12) | copy-start | bytes 100
  46.0 61.1 %copy-start.3 = (s32[64]{0:T(128)S(1)}, s32[64]{0:T(128)}, u32[]{:S(2)}) copy-start(s32[64]{0:T(128)} %param.13) | copy-start | bytes 772
  71.0 20.2 %all-to-all-start.2 = ((bf16[32,64,128]{2,1,0:T(8,128)(2,1)}), bf16[32,64,128]{2,1,0:T(8,128)(2,1)S(1)}, u32[]{:S(2)}, u32[]{:S(2)}) async-start(bf16[32,64,128]{2,1,0:T(8,128)(2,1)} %partial_features.3), calls=%async_computation.2 | async-start | bytes 1048576 | tf_op jit(solution)/shard_map/all_to_all | solution.py:27

commit v4 on v2

--- a/solution.py
+++ b/solution.py
@@ -11,6 +11,9 @@
 K = 4096
 DOMAINS = 4
 HALF = 32
+FOLD = 4
+GROUP = 8
+SLOTS = 12
 EVERY = ("param", "ex")
 
 
@@ -22,6 +25,191 @@
 
 def swap(blocks, axes):
     return lax.all_to_all(blocks, axes, split_axis=0, concat_axis=0, tiled=True)
+
+
+def spread(columns):
+    return jnp.concatenate([columns] * FOLD, axis=0).T
+
+
+def low_columns_kernel(parts_ref, queries_ref, rest_ref):
+    low = parts_ref[0]
+    for part in range(1, parts_ref.shape[0]):
+        low = low + parts_ref[part]
+    low = low.astype(jnp.bfloat16)
+    half = low.shape[0] // 2
+    for block in range(queries_ref.shape[0]):
+        queries_ref[block] = low[:half]
+    rest_ref[...] = spread(low[half:].astype(jnp.float32)).astype(jnp.bfloat16)
+
+
+def low_columns(parts, blocks):
+    _, columns, tokens = parts.shape
+    return pl.pallas_call(
+        low_columns_kernel,
+        out_shape=(
+            jax.ShapeDtypeStruct((blocks, columns // 2, tokens), jnp.bfloat16),
+            jax.ShapeDtypeStruct((tokens, FOLD * columns // 2), jnp.bfloat16),
+        ),
+        compiler_params=pltpu.CompilerParams(vmem_limit_bytes=16 << 20),
+        name="low_columns",
+    )(parts)
+
+
+def fold_rows(tall_ref, first, count):
+    folded = tall_ref[pl.ds(first, count // FOLD, stride=FOLD), :]
+    group = lax.broadcasted_iota(jnp.int32, folded.shape, 1) // (128 // FOLD)
+    for j in range(1, FOLD):
+        folded = jnp.where(group == j, tall_ref[pl.ds(first + j, count // FOLD, stride=FOLD), :], folded)
+    return folded
+
+
+def gradient_rows_kernel(out_ref, low_ref, wire_ref, tall_ref, wide_ref):
+    _, examples, tokens, channels = out_ref.shape
+    blocks = wire_ref.shape[0]
+    for n in range(examples):
+        factors = low_ref[n * tokens : (n + 1) * tokens, :].astype(jnp.float32)
+        column = lax.rem(lax.broadcasted_iota(jnp.int32, factors.shape, 1), 128 // FOLD)
+        value = column >= 64 // FOLD
+        factors = jnp.concatenate([jnp.where(value, 0.0, factors), jnp.where(value, factors, 0.0)], axis=0)
+        both = jnp.concatenate([out_ref[0, n], out_ref[1, n]], axis=0)
+        tall_ref[...] = lax.dot_general(
+            both, factors.astype(jnp.bfloat16), (((0,), (0,)), ((), ())), preferred_element_type=jnp.float32
+        )
+        wide_ref[pl.ds(n, channels // FOLD, stride=examples), :] = fold_rows(tall_ref, 0, channels)
+    tiles = channels // FOLD // blocks
+    for block in range(blocks):
+        for tile in range(tiles):
+            start = (block * tiles + tile) * examples
+            piece = wide_ref[start : start + examples, :].astype(jnp.bfloat16)
+            wire_ref[block, :, tile * 128 : (tile + 1) * 128] = piece
+
+
+def gradient_rows(output_gradients, low, blocks):
+    _, examples, _, channels = output_gradients.shape
+    lanes = channels * 128 // FOLD // blocks
+    return pl.pallas_call(
+        gradient_rows_kernel,
+        out_shape=jax.ShapeDtypeStruct((blocks, examples, lanes), jnp.bfloat16),
+        scratch_shapes=[
+            pltpu.VMEM((channels, 128), jnp.float32),
+            pltpu.VMEM((channels // FOLD * examples, 128), jnp.float32),
+        ],
+        compiler_params=pltpu.CompilerParams(vmem_limit_bytes=16 << 20),
+        name="gradient_rows",
+    )(output_gradients, low)
+
+
+def multiply_rows(grads_ref, rows_ref, half, held_ref, sems, acc_ref, prepare, total_ref):
+    slots, group, columns, _ = held_ref.shape
+    size = group * columns
+    count = rows_ref.shape[0] // group
+
+    def copy(i):
+        return pltpu.make_async_copy(
+            rows_ref.at[pl.ds(i * group, group), pl.ds(half * columns, columns)],
+            held_ref.at[i % slots],
+            sems.at[i % slots],
+        )
+
+    for i in range(min(slots, count)):
+        copy(i).start()
+    prepare()
+    for i in range(count):
+        copy(i).wait()
+        product = jnp.dot(
+            grads_ref[:, i * size : (i + 1) * size],
+            held_ref[i % slots].reshape(size, held_ref.shape[3]),
+            preferred_element_type=jnp.float32,
+        )
+        if i:
+            acc_ref[...] += product
+        elif total_ref is None:
+            acc_ref[...] = product
+        else:
+            acc_ref[...] = total_ref[...] + product
+        if i + slots < count:
+            copy(i + slots).start()
+
+
+def early_features_kernel(tokens_ref, low_ref, rows_ref, total_ref, grads_ref, tall_ref, wide_ref, held_ref, sems):
+    examples, length, channels = tokens_ref.shape
+    sources = low_ref.shape[0]
+    each = examples // sources
+
+    def prepare():
+        def source(index, carry):
+            factors = spread(low_ref[index].astype(jnp.float32)).astype(jnp.bfloat16)
+            for n in range(each):
+                tall_ref[n * channels : (n + 1) * channels, :] = lax.dot_general(
+                    tokens_ref[index * each + n],
+                    factors[n * length : (n + 1) * length],
+                    (((0,), (0,)), ((), ())),
+                    preferred_element_type=jnp.float32,
+                )
+            for n in range(each):
+                wide_ref[pl.ds(index * each + n, channels // FOLD, stride=examples), :] = fold_rows(
+                    tall_ref, n * channels, channels
+                )
+            return carry
+
+        lax.fori_loop(0, sources, source, 0)
+        for tile in range(channels // FOLD):
+            grads_ref[:, tile * 128 : (tile + 1) * 128] = wide_ref[
+                tile * examples : (tile + 1) * examples, :
+            ].astype(jnp.bfloat16)
+
+    multiply_rows(grads_ref, rows_ref, 0, held_ref, sems, total_ref, prepare, None)
+
+
+def held_rows(rows):
+    return [
+        pltpu.VMEM((SLOTS, GROUP, rows.shape[1] // 2, rows.shape[2]), rows.dtype),
+        pltpu.SemaphoreType.DMA((SLOTS,)),
+    ]
+
+
+def early_features(tokens, low, rows):
+    examples, _, channels = tokens.shape
+    in_vmem = pl.BlockSpec(memory_space=pltpu.VMEM)
+    return pl.pallas_call(
+        early_features_kernel,
+        out_shape=jax.ShapeDtypeStruct((examples, rows.shape[2]), jnp.float32),
+        in_specs=[in_vmem, in_vmem, pl.BlockSpec(memory_space=pl.ANY)],
+        out_specs=in_vmem,
+        scratch_shapes=[
+            pltpu.VMEM((examples, channels * 128 // FOLD), jnp.bfloat16),
+            pltpu.VMEM((examples // low.shape[0] * channels, 128), jnp.float32),
+            pltpu.VMEM((channels // FOLD * examples, 128), jnp.float32),
+        ]
+        + held_rows(rows),
+        compiler_params=pltpu.CompilerParams(vmem_limit_bytes=40 << 20),
+        name="early_features",
+    )(tokens, low, rows)
+
+
+def late_features_kernel(grads_ref, rows_ref, total_ref, out_ref, acc_ref, held_ref, sems):
+    multiply_rows(grads_ref, rows_ref, 1, held_ref, sems, acc_ref, lambda: None, total_ref)
+    if len(out_ref.shape) == 3:
+        lanes = out_ref.shape[2]
+        for block in range(out_ref.shape[0]):
+            out_ref[block] = acc_ref[:, block * lanes : (block + 1) * lanes].astype(out_ref.dtype)
+    else:
+        out_ref[...] = acc_ref[...].astype(out_ref.dtype)
+
+
+def late_features(grads, rows, total, blocks):
+    examples, columns = total.shape
+    shape = (examples, columns) if columns // blocks % 128 else (blocks, examples, columns // blocks)
+    in_vmem = pl.BlockSpec(memory_space=pltpu.VMEM)
+    return pl.pallas_call(
+        late_features_kernel,
+        out_shape=jax.ShapeDtypeStruct(shape, jnp.bfloat16),
+        in_specs=[in_vmem, pl.BlockSpec(memory_space=pl.ANY), in_vmem],
+        out_specs=in_vmem,
+        scratch_shapes=[pltpu.VMEM((examples, columns), jnp.float32)] + held_rows(rows),
+        compiler_params=pltpu.CompilerParams(vmem_limit_bytes=40 << 20),
+        name="late_features",
+    )(grads, rows, total)
 
 
 def packs(example_count):
@@ -47,6 +235,7 @@
     return pl.pallas_call(
         packed_gram_kernel,
         out_shape=jax.ShapeDtypeStruct((blocks.shape[0], HALF // 2 + 8, 128), jnp.float32),
+        compiler_params=pltpu.CompilerParams(vmem_limit_bytes=16 << 20),
         name="packed_gram",
     )(blocks, row)
 
@@ -122,6 +311,7 @@
         ],
         out_specs=(pl.BlockSpec(memory_space=pltpu.VMEM), pl.BlockSpec(memory_space=pltpu.VMEM)),
         scratch_shapes=[pltpu.VMEM((count, count), jnp.float32)],
+        compiler_params=pltpu.CompilerParams(vmem_limit_bytes=16 << 20),
         name="solve",
     )(jnp.reshape(slot, (1,)), pieces, target_ids[None])
 
@@ -142,34 +332,38 @@
     devices = lax.axis_size("param") * ex_size
     example_count = ex_rows * ex_size
 
+    tokens = activations.shape[1]
+    channels = activations.shape[2]
+    owned = channels // ex_size
+
+    wire = activations.reshape(ex_rows, tokens, ex_size, owned).transpose(2, 0, 1, 3)
+    moved = swap(wire, "ex").reshape(example_count, tokens, owned)
+
     up_terms = jnp.einsum(
-        "ansd,adr->ansr", output_gradients, adapter_up, preferred_element_type=single_float
+        "atd,adr->art",
+        output_gradients.reshape(2, ex_rows * tokens, channels),
+        adapter_up,
+        preferred_element_type=single_float,
     )
     down_terms = jnp.einsum(
-        "nsd,ard->ansr", activations, down_projection_weight, preferred_element_type=single_float
-    )
-    partial_low = jnp.concatenate([up_terms[0], up_terms[1], down_terms[0], down_terms[1]], axis=-1)
-    low = jnp.sum(lax.all_gather(partial_low, "param"), axis=0).astype(jnp.bfloat16)
-
-    first = jnp.einsum(
-        "erb,ery->eby", activations, low[..., : 2 * rank], preferred_element_type=single_float
-    )
-    second = jnp.einsum(
-        "fai,fav->fiv",
-        output_gradients[0],
-        low[..., 2 * rank : 3 * rank],
+        "td,ard->art",
+        activations.reshape(ex_rows * tokens, channels),
+        down_projection_weight,
         preferred_element_type=single_float,
     )
-    third = jnp.einsum(
-        "fai,fav->fiv", output_gradients[1], low[..., 3 * rank :], preferred_element_type=single_float
-    )
-    grads = jnp.concatenate([first, second, third], axis=-1).astype(jnp.bfloat16)
-    grads = grads.reshape(ex_rows, grads.shape[1] * grads.shape[2])
-    grads = lax.all_to_all(grads, "ex", split_axis=1, concat_axis=0, tiled=True)
-
-    partial_features = jnp.dot(grads, projection, preferred_element_type=single_float)
-    blocks = partial_features.astype(jnp.bfloat16).reshape(example_count, devices, K // devices)
-    arrived = swap(blocks.transpose(1, 0, 2), EVERY)
+    partial_low = jnp.concatenate([up_terms, down_terms], axis=0).reshape(4 * rank, ex_rows * tokens)
+    low_parts = lax.all_gather(partial_low, "param")
+    queries, rest = low_columns(low_parts, ex_size)
+    queries, moved = lax.optimization_barrier((queries, moved))
+
+    queries = swap(queries, "ex")
+    grads = swap(gradient_rows(output_gradients, rest, ex_size), "ex").reshape(example_count, owned * 2 * rank)
+    rows = projection.reshape(owned, 4 * rank, K)
+    total = early_features(moved, queries, rows)
+    partial_sums = late_features(grads, rows, total, devices)
+    if partial_sums.ndim == 2:
+        partial_sums = partial_sums.reshape(example_count, devices, K // devices).transpose(1, 0, 2)
+    arrived = swap(partial_sums, EVERY)
 
     slot = lax.axis_index("ex") * ex_rows
     mine = jnp.where(lax.axis_index("param") == 0, domains, 0).astype(single_float)

time: 129 us -> 110 us (0.85)
  blocking collectives: 59.7 us -> 24.6 us
  matrix products: 27.5 us -> 2.74 us
  Pallas kernels: 10.9 us -> 34.3 us
  starting transfers between devices: 2.6 us -> 16.7 us
  waiting for transfers between devices: 15.6 us -> 26.5 us
  local copies, waits for them, and re-layouts: 9.94 us -> 3.25 us
    all_to_all x1 -> x0, blocking collectives: 31.3 us -> none  [local(): grads = lax.all_to_all(grads, 'ex', split_axis=1, concat_axis=0, tiled=True)]
    pallas_call x0 -> x4, Pallas kernels: none -> 26.2 us  [the longest x1 12.2 us: late_features(): pl.pallas_call(late_features_kernel, out_shape=jax.ShapeDtypeStruct(shape...]
    dot_general x6 -> x2, matrix products: 27.5 us -> 2.74 us  [the longest x1 1.66 us: local(): jnp.einsum('atd,adr->art', output_gradients.reshape(2, ex_rows * tokens,...]
    all_to_all x1 -> x4, starting transfers between devices: 2.6 us -> 16.7 us  [swap(): return lax.all_to_all(blocks, axes, split_axis=0, concat_axis=0, tiled=True)]
    all_to_all x1 -> x4, waiting for transfers between devices: 15.6 us -> 26.5 us  [swap(): return lax.all_to_all(blocks, axes, split_axis=0, concat_axis=0, tiled=True)]
    convert_element_type x2 -> x0, local copies, waits for them, and re-layouts: 4.29 us -> none  [local(): jnp.concatenate([first, second, third], axis=-1).astype(jnp.bfloat16)]
    all_gather x1, blocking collectives: 11.6 us -> 9 us  [local(): low_parts = lax.all_gather(partial_low, 'param')]
    concatenate x2 -> x0, local copies, waits for them, and re-layouts: 2.14 us -> none  [the longest x1 2.02 us: local(): jnp.concatenate([first, second, third], axis=-1).astype(jnp.bfloat16)]
  transfers between devices with their start and end apart: 1 -> 4, of which waited for: 1 -> 4; matrix products, arithmetic and copies ran while one was open for 1% -> 3% of each run, Pallas kernels for 0% -> 13%
where the time goes in v4:
time: 110 us; the launch traced here: 109 us
  Pallas kernels  34.3 us (31%)
  waiting for transfers between devices  26.5 us (24%)
  blocking collectives  24.6 us (22%)
  starting transfers between devices  16.7 us (15%)
  local copies, waits for them, and re-layouts  3.25 us (3%)
  matrix products  2.74 us (2%)
    all_to_all x4, waiting for transfers between devices, swap(): return lax.all_to_all(blocks, axes, split_axis=0, concat_axis=0, tiled=True)  26.5 us
    all_to_all x4, starting transfers between devices, swap(): return lax.all_to_all(blocks, axes, split_axis=0, concat_axis=0, tiled=True)  16.7 us
    all_to_all x1, blocking collectives, swap(): return lax.all_to_all(blocks, axes, split_axis=0, concat_axis=0, tiled=True)  15.6 us
    pallas_call x1, Pallas kernels, late_features(): pl.pallas_call(late_features_kernel, out_shape=jax.ShapeDtypeStruct(shape...  12.2 us
    pallas_call x1, Pallas kernels, early_features(): pl.pallas_call(early_features_kernel, out_shape=jax.ShapeDtypeStruct((exa...  11.5 us
    all_gather x1, blocking collectives, local(): low_parts = lax.all_gather(partial_low, 'param')  9 us
    pallas_call x1, Pallas kernels, solve(): pl.pallas_call(functools.partial(solve_kernel, count), out_shape=(jax.Sha...  7.73 us
    unnamed x8, local copies, waits for them, and re-layouts  2.27 us
  transfers between devices with their start and end apart: 4, of which 4 were waited for; matrix products, arithmetic and copies ran while one was open for 3% of the time, Pallas kernels for 13%

profile of v4, /device:TPU:0, one launch (start us, length us, event | category | flops | bytes accessed | tf_op | source)
XLA Modules:
  0.0 108.9 jit_solution(14622859078742865966)
XLA Ops:
  0.6 0.0 copy-start
  0.6 1.0 copy-done
  1.7 0.9 bitcast_bitcast_fusion
  2.6 6.3 %all-to-all-start.1 = ((bf16[8,8,32,128]{3,2,1,0:T(8,128)(2,1)}), bf16[8,8,32,128]{3,2,1,0:T(8,128)(2,1)S(1)}, u32[]{:S(2)}, u32[]{:S(2)}) async-start(bf16[8,8,32,128]{3,2,1,0:T(8,128)(2,1)} %bitcast_bitcast_fusion), calls=%async_computation.1 | async-start | bytes 1048576 | tf_op jit(solution)/shard_map/all_to_all | solution.py:27
  8.9 1.1 fusion.3
  10.0 1.7 %fusion.2 = f32[2,16,256]{2,1,0:T(8,128)S(1)} fusion(bf16[2,1024,16]{1,2,0:T(8,128)(2,1)} %param.10, bf16[2,256,1024]{2,1,0:T(8,128)(2,1)} %bitcast.26), kind=kOutput, calls=%fused_computation.6 | convolution fusion | flops 16777216 | bytes 1146880 | tf_op jit(solution)/shard_map/atd,adr->art/dot_general | solution.py:342
  11.7 9.0 %all_gather.3.parts_ref = f32[4,64,256]{2,1,0:T(8,128)S(1)} all-gather(f32[1,64,256]{2,1,0:T(8,128)S(1)} %bitcast.30), channel_id=1, replica_groups=mesh['param'=4,'ex'=8] {'param'}, dimensions={0}, use_global_device_ids=true | all-gather | bytes 327680 | tf_op jit(solution)/shard_map/all_gather | solution.py:355
  20.7 0.7 low_columns.1
  21.3 2.9 %all-to-all-done.1 = bf16[8,8,32,128]{3,2,1,0:T(8,128)(2,1)S(1)} async-done(((bf16[8,8,32,128]{3,2,1,0:T(8,128)(2,1)}), bf16[8,8,32,128]{3,2,1,0:T(8,128)(2,1)S(1)}, u32[]{:S(2)}, u32[]{:S(2)}) %all-to-all-start.1) | async-done | bytes 524320 | tf_op jit(solution)/shard_map/all_to_all | solution.py:27
  24.3 3.4 %all-to-all-start.2 = ((bf16[8,32,256]{2,1,0:T(8,128)(2,1)}), bf16[8,32,256]{2,1,0:T(8,128)(2,1)S(1)}, u32[]{:S(2)}, u32[]{:S(2)}) async-start(bf16[8,32,256]{2,1,0:T(8,128)(2,1)} %get-tuple-element.11), calls=%async_computation.2 | async-start | bytes 262144 | tf_op jit(solution)/shard_map/all_to_all | solution.py:27
  27.6 0.0 copy-start.1
  27.7 1.2 %copy-done.1 = bf16[2,8,32,1024]{3,2,1,0:T(8,128)(2,1)S(1)} copy-done((bf16[2,8,32,1024]{3,2,1,0:T(8,128)(2,1)S(1)}, bf16[2,8,32,1024]{3,2,1,0:T(8,128)(2,1)}, u32[]{:S(2)}) %copy-start.1) | copy-done | bytes 1048600
  28.9 1.8 %gradient_rows.1 = bf16[8,8,4096]{2,1,0:T(8,128)(2,1)} custom-call(bf16[2,8,32,1024]{3,2,1,0:T(8,128)(2,1)S(1)} %copy-done.1, bf16[256,128]{1,0:T(8,128)(2,1)S(1)} %get-tuple-element.8.low_ref), custom_call_target="tpu_custom_call" | custom-call | tf_op jit(solution)/shard_map/gradient_rows/pallas_call | solution.py:90
  30.7 3.7 %all-to-all-done.2.low_ref = bf16[8,32,256]{2,1,0:T(8,128)(2,1)S(1)} async-done(((bf16[8,32,256]{2,1,0:T(8,128)(2,1)}), bf16[8,32,256]{2,1,0:T(8,128)(2,1)S(1)}, u32[]{:S(2)}, u32[]{:S(2)}) %all-to-all-start.2) | async-done | bytes 131104 | tf_op jit(solution)/shard_map/all_to_all | solution.py:27
  34.4 3.5 %all-to-all-start = ((bf16[8,8,4096]{2,1,0:T(8,128)(2,1)}), bf16[8,8,4096]{2,1,0:T(8,128)(2,1)S(1)}, u32[]{:S(2)}, u32[]{:S(2)}) async-start(bf16[8,8,4096]{2,1,0:T(8,128)(2,1)} %gradient_rows.1), calls=%async_computation | async-start | bytes 1048576 | tf_op jit(solution)/shard_map/all_to_all | solution.py:27
  37.9 0.0 copy-start.3
  37.9 0.0 copy-start.2
  37.9 11.5 %early_features.1.total_ref = f32[64,4096]{1,0:T(8,128)S(1)} custom-call(bf16[64,32,128]{2,1,0:T(8,128)(2,1)S(1)} %bitcast.27, bf16[8,32,256]{2,1,0:T(8,128)(2,1)S(1)} %all-to-all-done.2.low_ref, bf16[128,64,4096]{2,1,0:T(8,128)(2,1)} %bitcast.6.rows_ref), custom_call_target="tpu_custom_call" | custom-call | tf_op jit(solution)/shard_map/early_features/pallas_call | solution.py:174
  49.3 3.8 %all-to-all-done = bf16[8,8,4096]{2,1,0:T(8,128)(2,1)S(1)} async-done(((bf16[8,8,4096]{2,1,0:T(8,128)(2,1)}), bf16[8,8,4096]{2,1,0:T(8,128)(2,1)S(1)}, u32[]{:S(2)}, u32[]{:S(2)}) %all-to-all-start) | async-done | bytes 524320 | tf_op jit(solution)/shard_map/all_to_all | solution.py:27
  53.1 12.2 %late_features.1 = bf16[32,64,128]{2,1,0:T(8,128)(2,1)} custom-call(bf16[64,4096]{1,0:T(8,128)(2,1)S(1)} %bitcast.28, bf16[128,64,4096]{2,1,0:T(8,128)(2,1)} %bitcast.6.rows_ref, f32[64,4096]{1,0:T(8,128)S(1)} %early_features.1.total_ref), custom_call_target="tpu_custom_call" | custom-call | tf_op jit(solution)/shard_map/late_features/pallas_call | solution.py:204
  65.4 3.5 %all-to-all-start.3 = ((bf16[32,64,128]{2,1,0:T(8,128)(2,1)}), bf16[32,64,128]{2,1,0:T(8,128)(2,1)S(1)}, u32[]{:S(2)}, u32[]{:S(2)}) async-start(bf16[32,64,128]{2,1,0:T(8,128)(2,1)} %late_features.1), calls=%async_computation.3 | async-start | bytes 1048576 | tf_op jit(solution)/shard_map/all_to_all | solution.py:27
  68.9 0.0 copy-done.3
  68.9 0.1 fusion.1
  69.0 0.1 pad_bitcast_fusion.row_ref
  69.1 16.1 %all-to-all-done.3.blocks_ref = bf16[32,64,128]{2,1,0:T(8,128)(2,1)S(1)} async-done(((bf16[32,64,128]{2,1,0:T(8,128)(2,1)}), bf16[32,64,128]{2,1,0:T(8,128)(2,1)S(1)}, u32[]{:S(2)}, u32[]{:S(2)}) %all-to-all-start.3) | async-done | bytes 524320 | tf_op jit(solution)/shard_map/all_to_all | solution.py:27
  85.2 0.4 packed_gram.1
  85.6 15.6 %all_to_all.25.pieces_ref = f32[32,24,128]{2,1,0:T(8,128)S(1)} all-to-all(f32[32,24,128]{2,1,0:T(8,128)S(1)} %packed_gram.1), channel_id=1, replica_groups=mesh['param'=4,'ex'=8] {'param','ex'}, dimensions={0} | all-to-all | bytes 786432 | tf_op jit(solution)/shard_map/all_to_all | solution.py:27
  101.2 0.0 copy-done.2
  101.2 7.7 %solve.1 = (f32[8,64]{1,0:T(8,128)}, f32[4,64]{1,0:T(4,128)}) custom-call(s32[1]{0:T(128)} %bitcast.slot_ref, f32[32,24,128]{2,1,0:T(8,128)S(1)} %all_to_all.25.pieces_ref, s32[1,64]{1,0:T(1,128)S(1)} %bitcast.29), custom_call_target="tpu_custom_call" | custom-call | tf_op jit(solution)/shard_map/solve/pallas_call | solution.py:301
  (2 shorter events, 0.0 us)
Async XLA Ops:
  0.6 1.0 copy-start
  2.6 21.7 %all-to-all-start.1 = ((bf16[8,8,32,128]{3,2,1,0:T(8,128)(2,1)}), bf16[8,8,32,128]{3,2,1,0:T(8,128)(2,1)S(1)}, u32[]{:S(2)}, u32[]{:S(2)}) async-start(bf16[8,8,32,128]{3,2,1,0:T(8,128)(2,1)} %bitcast_bitcast_fusion), calls=%async_computation.1 | async-start | bytes 1048576 | tf_op jit(solution)/shard_map/all_to_all | solution.py:27
  24.3 10.1 %all-to-all-start.2 = ((bf16[8,32,256]{2,1,0:T(8,128)(2,1)}), bf16[8,32,256]{2,1,0:T(8,128)(2,1)S(1)}, u32[]{:S(2)}, u32[]{:S(2)}) async-start(bf16[8,32,256]{2,1,0:T(8,128)(2,1)} %get-tuple-element.11), calls=%async_computation.2 | async-start | bytes 262144 | tf_op jit(solution)/shard_map/all_to_all | solution.py:27
  27.6 1.2 %copy-start.1 = (bf16[2,8,32,1024]{3,2,1,0:T(8,128)(2,1)S(1)}, bf16[2,8,32,1024]{3,2,1,0:T(8,128)(2,1)}, u32[]{:S(2)}) copy-start(bf16[2,8,32,1024]{3,2,1,0:T(8,128)(2,1)} %out_ref.1) | copy-start | bytes 3145732
  34.4 18.8 %all-to-all-start = ((bf16[8,8,4096]{2,1,0:T(8,128)(2,1)}), bf16[8,8,4096]{2,1,0:T(8,128)(2,1)S(1)}, u32[]{:S(2)}, u32[]{:S(2)}) async-start(bf16[8,8,4096]{2,1,0:T(8,128)(2,1)} %gradient_rows.1), calls=%async_computation | async-start | bytes 1048576 | tf_op jit(solution)/shard_map/all_to_all | solution.py:27
  37.9 31.1 %copy-start.3 = (s32[8]{0:T(128)S(1)}, s32[8]{0:T(128)}, u32[]{:S(2)}) copy-start(s32[8]{0:T(128)} %param.12) | copy-start | bytes 100
  37.9 63.4 %copy-start.2 = (s32[64]{0:T(128)S(1)}, s32[64]{0:T(128)}, u32[]{:S(2)}) copy-start(s32[64]{0:T(128)} %param.13) | copy-start | bytes 772
  65.4 19.9 %all-to-all-start.3 = ((bf16[32,64,128]{2,1,0:T(8,128)(2,1)}), bf16[32,64,128]{2,1,0:T(8,128)(2,1)S(1)}, u32[]{:S(2)}, u32[]{:S(2)}) async-start(bf16[32,64,128]{2,1,0:T(8,128)(2,1)} %late_features.1), calls=%async_computation.3 | async-start | bytes 1048576 | tf_op jit(solution)/shard_map/all_to_all | solution.py:27

commit v5 on v4

--- a/solution.py
+++ b/solution.py
@@ -29,6 +29,10 @@
 
 def spread(columns):
     return jnp.concatenate([columns] * FOLD, axis=0).T
+
+
+def meets(ex_size):
+    return ex_size == 8
 
 
 def low_columns_kernel(parts_ref, queries_ref, rest_ref):
@@ -131,14 +135,20 @@
             copy(i + slots).start()
 
 
-def early_features_kernel(tokens_ref, low_ref, rows_ref, total_ref, grads_ref, tall_ref, wide_ref, held_ref, sems):
+def early_features_kernel(parts, offset_ref, tokens_ref, *refs):
+    rows_ref, total_ref, low_ref, grads_ref, tall_ref, wide_ref, held_ref, sems = refs[parts:]
     examples, length, channels = tokens_ref.shape
     sources = low_ref.shape[0]
     each = examples // sources
 
     def prepare():
+        first = 0
+        for part in refs[:parts]:
+            low_ref[first : first + part.shape[0]] = part[...]
+            first += part.shape[0]
+
         def source(index, carry):
-            factors = spread(low_ref[index].astype(jnp.float32)).astype(jnp.bfloat16)
+            factors = spread(low_ref[lax.bitwise_xor(index, offset_ref[0])].astype(jnp.float32)).astype(jnp.bfloat16)
             for n in range(each):
                 tall_ref[n * channels : (n + 1) * channels, :] = lax.dot_general(
                     tokens_ref[index * each + n],
@@ -168,23 +178,27 @@
     ]
 
 
-def early_features(tokens, low, rows):
+def early_features(tokens, offset, low, rows):
     examples, _, channels = tokens.shape
+    sources = sum(part.shape[0] for part in low)
     in_vmem = pl.BlockSpec(memory_space=pltpu.VMEM)
     return pl.pallas_call(
-        early_features_kernel,
+        functools.partial(early_features_kernel, len(low)),
         out_shape=jax.ShapeDtypeStruct((examples, rows.shape[2]), jnp.float32),
-        in_specs=[in_vmem, in_vmem, pl.BlockSpec(memory_space=pl.ANY)],
+        in_specs=[pl.BlockSpec(memory_space=pltpu.SMEM), in_vmem]
+        + [in_vmem] * len(low)
+        + [pl.BlockSpec(memory_space=pl.ANY)],
         out_specs=in_vmem,
         scratch_shapes=[
+            pltpu.VMEM((sources, *low[0].shape[1:]), jnp.bfloat16),
             pltpu.VMEM((examples, channels * 128 // FOLD), jnp.bfloat16),
-            pltpu.VMEM((examples // low.shape[0] * channels, 128), jnp.float32),
+            pltpu.VMEM((examples // sources * channels, 128), jnp.float32),
             pltpu.VMEM((channels // FOLD * examples, 128), jnp.float32),
         ]
         + held_rows(rows),
         compiler_params=pltpu.CompilerParams(vmem_limit_bytes=40 << 20),
         name="early_features",
-    )(tokens, low, rows)
+    )(jnp.reshape(offset, (1,)), tokens, *low, rows)
 
 
 def late_features_kernel(grads_ref, rows_ref, total_ref, out_ref, acc_ref, held_ref, sems):
@@ -210,6 +224,10 @@
         compiler_params=pltpu.CompilerParams(vmem_limit_bytes=40 << 20),
         name="late_features",
     )(grads, rows, total)
+
+
+def flip(array, bits):
+    return lax.ppermute(array, "ex", [(i, i ^ bits) for i in range(lax.axis_size("ex"))])
 
 
 def packs(example_count):
@@ -270,18 +288,28 @@
     gram = gram * lax.rsqrt(jnp.sum(on_diagonal, axis=0, keepdims=True) + 1e-06)
 
     work_ref[...] = gram + jnp.where(rows == cols, 0.25, 0.0)
-
-    def sweep(k, carry):
+    along, down = cols[:1], rows[:, :1]
+
+    def at(array, k):
+        return jnp.sum(jnp.where(along == k, array, 0.0), axis=1, keepdims=True)
+
+    def sweep(step, carry):
+        k = 2 * step
         held = work_ref[...]
-        row = work_ref[pl.ds(k, 1), :]
-        pivot = 1.0 / jnp.sum(jnp.where(cols[:1] == k, row, 0.0), axis=1, keepdims=True)
-        column = jnp.sum(jnp.where(cols == k, held, 0.0), axis=1, keepdims=True)
-        row = jnp.where(cols[:1] == k, -pivot, row * pivot)
-        column = jnp.where(rows[:, :1] == k, -1.0, column)
-        work_ref[...] = jnp.where((cols == k) | (rows == k), 0.0, held) - column * row
+        row0, row1 = work_ref[pl.ds(k, 1), :], work_ref[pl.ds(k + 1, 1), :]
+        a, b, d = at(row0, k), at(row1, k), at(row1, k + 1)
+        scale = 1.0 / (a * d - b * b)
+        a, b, d = a * scale, b * scale, d * scale
+        column0, column1 = at(held, k), at(held, k + 1)
+        new0 = jnp.where(along == k, -d, jnp.where(along == k + 1, b, d * row0 - b * row1))
+        new1 = jnp.where(along == k, b, jnp.where(along == k + 1, -a, a * row1 - b * row0))
+        column0 = jnp.where(down == k, -1.0, jnp.where(down == k + 1, 0.0, column0))
+        column1 = jnp.where(down == k, 0.0, jnp.where(down == k + 1, -1.0, column1))
+        swept = (cols == k) | (cols == k + 1) | (rows == k) | (rows == k + 1)
+        work_ref[...] = jnp.where(swept, 0.0, held) - column0 * new0 - column1 * new1
         return carry
 
-    lax.fori_loop(0, count, sweep, 0)
+    lax.fori_loop(0, count // 2, sweep, 0)
 
     targets = ids_ref.shape[1]
     places = lax.broadcasted_iota(jnp.int32, (count, targets), 0)
@@ -353,13 +381,22 @@
     )
     partial_low = jnp.concatenate([up_terms, down_terms], axis=0).reshape(4 * rank, ex_rows * tokens)
     low_parts = lax.all_gather(partial_low, "param")
-    queries, rest = low_columns(low_parts, ex_size)
-    queries, moved = lax.optimization_barrier((queries, moved))
-
-    queries = swap(queries, "ex")
-    grads = swap(gradient_rows(output_gradients, rest, ex_size), "ex").reshape(example_count, owned * 2 * rank)
+    if meets(ex_size):
+        queries, rest = low_columns(low_parts, 1)
+        pair = jnp.concatenate([queries, flip(queries, 1)], axis=0)
+        queries = [pair] + [flip(pair, bits) for bits in (2, 4, 6)]
+        offset = lax.axis_index("ex")
+    else:
+        queries, rest = low_columns(low_parts, ex_size)
+        queries, moved = lax.optimization_barrier((queries, moved))
+        queries = [swap(queries, "ex")]
+        offset = jnp.int32(0)
+
+    wire = gradient_rows(output_gradients, rest, ex_size)
+    queries, wire = lax.optimization_barrier((queries, wire))
+    grads = swap(wire, "ex").reshape(example_count, owned * 2 * rank)
     rows = projection.reshape(owned, 4 * rank, K)
-    total = early_features(moved, queries, rows)
+    total = early_features(moved, offset, queries, rows)
     partial_sums = late_features(grads, rows, total, devices)
     if partial_sums.ndim == 2:
         partial_sums = partial_sums.reshape(example_count, devices, K // devices).transpose(1, 0, 2)

time: 110 us -> 103 us (0.936)
  Pallas kernels: 34.3 us -> 30.9 us
  waiting for transfers between devices: 26.5 us -> 23.8 us
    all_to_all x4 -> x3, waiting for transfers between devices: 26.5 us -> 19.9 us  [swap(): return lax.all_to_all(blocks, axes, split_axis=0, concat_axis=0, tiled=True)]
    ppermute x0 -> x4, starting transfers between devices: none -> 4.46 us  [flip(): lax.ppermute(array, 'ex', [(i, i ^ bits) for i in range(lax.axis_size('ex...]
    all_to_all x4 -> x3, starting transfers between devices: 16.7 us -> 12.4 us  [swap(): return lax.all_to_all(blocks, axes, split_axis=0, concat_axis=0, tiled=True)]
    ppermute x0 -> x4, waiting for transfers between devices: none -> 3.84 us  [flip(): lax.ppermute(array, 'ex', [(i, i ^ bits) for i in range(lax.axis_size('ex...]
    pallas_call x1, Pallas kernels: 7.73 us -> 4.9 us  [solve(): pl.pallas_call(functools.partial(solve_kernel, count), out_shape=(jax.Sha...]
    unnamed x8 -> x9, local copies, waits for them, and re-layouts: 2.27 us -> 2.28 us
  transfers between devices with their start and end apart: 4 -> 7, of which waited for: 4 -> 4; matrix products, arithmetic and copies ran while one was open for 3% -> 3% of each run, Pallas kernels for 13% -> 13%
where the time goes in v5:
time: 103 us
  Pallas kernels  30.9 us (30%)
  blocking collectives  24.5 us (24%)
  waiting for transfers between devices  23.8 us (23%)
  starting transfers between devices  16.9 us (16%)
  local copies, waits for them, and re-layouts  3.26 us (3%)
  matrix products  2.74 us (3%)
    all_to_all x3, waiting for transfers between devices, swap(): return lax.all_to_all(blocks, axes, split_axis=0, concat_axis=0, tiled=True)  19.9 us
    all_to_all x1, blocking collectives, swap(): return lax.all_to_all(blocks, axes, split_axis=0, concat_axis=0, tiled=True)  15.5 us
    all_to_all x3, starting transfers between devices, swap(): return lax.all_to_all(blocks, axes, split_axis=0, concat_axis=0, tiled=True)  12.4 us
    pallas_call x1, Pallas kernels, late_features(): pl.pallas_call(late_features_kernel, out_shape=jax.ShapeDtypeStruct(shape...  12.2 us
    pallas_call x1, Pallas kernels, early_features(): pl.pallas_call(functools.partial(early_features_kernel, len(low)), out_sh...  11.5 us
    all_gather x1, blocking collectives, local(): low_parts = lax.all_gather(partial_low, 'param')  9 us
    pallas_call x1, Pallas kernels, solve(): pl.pallas_call(functools.partial(solve_kernel, count), out_shape=(jax.Sha...  4.9 us
    ppermute x4, starting transfers between devices, flip(): lax.ppermute(array, 'ex', [(i, i ^ bits) for i in range(lax.axis_size('ex...  4.46 us
  transfers between devices with their start and end apart: 7, of which 4 were waited for; matrix products, arithmetic and copies ran while one was open for 3% of the time, Pallas kernels for 13%

profile of v5, /device:TPU:0, one launch (start us, length us, event | category | flops | bytes accessed | tf_op | source)
XLA Modules:
  0.0 102.9 jit_solution(2181761275884332642)
XLA Ops:
  0.6 0.0 copy-start
  0.6 1.0 %copy-done = bf16[8,32,1024]{2,1,0:T(8,128)(2,1)S(1)} copy-done((bf16[8,32,1024]{2,1,0:T(8,128)(2,1)S(1)}, bf16[8,32,1024]{2,1,0:T(8,128)(2,1)}, u32[]{:S(2)}) %copy-start) | copy-done | bytes 524312
  1.7 0.9 bitcast_bitcast_fusion
  2.6 6.3 %all-to-all-start.1 = ((bf16[8,8,32,128]{3,2,1,0:T(8,128)(2,1)}), bf16[8,8,32,128]{3,2,1,0:T(8,128)(2,1)S(1)}, u32[]{:S(2)}, u32[]{:S(2)}) async-start(bf16[8,8,32,128]{3,2,1,0:T(8,128)(2,1)} %bitcast_bitcast_fusion), calls=%async_computation.1 | async-start | bytes 1048576 | tf_op jit(solution)/shard_map/all_to_all | solution.py:27
  8.9 1.1 %fusion.3 = f32[2,16,256]{2,1,0:T(8,128)S(1)} fusion(bf16[2,16,1024]{2,1,0:T(8,128)(2,1)} %param.9, bf16[256,1024,1]{1,0,2:T(8,128)(2,1)S(1)} %bitcast.26), kind=kOutput, calls=%fused_computation.9 | convolution fusion | flops 16777216 | bytes 622592 | tf_op jit(solution)/shard_map/td,ard->art/dot_general | solution.py:376
  10.0 1.7 %fusion.2 = f32[2,16,256]{2,1,0:T(8,128)S(1)} fusion(bf16[2,1024,16]{1,2,0:T(8,128)(2,1)} %param.10, bf16[2,256,1024]{2,1,0:T(8,128)(2,1)} %bitcast.27), kind=kOutput, calls=%fused_computation.8 | convolution fusion | flops 16777216 | bytes 1146880 | tf_op jit(solution)/shard_map/atd,adr->art/dot_general | solution.py:370
  11.7 9.0 %all_gather.3.parts_ref = f32[4,64,256]{2,1,0:T(8,128)S(1)} all-gather(f32[1,64,256]{2,1,0:T(8,128)S(1)} %bitcast.31), channel_id=1, replica_groups=mesh['param'=4,'ex'=8] {'param'}, dimensions={0}, use_global_device_ids=true | all-gather | bytes 327680 | tf_op jit(solution)/shard_map/all_gather | solution.py:383
  20.7 0.1 low_columns.1
  20.8 0.1 collective-permute-start
  20.9 1.2 %collective-permute-done = bf16[1,32,256]{2,1,0:T(8,128)(2,1)S(1)} collective-permute-done((bf16[1,32,256]{2,1,0:T(8,128)(2,1)S(1)}, bf16[1,32,256]{2,1,0:T(8,128)(2,1)S(1)}, u32[]{:S(2)}, u32[]{:S(2)}) %collective-permute-start) | collective-permute-done | bytes 16416 | tf_op jit(solution)/shard_map/ppermute | solution.py:230
  22.0 2.0 %collective-permute-start.1 = (bf16[2,32,256]{2,1,0:T(8,128)(2,1)S(1)}, bf16[2,32,256]{2,1,0:T(8,128)(2,1)S(1)}, u32[]{:S(2)}, u32[]{:S(2)}) collective-permute-start(bf16[2,32,256]{2,1,0:T(8,128)(2,1)S(1)} %constant_dynamic-update-slice_fusion.refs_0_), channel_id=1, source_target_pairs={{0,2},{1,3},{2,0},{3,1},{4,6},{5,7},{6,4},{7,5},{8,10},{9,11},{10,... | collective-permute-start | bytes 98312 | tf_op jit(solution)/shard_map/ppermute | solution.py:230
  24.1 2.4 %collective-permute-start.2 = (bf16[2,32,256]{2,1,0:T(8,128)(2,1)S(1)}, bf16[2,32,256]{2,1,0:T(8,128)(2,1)S(1)}, u32[]{:S(2)}, u32[]{:S(2)}) collective-permute-start(bf16[2,32,256]{2,1,0:T(8,128)(2,1)S(1)} %constant_dynamic-update-slice_fusion.refs_0_), channel_id=1, source_target_pairs={{0,4},{1,5},{2,6},{3,7},{4,0},{5,1},{6,2},{7,3},{8,12},{9,13},{10,... | collective-permute-start | bytes 98312 | tf_op jit(solution)/shard_map/ppermute | solution.py:230
  26.4 0.0 collective-permute-start.3
  26.4 0.0 copy-start.1
  26.4 1.2 %copy-done.1 = bf16[2,8,32,1024]{3,2,1,0:T(8,128)(2,1)S(1)} copy-done((bf16[2,8,32,1024]{3,2,1,0:T(8,128)(2,1)S(1)}, bf16[2,8,32,1024]{3,2,1,0:T(8,128)(2,1)}, u32[]{:S(2)}) %copy-start.1) | copy-done | bytes 1048600
  27.6 1.8 %gradient_rows.1 = bf16[8,8,4096]{2,1,0:T(8,128)(2,1)} custom-call(bf16[2,8,32,1024]{3,2,1,0:T(8,128)(2,1)S(1)} %copy-done.1, bf16[256,128]{1,0:T(8,128)(2,1)S(1)} %get-tuple-element.12.low_ref), custom_call_target="tpu_custom_call" | custom-call | tf_op jit(solution)/shard_map/gradient_rows/pallas_call | solution.py:94
  29.4 0.0 collective-permute-done.1.refs_1_
  29.5 0.0 collective-permute-done.2.refs_2_
  29.5 2.7 %collective-permute-done.3.refs_3_ = bf16[2,32,256]{2,1,0:T(8,128)(2,1)S(1)} collective-permute-done((bf16[2,32,256]{2,1,0:T(8,128)(2,1)S(1)}, bf16[2,32,256]{2,1,0:T(8,128)(2,1)S(1)}, u32[]{:S(2)}, u32[]{:S(2)}) %collective-permute-start.3) | collective-permute-done | bytes 32800 | tf_op jit(solution)/shard_map/ppermute | solution.py:230
  32.1 0.0 all-to-all-done.1
  32.1 3.5 %all-to-all-start = ((bf16[8,8,4096]{2,1,0:T(8,128)(2,1)}), bf16[8,8,4096]{2,1,0:T(8,128)(2,1)S(1)}, u32[]{:S(2)}, u32[]{:S(2)}) async-start(bf16[8,8,4096]{2,1,0:T(8,128)(2,1)} %gradient_rows.1), calls=%async_computation | async-start | bytes 1048576 | tf_op jit(solution)/shard_map/all_to_all | solution.py:27
  35.6 0.0 copy-start.3
  35.6 0.0 copy-start.2
  35.7 11.5 %early_features.1.total_ref = f32[64,4096]{1,0:T(8,128)S(1)} custom-call(s32[1]{0:T(128)} %bitcast.7.offset_ref, bf16[64,32,128]{2,1,0:T(8,128)(2,1)S(1)} %bitcast.28, bf16[2,32,256]{2,1,0:T(8,128)(2,1)S(1)} %constant_dynamic-update-slice_fusion.refs_0_, bf16[2,32,256]{2,1,0:T(8,128)(2,1)S(1)} %collective-permute-done.1.refs_1_, ...), custom_call_target="tpu_custom_call" | custom-call | tf_op jit(solution)/shard_map/early_features/pallas_call | solution.py:185
  47.1 3.8 %all-to-all-done = bf16[8,8,4096]{2,1,0:T(8,128)(2,1)S(1)} async-done(((bf16[8,8,4096]{2,1,0:T(8,128)(2,1)}), bf16[8,8,4096]{2,1,0:T(8,128)(2,1)S(1)}, u32[]{:S(2)}, u32[]{:S(2)}) %all-to-all-start) | async-done | bytes 524320 | tf_op jit(solution)/shard_map/all_to_all | solution.py:27
  50.9 12.2 %late_features.1 = bf16[32,64,128]{2,1,0:T(8,128)(2,1)} custom-call(bf16[64,4096]{1,0:T(8,128)(2,1)S(1)} %bitcast.29, bf16[128,64,4096]{2,1,0:T(8,128)(2,1)} %bitcast.6.refs_4_.rows_ref, f32[64,4096]{1,0:T(8,128)S(1)} %early_features.1.total_ref), custom_call_target="tpu_custom_call" | custom-call | tf_op jit(solution)/shard_map/late_features/pallas_call | solution.py:218
  63.2 2.6 %all-to-all-start.2 = ((bf16[32,64,128]{2,1,0:T(8,128)(2,1)}), bf16[32,64,128]{2,1,0:T(8,128)(2,1)S(1)}, u32[]{:S(2)}, u32[]{:S(2)}) async-start(bf16[32,64,128]{2,1,0:T(8,128)(2,1)} %late_features.1), calls=%async_computation.2 | async-start | bytes 1048576 | tf_op jit(solution)/shard_map/all_to_all | solution.py:27
  65.8 0.0 copy-done.3
  65.8 0.1 fusion.1
  65.9 0.1 pad_bitcast_fusion.row_ref
  66.0 16.1 %all-to-all-done.2.blocks_ref = bf16[32,64,128]{2,1,0:T(8,128)(2,1)S(1)} async-done(((bf16[32,64,128]{2,1,0:T(8,128)(2,1)}), bf16[32,64,128]{2,1,0:T(8,128)(2,1)S(1)}, u32[]{:S(2)}, u32[]{:S(2)}) %all-to-all-start.2) | async-done | bytes 524320 | tf_op jit(solution)/shard_map/all_to_all | solution.py:27
  82.1 0.4 packed_gram.1
  82.5 15.5 %all_to_all.20.pieces_ref = f32[32,24,128]{2,1,0:T(8,128)S(1)} all-to-all(f32[32,24,128]{2,1,0:T(8,128)S(1)} %packed_gram.1), channel_id=1, replica_groups=mesh['param'=4,'ex'=8] {'param','ex'}, dimensions={0} | all-to-all | bytes 786432 | tf_op jit(solution)/shard_map/all_to_all | solution.py:27
  98.0 0.0 copy-done.2
  98.0 4.9 %solve.1 = (f32[8,64]{1,0:T(8,128)}, f32[4,64]{1,0:T(4,128)}) custom-call(s32[1]{0:T(128)} %bitcast.slot_ref, f32[32,24,128]{2,1,0:T(8,128)S(1)} %all_to_all.20.pieces_ref, s32[1,64]{1,0:T(1,128)S(1)} %bitcast.30), custom_call_target="tpu_custom_call" | custom-call | tf_op jit(solution)/shard_map/solve/pallas_call | solution.py:329
  (4 shorter events, 0.0 us)
Async XLA Ops:
  0.6 1.0 %copy-start = (bf16[8,32,1024]{2,1,0:T(8,128)(2,1)S(1)}, bf16[8,32,1024]{2,1,0:T(8,128)(2,1)}, u32[]{:S(2)}) copy-start(bf16[8,32,1024]{2,1,0:T(8,128)(2,1)} %param.7) | copy-start | bytes 1572868
  2.6 29.6 %all-to-all-start.1 = ((bf16[8,8,32,128]{3,2,1,0:T(8,128)(2,1)}), bf16[8,8,32,128]{3,2,1,0:T(8,128)(2,1)S(1)}, u32[]{:S(2)}, u32[]{:S(2)}) async-start(bf16[8,8,32,128]{3,2,1,0:T(8,128)(2,1)} %bitcast_bitcast_fusion), calls=%async_computation.1 | async-start | bytes 1048576 | tf_op jit(solution)/shard_map/all_to_all | solution.py:27
  20.8 1.2 %collective-permute-start = (bf16[1,32,256]{2,1,0:T(8,128)(2,1)S(1)}, bf16[1,32,256]{2,1,0:T(8,128)(2,1)S(1)}, u32[]{:S(2)}, u32[]{:S(2)}) collective-permute-start(bf16[1,32,256]{2,1,0:T(8,128)(2,1)S(1)} %get-tuple-element.11), channel_id=1, source_target_pairs={{0,1},{1,0},{2,3},{3,2},{4,5},{5,4},{6,7},{7,6},{8,9},{9,8},{10,11... | collective-permute-start | bytes 49160 | tf_op jit(solution)/shard_map/ppermute | solution.py:230
  22.0 7.4 %collective-permute-start.1 = (bf16[2,32,256]{2,1,0:T(8,128)(2,1)S(1)}, bf16[2,32,256]{2,1,0:T(8,128)(2,1)S(1)}, u32[]{:S(2)}, u32[]{:S(2)}) collective-permute-start(bf16[2,32,256]{2,1,0:T(8,128)(2,1)S(1)} %constant_dynamic-update-slice_fusion.refs_0_), channel_id=1, source_target_pairs={{0,2},{1,3},{2,0},{3,1},{4,6},{5,7},{6,4},{7,5},{8,10},{9,11},{10,... | collective-permute-start | bytes 98312 | tf_op jit(solution)/shard_map/ppermute | solution.py:230
  24.1 5.4 %collective-permute-start.2 = (bf16[2,32,256]{2,1,0:T(8,128)(2,1)S(1)}, bf16[2,32,256]{2,1,0:T(8,128)(2,1)S(1)}, u32[]{:S(2)}, u32[]{:S(2)}) collective-permute-start(bf16[2,32,256]{2,1,0:T(8,128)(2,1)S(1)} %constant_dynamic-update-slice_fusion.refs_0_), channel_id=1, source_target_pairs={{0,4},{1,5},{2,6},{3,7},{4,0},{5,1},{6,2},{7,3},{8,12},{9,13},{10,... | collective-permute-start | bytes 98312 | tf_op jit(solution)/shard_map/ppermute | solution.py:230
  26.4 5.7 %collective-permute-start.3 = (bf16[2,32,256]{2,1,0:T(8,128)(2,1)S(1)}, bf16[2,32,256]{2,1,0:T(8,128)(2,1)S(1)}, u32[]{:S(2)}, u32[]{:S(2)}) collective-permute-start(bf16[2,32,256]{2,1,0:T(8,128)(2,1)S(1)} %constant_dynamic-update-slice_fusion.refs_0_), channel_id=1, source_target_pairs={{0,6},{1,7},{2,4},{3,5},{4,2},{5,3},{6,0},{7,1},{8,14},{9,15},{10,... | collective-permute-start | bytes 98312 | tf_op jit(solution)/shard_map/ppermute | solution.py:230
  26.4 1.2 %copy-start.1 = (bf16[2,8,32,1024]{3,2,1,0:T(8,128)(2,1)S(1)}, bf16[2,8,32,1024]{3,2,1,0:T(8,128)(2,1)}, u32[]{:S(2)}) copy-start(bf16[2,8,32,1024]{3,2,1,0:T(8,128)(2,1)} %out_ref.1) | copy-start | bytes 3145732
  32.1 18.8 %all-to-all-start = ((bf16[8,8,4096]{2,1,0:T(8,128)(2,1)}), bf16[8,8,4096]{2,1,0:T(8,128)(2,1)S(1)}, u32[]{:S(2)}, u32[]{:S(2)}) async-start(bf16[8,8,4096]{2,1,0:T(8,128)(2,1)} %gradient_rows.1), calls=%async_computation | async-start | bytes 1048576 | tf_op jit(solution)/shard_map/all_to_all | solution.py:27
  35.6 30.2 %copy-start.3 = (s32[8]{0:T(128)S(1)}, s32[8]{0:T(128)}, u32[]{:S(2)}) copy-start(s32[8]{0:T(128)} %param.12) | copy-start | bytes 100
  35.6 62.4 %copy-start.2 = (s32[64]{0:T(128)S(1)}, s32[64]{0:T(128)}, u32[]{:S(2)}) copy-start(s32[64]{0:T(128)} %param.13) | copy-start | bytes 772
  63.2 19.0 %all-to-all-start.2 = ((bf16[32,64,128]{2,1,0:T(8,128)(2,1)}), bf16[32,64,128]{2,1,0:T(8,128)(2,1)S(1)}, u32[]{:S(2)}, u32[]{:S(2)}) async-start(bf16[32,64,128]{2,1,0:T(8,128)(2,1)} %late_features.1), calls=%async_computation.2 | async-start | bytes 1048576 | tf_op jit(solution)/shard_map/all_to_all | solution.py:27

commit v6 on v5

--- a/solution.py
+++ b/solution.py
@@ -23,8 +23,11 @@
     )
 
 
-def swap(blocks, axes):
-    return lax.all_to_all(blocks, axes, split_axis=0, concat_axis=0, tiled=True)
+def swap(blocks, axes, groups=1):
+    members = None
+    if groups > 1:
+        members = [list(range(i, groups * blocks.shape[0], groups)) for i in range(groups)]
+    return lax.all_to_all(blocks, axes, split_axis=0, concat_axis=0, axis_index_groups=members, tiled=True)
 
 
 def spread(columns):
@@ -203,17 +206,38 @@
 
 def late_features_kernel(grads_ref, rows_ref, total_ref, out_ref, acc_ref, held_ref, sems):
     multiply_rows(grads_ref, rows_ref, 1, held_ref, sems, acc_ref, lambda: None, total_ref)
-    if len(out_ref.shape) == 3:
-        lanes = out_ref.shape[2]
-        for block in range(out_ref.shape[0]):
-            out_ref[block] = acc_ref[:, block * lanes : (block + 1) * lanes].astype(out_ref.dtype)
-    else:
-        out_ref[...] = acc_ref[...].astype(out_ref.dtype)
-
-
-def late_features(grads, rows, total, blocks):
+    out_ref[...] = acc_ref[...].astype(out_ref.dtype)
+
+
+def late_features_paired_kernel(core_ref, grads_ref, rows_ref, total_ref, own_ref, other_ref, acc_ref, held_ref, sems):
+    multiply_rows(grads_ref, rows_ref, 1, held_ref, sems, acc_ref, lambda: None, total_ref)
+    pairs, _, lanes = own_ref.shape
+    first = core_ref[0] == 0
+    for pair in range(pairs):
+        even = acc_ref[:, 2 * pair * lanes : (2 * pair + 1) * lanes]
+        odd = acc_ref[:, (2 * pair + 1) * lanes : (2 * pair + 2) * lanes]
+        own_ref[pair] = jnp.where(first, even, odd)
+        other_ref[pair] = jnp.where(first, odd, even)
+
+
+def late_features_paired(grads, rows, total, core, pairs):
     examples, columns = total.shape
-    shape = (examples, columns) if columns // blocks % 128 else (blocks, examples, columns // blocks)
+    in_vmem = pl.BlockSpec(memory_space=pltpu.VMEM)
+    shape = jax.ShapeDtypeStruct((pairs, examples, columns // pairs // 2), jnp.float32)
+    return pl.pallas_call(
+        late_features_paired_kernel,
+        out_shape=(shape, shape),
+        in_specs=[pl.BlockSpec(memory_space=pltpu.SMEM), in_vmem, pl.BlockSpec(memory_space=pl.ANY), in_vmem],
+        out_specs=(in_vmem, in_vmem),
+        scratch_shapes=[pltpu.VMEM((examples, columns), jnp.float32)] + held_rows(rows),
+        compiler_params=pltpu.CompilerParams(vmem_limit_bytes=40 << 20),
+        name="late_features",
+    )(jnp.reshape(core, (1,)), grads, rows, total)
+
+
+def late_features(grads, rows, total):
+    examples, columns = total.shape
+    shape = (examples, columns)
     in_vmem = pl.BlockSpec(memory_space=pltpu.VMEM)
     return pl.pallas_call(
         late_features_kernel,
@@ -246,13 +270,13 @@
     diagonal = jnp.sum(jnp.where(rows == cols, under, 0.0), axis=0, keepdims=True)
     last = row_ref[...] + jnp.concatenate([diagonal, jnp.zeros((1, 128 - HALF), jnp.float32)], axis=1)
     piece = jnp.concatenate([body, jnp.broadcast_to(last, (8, 128))], axis=0)
-    out_ref[...] = jnp.broadcast_to(piece[None], out_ref.shape)
+    out_ref[...] = piece
 
 
 def packed_gram(blocks, row):
     return pl.pallas_call(
         packed_gram_kernel,
-        out_shape=jax.ShapeDtypeStruct((blocks.shape[0], HALF // 2 + 8, 128), jnp.float32),
+        out_shape=jax.ShapeDtypeStruct((HALF // 2 + 8, 128), jnp.float32),
         compiler_params=pltpu.CompilerParams(vmem_limit_bytes=16 << 20),
         name="packed_gram",
     )(blocks, row)
@@ -397,18 +421,22 @@
     grads = swap(wire, "ex").reshape(example_count, owned * 2 * rank)
     rows = projection.reshape(owned, 4 * rank, K)
     total = early_features(moved, offset, queries, rows)
-    partial_sums = late_features(grads, rows, total, devices)
-    if partial_sums.ndim == 2:
-        partial_sums = partial_sums.reshape(example_count, devices, K // devices).transpose(1, 0, 2)
-    arrived = swap(partial_sums, EVERY)
 
     slot = lax.axis_index("ex") * ex_rows
     mine = jnp.where(lax.axis_index("param") == 0, domains, 0).astype(single_float)
     domain_row = lax.dynamic_update_slice(jnp.zeros((example_count,), single_float), mine, (slot,))
     if packs(example_count):
         row = jnp.pad(domain_row, (HALF, 128 - HALF - example_count))[None]
-        pieces = swap(packed_gram(arrived, row), EVERY)
+        core = lax.rem(lax.axis_index("ex"), 2)
+        own, other = late_features_paired(grads, rows, total, core, devices // 2)
+        own = (own + flip(other, 1)).astype(jnp.bfloat16)
+        piece = packed_gram(swap(own, EVERY, 2), row)
+        piece = piece + flip(piece, 1)
+        pieces = swap(jnp.broadcast_to(piece[None], (devices // 2, *piece.shape)), EVERY, 2)
     else:
+        partial_sums = late_features(grads, rows, total)
+        partial_sums = partial_sums.reshape(example_count, devices, K // devices).transpose(1, 0, 2)
+        arrived = swap(partial_sums, EVERY)
         features = jnp.sum(arrived.astype(single_float), axis=0)
         gram = exact_dot(features, features, ((1,), (1,)))
         gram = jnp.concatenate([gram, jnp.broadcast_to(domain_row, (devices, example_count))], axis=0)

time: 103 us -> 98.2 us (0.953)
  waiting for transfers between devices: 23.8 us -> 20.2 us
  blocking collectives: 24.5 us -> 21.4 us
  starting transfers between devices: 16.9 us -> 18.4 us
    all_to_all x3, waiting for transfers between devices: 19.9 us -> 14.8 us  [swap(): lax.all_to_all(blocks, axes, split_axis=0, concat_axis=0, axis_index_grou...]
    all_to_all x1, blocking collectives: 15.5 us -> 12.4 us  [swap(): lax.all_to_all(blocks, axes, split_axis=0, concat_axis=0, axis_index_grou...]
    ppermute x4 -> x6, waiting for transfers between devices: 3.84 us -> 5.42 us  [flip(): lax.ppermute(array, 'ex', [(i, i ^ bits) for i in range(lax.axis_size('ex...]
    all_to_all x3, starting transfers between devices: 12.4 us -> 13.8 us  [swap(): lax.all_to_all(blocks, axes, split_axis=0, concat_axis=0, axis_index_grou...]
    ppermute x4 -> x6, starting transfers between devices: 4.46 us -> 4.56 us  [flip(): lax.ppermute(array, 'ex', [(i, i ^ bits) for i in range(lax.axis_size('ex...]
  transfers between devices with their start and end apart: 7 -> 9, of which waited for: 4 -> 6; matrix products, arithmetic and copies ran while one was open for 3% -> 3% of each run, Pallas kernels for 13% -> 14%
where the time goes in v6:
time: 98.2 us; the launch traced here: 97.6 us
  Pallas kernels  30 us (31%)
  blocking collectives  21.4 us (22%)
  waiting for transfers between devices  20.2 us (21%)
  starting transfers between devices  18.4 us (19%)
  local copies, waits for them, and re-layouts  3.28 us (3%)
  matrix products  2.74 us (3%)
    all_to_all x3, waiting for transfers between devices, swap(): lax.all_to_all(blocks, axes, split_axis=0, concat_axis=0, axis_index_grou...  14.8 us
    all_to_all x3, starting transfers between devices, swap(): lax.all_to_all(blocks, axes, split_axis=0, concat_axis=0, axis_index_grou...  13.8 us
    all_to_all x1, blocking collectives, swap(): lax.all_to_all(blocks, axes, split_axis=0, concat_axis=0, axis_index_grou...  12.4 us
    pallas_call x1, Pallas kernels, early_features(): pl.pallas_call(functools.partial(early_features_kernel, len(low)), out_sh...  11.5 us
    pallas_call x1, Pallas kernels, late_features_paired(): pl.pallas_call(late_features_paired_kernel, out_shape=(shape, shape), in_...  11.4 us
    all_gather x1, blocking collectives, local(): low_parts = lax.all_gather(partial_low, 'param')  9 us
    ppermute x6, waiting for transfers between devices, flip(): lax.ppermute(array, 'ex', [(i, i ^ bits) for i in range(lax.axis_size('ex...  5.42 us
    pallas_call x1, Pallas kernels, solve(): pl.pallas_call(functools.partial(solve_kernel, count), out_shape=(jax.Sha...  4.88 us
  transfers between devices with their start and end apart: 9, of which 6 were waited for; matrix products, arithmetic and copies ran while one was open for 3% of the time, Pallas kernels for 14%

profile of v6, /device:TPU:0, one launch (start us, length us, event | category | flops | bytes accessed | tf_op | source)
XLA Modules:
  0.0 97.6 jit_solution(5549833659824512564)
XLA Ops:
  0.6 0.0 copy-start
  0.6 1.0 %copy-done = bf16[8,32,1024]{2,1,0:T(8,128)(2,1)S(1)} copy-done((bf16[8,32,1024]{2,1,0:T(8,128)(2,1)S(1)}, bf16[8,32,1024]{2,1,0:T(8,128)(2,1)}, u32[]{:S(2)}) %copy-start) | copy-done | bytes 524312
  1.7 0.9 bitcast_bitcast_fusion
  2.6 6.3 %all-to-all-start.1 = ((bf16[8,8,32,128]{3,2,1,0:T(8,128)(2,1)}), bf16[8,8,32,128]{3,2,1,0:T(8,128)(2,1)S(1)}, u32[]{:S(2)}, u32[]{:S(2)}) async-start(bf16[8,8,32,128]{3,2,1,0:T(8,128)(2,1)} %bitcast_bitcast_fusion), calls=%async_computation.1 | async-start | bytes 1048576 | tf_op jit(solution)/shard_map/all_to_all | solution.py:30
  8.9 1.1 %fusion.3 = f32[2,16,256]{2,1,0:T(8,128)S(1)} fusion(bf16[2,16,1024]{2,1,0:T(8,128)(2,1)} %param.9, bf16[256,1024,1]{1,0,2:T(8,128)(2,1)S(1)} %bitcast.27), kind=kOutput, calls=%fused_computation.10 | convolution fusion | flops 16777216 | bytes 622592 | tf_op jit(solution)/shard_map/td,ard->art/dot_general | solution.py:400
  10.0 1.7 %fusion.2 = f32[2,16,256]{2,1,0:T(8,128)S(1)} fusion(bf16[2,1024,16]{1,2,0:T(8,128)(2,1)} %param.10, bf16[2,256,1024]{2,1,0:T(8,128)(2,1)} %bitcast.28), kind=kOutput, calls=%fused_computation.9 | convolution fusion | flops 16777216 | bytes 1146880 | tf_op jit(solution)/shard_map/atd,adr->art/dot_general | solution.py:394
  11.7 9.0 %all_gather.3.parts_ref = f32[4,64,256]{2,1,0:T(8,128)S(1)} all-gather(f32[1,64,256]{2,1,0:T(8,128)S(1)} %bitcast.32), channel_id=1, replica_groups=mesh['param'=4,'ex'=8] {'param'}, dimensions={0}, use_global_device_ids=true | all-gather | bytes 327680 | tf_op jit(solution)/shard_map/all_gather | solution.py:407
  20.7 0.1 low_columns.1
  20.8 0.1 collective-permute-start
  20.9 1.2 %collective-permute-done = bf16[1,32,256]{2,1,0:T(8,128)(2,1)S(1)} collective-permute-done((bf16[1,32,256]{2,1,0:T(8,128)(2,1)S(1)}, bf16[1,32,256]{2,1,0:T(8,128)(2,1)S(1)}, u32[]{:S(2)}, u32[]{:S(2)}) %collective-permute-start) | collective-permute-done | bytes 16416 | tf_op jit(solution)/shard_map/ppermute | solution.py:254
  22.0 3.8 %collective-permute-start.3 = (bf16[2,32,256]{2,1,0:T(8,128)(2,1)S(1)}, bf16[2,32,256]{2,1,0:T(8,128)(2,1)S(1)}, u32[]{:S(2)}, u32[]{:S(2)}) collective-permute-start(bf16[2,32,256]{2,1,0:T(8,128)(2,1)S(1)} %constant_dynamic-update-slice_fusion.refs_0_), channel_id=1, source_target_pairs={{0,6},{1,7},{2,4},{3,5},{4,2},{5,3},{6,0},{7,1},{8,14},{9,15},{10,... | collective-permute-start | bytes 98312 | tf_op jit(solution)/shard_map/ppermute | solution.py:254
  25.9 0.0 collective-permute-start.2
  25.9 0.6 collective-permute-start.1
  26.4 0.0 copy-start.1
  26.4 1.2 %copy-done.1 = bf16[2,8,32,1024]{3,2,1,0:T(8,128)(2,1)S(1)} copy-done((bf16[2,8,32,1024]{3,2,1,0:T(8,128)(2,1)S(1)}, bf16[2,8,32,1024]{3,2,1,0:T(8,128)(2,1)}, u32[]{:S(2)}) %copy-start.1) | copy-done | bytes 1048600
  27.6 1.8 %gradient_rows.1 = bf16[8,8,4096]{2,1,0:T(8,128)(2,1)} custom-call(bf16[2,8,32,1024]{3,2,1,0:T(8,128)(2,1)S(1)} %copy-done.1, bf16[256,128]{1,0:T(8,128)(2,1)S(1)} %get-tuple-element.14.low_ref), custom_call_target="tpu_custom_call" | custom-call | tf_op jit(solution)/shard_map/gradient_rows/pallas_call | solution.py:97
  29.5 0.0 collective-permute-done.3.refs_3_
  29.5 1.2 %collective-permute-done.2.refs_2_ = bf16[2,32,256]{2,1,0:T(8,128)(2,1)S(1)} collective-permute-done((bf16[2,32,256]{2,1,0:T(8,128)(2,1)S(1)}, bf16[2,32,256]{2,1,0:T(8,128)(2,1)S(1)}, u32[]{:S(2)}, u32[]{:S(2)}) %collective-permute-start.2) | collective-permute-done | bytes 32800 | tf_op jit(solution)/shard_map/ppermute | solution.py:254
  30.7 0.0 collective-permute-done.1.refs_1_
  30.7 0.0 all-to-all-done.1
  30.7 3.9 %all-to-all-start = ((bf16[8,8,4096]{2,1,0:T(8,128)(2,1)}), bf16[8,8,4096]{2,1,0:T(8,128)(2,1)S(1)}, u32[]{:S(2)}, u32[]{:S(2)}) async-start(bf16[8,8,4096]{2,1,0:T(8,128)(2,1)} %gradient_rows.1), calls=%async_computation | async-start | bytes 1048576 | tf_op jit(solution)/shard_map/all_to_all | solution.py:30
  34.6 0.0 copy-start.3
  34.6 0.0 copy-start.2
  34.6 11.5 %early_features.1.total_ref = f32[64,4096]{1,0:T(8,128)S(1)} custom-call(s32[1]{0:T(128)} %bitcast.8.offset_ref, bf16[64,32,128]{2,1,0:T(8,128)(2,1)S(1)} %bitcast.29, bf16[2,32,256]{2,1,0:T(8,128)(2,1)S(1)} %constant_dynamic-update-slice_fusion.refs_0_, bf16[2,32,256]{2,1,0:T(8,128)(2,1)S(1)} %collective-permute-done.1.refs_1_, ...), custom_call_target="tpu_custom_call" | custom-call | tf_op jit(solution)/shard_map/early_features/pallas_call | solution.py:188
  46.1 3.9 %all-to-all-done = bf16[8,8,4096]{2,1,0:T(8,128)(2,1)S(1)} async-done(((bf16[8,8,4096]{2,1,0:T(8,128)(2,1)}), bf16[8,8,4096]{2,1,0:T(8,128)(2,1)S(1)}, u32[]{:S(2)}, u32[]{:S(2)}) %all-to-all-start) | async-done | bytes 524320 | tf_op jit(solution)/shard_map/all_to_all | solution.py:30
  50.0 11.4 %late_features.1 = (f32[16,64,128]{2,1,0:T(8,128)S(1)}, f32[16,64,128]{2,1,0:T(8,128)S(1)}) custom-call(s32[1]{0:T(128)} %bitcast.1.core_ref, bf16[64,4096]{1,0:T(8,128)(2,1)S(1)} %bitcast.30, bf16[128,64,4096]{2,1,0:T(8,128)(2,1)} %bitcast.7.refs_4_.rows_ref, f32[64,4096]{1,0:T(8,128)S(1)} %early_features.1.total_ref), custom_call_target="tpu_custom_call" | custom-call | tf_op jit(solution)/shard_map/late_features/pallas_call | solution.py:227
  61.4 0.1 collective-permute-start.4
  61.5 1.9 %collective-permute-done.4 = f32[16,64,128]{2,1,0:T(8,128)S(1)} collective-permute-done((f32[16,64,128]{2,1,0:T(8,128)S(1)}, f32[16,64,128]{2,1,0:T(8,128)S(1)}, u32[]{:S(2)}, u32[]{:S(2)}) %collective-permute-start.4) | collective-permute-done | bytes 524320 | tf_op jit(solution)/shard_map/ppermute | solution.py:254
  63.4 0.8 add_convert_fusion
  64.2 3.6 %all-to-all-start.2 = ((bf16[16,64,128]{2,1,0:T(8,128)(2,1)}), bf16[16,64,128]{2,1,0:T(8,128)(2,1)S(1)}, u32[]{:S(2)}, u32[]{:S(2)}) async-start(bf16[16,64,128]{2,1,0:T(8,128)(2,1)} %add_convert_fusion), calls=%async_computation.2 | async-start | bytes 524288 | tf_op jit(solution)/shard_map/all_to_all | solution.py:30
  67.8 0.0 copy-done.3
  67.8 0.1 fusion.1
  67.9 0.1 pad_bitcast_fusion.row_ref
  68.0 10.9 %all-to-all-done.2.blocks_ref = bf16[16,64,128]{2,1,0:T(8,128)(2,1)S(1)} async-done(((bf16[16,64,128]{2,1,0:T(8,128)(2,1)}), bf16[16,64,128]{2,1,0:T(8,128)(2,1)S(1)}, u32[]{:S(2)}, u32[]{:S(2)}) %all-to-all-start.2) | async-done | bytes 262176 | tf_op jit(solution)/shard_map/all_to_all | solution.py:30
  78.8 0.3 packed_gram.1
  79.2 0.0 collective-permute-start.5
  79.2 1.2 %collective-permute-done.5 = f32[24,128]{1,0:T(8,128)S(1)} collective-permute-done((f32[24,128]{1,0:T(8,128)S(1)}, f32[24,128]{1,0:T(8,128)S(1)}, u32[]{:S(2)}, u32[]{:S(2)}) %collective-permute-start.5) | collective-permute-done | bytes 12320 | tf_op jit(solution)/shard_map/ppermute | solution.py:254
  80.4 12.4 %all_to_all.20.pieces_ref = f32[16,24,128]{2,1,0:T(8,128)S(1)} all-to-all(f32[16,24,128]{2,1,0:T(8,128)S(1)} %broadcast_in_dim.22), channel_id=1, replica_groups={{0,2,4,6,8,10,12,14,16,18,20,22,24,26,28,30},{1,3,5,7,9,11,13,15,17,19,..., dimensions={0} | all-to-all | bytes 393216 | tf_op jit(solution)/shard_map/all_to_all | solution.py:30
  92.8 0.0 copy-done.2
  92.8 4.9 %solve.1 = (f32[8,64]{1,0:T(8,128)}, f32[4,64]{1,0:T(4,128)}) custom-call(s32[1]{0:T(128)} %bitcast.slot_ref, f32[16,24,128]{2,1,0:T(8,128)S(1)} %all_to_all.20.pieces_ref, s32[1,64]{1,0:T(1,128)S(1)} %bitcast.31), custom_call_target="tpu_custom_call" | custom-call | tf_op jit(solution)/shard_map/solve/pallas_call | solution.py:353
  (6 shorter events, 0.0 us)
Async XLA Ops:
  0.6 1.0 %copy-start = (bf16[8,32,1024]{2,1,0:T(8,128)(2,1)S(1)}, bf16[8,32,1024]{2,1,0:T(8,128)(2,1)}, u32[]{:S(2)}) copy-start(bf16[8,32,1024]{2,1,0:T(8,128)(2,1)} %param.7) | copy-start | bytes 1572868
  2.6 28.1 %all-to-all-start.1 = ((bf16[8,8,32,128]{3,2,1,0:T(8,128)(2,1)}), bf16[8,8,32,128]{3,2,1,0:T(8,128)(2,1)S(1)}, u32[]{:S(2)}, u32[]{:S(2)}) async-start(bf16[8,8,32,128]{3,2,1,0:T(8,128)(2,1)} %bitcast_bitcast_fusion), calls=%async_computation.1 | async-start | bytes 1048576 | tf_op jit(solution)/shard_map/all_to_all | solution.py:30
  20.8 1.2 %collective-permute-start = (bf16[1,32,256]{2,1,0:T(8,128)(2,1)S(1)}, bf16[1,32,256]{2,1,0:T(8,128)(2,1)S(1)}, u32[]{:S(2)}, u32[]{:S(2)}) collective-permute-start(bf16[1,32,256]{2,1,0:T(8,128)(2,1)S(1)} %get-tuple-element.13), channel_id=1, source_target_pairs={{0,1},{1,0},{2,3},{3,2},{4,5},{5,4},{6,7},{7,6},{8,9},{9,8},{10,11... | collective-permute-start | bytes 49160 | tf_op jit(solution)/shard_map/ppermute | solution.py:254
  22.0 7.4 %collective-permute-start.3 = (bf16[2,32,256]{2,1,0:T(8,128)(2,1)S(1)}, bf16[2,32,256]{2,1,0:T(8,128)(2,1)S(1)}, u32[]{:S(2)}, u32[]{:S(2)}) collective-permute-start(bf16[2,32,256]{2,1,0:T(8,128)(2,1)S(1)} %constant_dynamic-update-slice_fusion.refs_0_), channel_id=1, source_target_pairs={{0,6},{1,7},{2,4},{3,5},{4,2},{5,3},{6,0},{7,1},{8,14},{9,15},{10,... | collective-permute-start | bytes 98312 | tf_op jit(solution)/shard_map/ppermute | solution.py:254
  25.9 4.8 %collective-permute-start.2 = (bf16[2,32,256]{2,1,0:T(8,128)(2,1)S(1)}, bf16[2,32,256]{2,1,0:T(8,128)(2,1)S(1)}, u32[]{:S(2)}, u32[]{:S(2)}) collective-permute-start(bf16[2,32,256]{2,1,0:T(8,128)(2,1)S(1)} %constant_dynamic-update-slice_fusion.refs_0_), channel_id=1, source_target_pairs={{0,4},{1,5},{2,6},{3,7},{4,0},{5,1},{6,2},{7,3},{8,12},{9,13},{10,... | collective-permute-start | bytes 98312 | tf_op jit(solution)/shard_map/ppermute | solution.py:254
  25.9 4.8 %collective-permute-start.1 = (bf16[2,32,256]{2,1,0:T(8,128)(2,1)S(1)}, bf16[2,32,256]{2,1,0:T(8,128)(2,1)S(1)}, u32[]{:S(2)}, u32[]{:S(2)}) collective-permute-start(bf16[2,32,256]{2,1,0:T(8,128)(2,1)S(1)} %constant_dynamic-update-slice_fusion.refs_0_), channel_id=1, source_target_pairs={{0,2},{1,3},{2,0},{3,1},{4,6},{5,7},{6,4},{7,5},{8,10},{9,11},{10,... | collective-permute-start | bytes 98312 | tf_op jit(solution)/shard_map/ppermute | solution.py:254
  26.4 1.2 %copy-start.1 = (bf16[2,8,32,1024]{3,2,1,0:T(8,128)(2,1)S(1)}, bf16[2,8,32,1024]{3,2,1,0:T(8,128)(2,1)}, u32[]{:S(2)}) copy-start(bf16[2,8,32,1024]{3,2,1,0:T(8,128)(2,1)} %out_ref.1) | copy-start | bytes 3145732
  30.7 19.3 %all-to-all-start = ((bf16[8,8,4096]{2,1,0:T(8,128)(2,1)}), bf16[8,8,4096]{2,1,0:T(8,128)(2,1)S(1)}, u32[]{:S(2)}, u32[]{:S(2)}) async-start(bf16[8,8,4096]{2,1,0:T(8,128)(2,1)} %gradient_rows.1), calls=%async_computation | async-start | bytes 1048576 | tf_op jit(solution)/shard_map/all_to_all | solution.py:30
  34.6 33.2 %copy-start.3 = (s32[8]{0:T(128)S(1)}, s32[8]{0:T(128)}, u32[]{:S(2)}) copy-start(s32[8]{0:T(128)} %param.12) | copy-start | bytes 100
  34.6 58.2 %copy-start.2 = (s32[64]{0:T(128)S(1)}, s32[64]{0:T(128)}, u32[]{:S(2)}) copy-start(s32[64]{0:T(128)} %param.13) | copy-start | bytes 772
  61.4 2.0 %collective-permute-start.4 = (f32[16,64,128]{2,1,0:T(8,128)S(1)}, f32[16,64,128]{2,1,0:T(8,128)S(1)}, u32[]{:S(2)}, u32[]{:S(2)}) collective-permute-start(f32[16,64,128]{2,1,0:T(8,128)S(1)} %get-tuple-element.21), channel_id=1, source_target_pairs={{0,1},{1,0},{2,3},{3,2},{4,5},{5,4},{6,7},{7,6},{8,9},{9,8},{10,11... | collective-permute-start | bytes 1572872 | tf_op jit(solution)/shard_map/ppermute | solution.py:254
  64.2 14.7 %all-to-all-start.2 = ((bf16[16,64,128]{2,1,0:T(8,128)(2,1)}), bf16[16,64,128]{2,1,0:T(8,128)(2,1)S(1)}, u32[]{:S(2)}, u32[]{:S(2)}) async-start(bf16[16,64,128]{2,1,0:T(8,128)(2,1)} %add_convert_fusion), calls=%async_computation.2 | async-start | bytes 524288 | tf_op jit(solution)/shard_map/all_to_all | solution.py:30
  79.2 1.2 %collective-permute-start.5 = (f32[24,128]{1,0:T(8,128)S(1)}, f32[24,128]{1,0:T(8,128)S(1)}, u32[]{:S(2)}, u32[]{:S(2)}) collective-permute-start(f32[24,128]{1,0:T(8,128)S(1)} %packed_gram.1), channel_id=1, source_target_pairs={{0,1},{1,0},{2,3},{3,2},{4,5},{5,4},{6,7},{7,6},{8,9},{9,8},{10,11... | collective-permute-start | bytes 36872 | tf_op jit(solution)/shard_map/ppermute | solution.py:254

commit v7 on v6

--- a/solution.py
+++ b/solution.py
@@ -28,6 +28,50 @@
     if groups > 1:
         members = [list(range(i, groups * blocks.shape[0], groups)) for i in range(groups)]
     return lax.all_to_all(blocks, axes, split_axis=0, concat_axis=0, axis_index_groups=members, tiled=True)
+
+
+def first_sums_kernel(blocked, *refs):
+    sources, low_ref, wire_ref = refs[:4], refs[4], refs[5 : 5 + blocked]
+    held, sems = refs[5 + blocked : -1], refs[-1]
+    copies = [pltpu.make_async_copy(source, here, sems.at[i]) for i, (source, here) in enumerate(zip(sources, held))]
+    for copy in copies:
+        copy.start()
+    act_ref, out_ref, down_ref, up_ref = held
+    examples, tokens, channels = act_ref.shape
+    copies[0].wait()
+    for wire in wire_ref:
+        owned = wire.shape[3]
+        for block in range(wire.shape[0]):
+            wire[block] = act_ref[:, :, block * owned : (block + 1) * owned]
+    for copy in copies[1:]:
+        copy.wait()
+    rank = down_ref.shape[1]
+    inputs = act_ref[...].reshape(examples * tokens, channels)
+    pairs = [(up_ref[i], out_ref[i].reshape(examples * tokens, channels)) for i in range(2)]
+    pairs += [(down_ref[i], inputs) for i in range(2)]
+    for i, (weight, values) in enumerate(pairs):
+        low_ref[i * rank : (i + 1) * rank, :] = lax.dot_general(
+            weight, values, (((1,), (1,)), ((), ())), preferred_element_type=jnp.float32
+        )
+
+
+def first_sums(activations, output_gradients, down, up, blocks):
+    examples, tokens, channels = activations.shape
+    out_shape = [jax.ShapeDtypeStruct((4 * down.shape[1], examples * tokens), jnp.float32)]
+    if channels // blocks % 128 == 0:
+        out_shape.append(jax.ShapeDtypeStruct((blocks, examples, tokens, channels // blocks), activations.dtype))
+    operands = (activations, output_gradients, down, up)
+    kept = [pltpu.with_memory_space_constraint(operand, pltpu.HBM) for operand in operands]
+    low, *wire = pl.pallas_call(
+        functools.partial(first_sums_kernel, len(out_shape) - 1),
+        out_shape=out_shape,
+        in_specs=[pl.BlockSpec(memory_space=pltpu.HBM)] * 4,
+        scratch_shapes=[pltpu.VMEM(operand.shape, operand.dtype) for operand in operands]
+        + [pltpu.SemaphoreType.DMA((4,))],
+        compiler_params=pltpu.CompilerParams(vmem_limit_bytes=16 << 20),
+        name="first_sums",
+    )(*kept)
+    return (wire[0] if wire else None), low
 
 
 def spread(columns):
@@ -388,22 +432,13 @@
     channels = activations.shape[2]
     owned = channels // ex_size
 
-    wire = activations.reshape(ex_rows, tokens, ex_size, owned).transpose(2, 0, 1, 3)
+    wire, partial_low = first_sums(
+        activations, output_gradients, down_projection_weight, adapter_up.swapaxes(1, 2), ex_size
+    )
+    if wire is None:
+        wire = activations.reshape(ex_rows, tokens, ex_size, owned).transpose(2, 0, 1, 3)
     moved = swap(wire, "ex").reshape(example_count, tokens, owned)
 
-    up_terms = jnp.einsum(
-        "atd,adr->art",
-        output_gradients.reshape(2, ex_rows * tokens, channels),
-        adapter_up,
-        preferred_element_type=single_float,
-    )
-    down_terms = jnp.einsum(
-        "td,ard->art",
-        activations.reshape(ex_rows * tokens, channels),
-        down_projection_weight,
-        preferred_element_type=single_float,
-    )
-    partial_low = jnp.concatenate([up_terms, down_terms], axis=0).reshape(4 * rank, ex_rows * tokens)
     low_parts = lax.all_gather(partial_low, "param")
     if meets(ex_size):
         queries, rest = low_columns(low_parts, 1)

time: 98.2 us -> 95.7 us (0.975)
  matrix products: 2.74 us -> 0 us
  Pallas kernels: 30 us -> 32.3 us
  local copies, waits for them, and re-layouts: 3.28 us -> 1.34 us
    dot_general x2 -> x0, matrix products: 2.74 us -> none  [the longest x1 1.66 us: local(): jnp.einsum('atd,adr->art', output_gradients.reshape(2, ex_rows * tokens,...]
    pallas_call x0 -> x1, Pallas kernels: none -> 2.23 us  [first_sums(): pl.pallas_call(functools.partial(first_sums_kernel, len(out_shape) - 1),...]
    unnamed x9 -> x7, local copies, waits for them, and re-layouts: 2.28 us -> 1.24 us
  transfers between devices with their start and end apart: 9 -> 9, of which waited for: 6 -> 6; matrix products, arithmetic and copies ran while one was open for 3% -> 0% of each run, Pallas kernels for 14% -> 14%
where the time goes in v7:
time: 95.7 us; the launch traced here: 95.2 us
  Pallas kernels  32.3 us (34%)
  blocking collectives  21.4 us (22%)
  waiting for transfers between devices  20.2 us (21%)
  starting transfers between devices  18.4 us (19%)
  local copies, waits for them, and re-layouts  1.34 us (1%)
    all_to_all x3, waiting for transfers between devices, swap(): lax.all_to_all(blocks, axes, split_axis=0, concat_axis=0, axis_index_grou...  14.7 us
    all_to_all x3, starting transfers between devices, swap(): lax.all_to_all(blocks, axes, split_axis=0, concat_axis=0, axis_index_grou...  13.8 us
    all_to_all x1, blocking collectives, swap(): lax.all_to_all(blocks, axes, split_axis=0, concat_axis=0, axis_index_grou...  12.4 us
    pallas_call x1, Pallas kernels, early_features(): pl.pallas_call(functools.partial(early_features_kernel, len(low)), out_sh...  11.5 us
    pallas_call x1, Pallas kernels, late_features_paired(): pl.pallas_call(late_features_paired_kernel, out_shape=(shape, shape), in_...  11.4 us
    all_gather x1, blocking collectives, local(): low_parts = lax.all_gather(partial_low, 'param')  8.99 us
    ppermute x6, waiting for transfers between devices, flip(): lax.ppermute(array, 'ex', [(i, i ^ bits) for i in range(lax.axis_size('ex...  5.43 us
    pallas_call x1, Pallas kernels, solve(): pl.pallas_call(functools.partial(solve_kernel, count), out_shape=(jax.Sha...  4.88 us
  transfers between devices with their start and end apart: 9, of which 6 were waited for; matrix products, arithmetic and copies ran while one was open for 0% of the time, Pallas kernels for 14%

profile of v7, /device:TPU:0, one launch (start us, length us, event | category | flops | bytes accessed | tf_op | source)
XLA Modules:
  0.0 95.2 jit_solution(15111127243487869426)
XLA Ops:
  0.6 2.2 %first_sums.1 = (f32[64,256]{1,0:T(8,128)S(1)}, bf16[8,8,32,128]{3,2,1,0:T(8,128)(2,1)}) custom-call(bf16[8,32,1024]{2,1,0:T(8,128)(2,1)} %refs_0_.1, bf16[2,8,32,1024]{3,2,1,0:T(8,128)(2,1)} %out_ref.1, bf16[2,16,1024]{2,1,0:T(8,128)(2,1)} %refs_2_.1, bf16[2,16,1024]{2,1,0:T(8,128)(2,1)} %bitcast.17), custom_call_target="tpu_custom_call" | custom-call | tf_op jit(solution)/shard_map/first_sums/pallas_call | solution.py:65
  2.9 6.3 %all-to-all-start.1 = ((bf16[8,8,32,128]{3,2,1,0:T(8,128)(2,1)}), bf16[8,8,32,128]{3,2,1,0:T(8,128)(2,1)S(1)}, u32[]{:S(2)}, u32[]{:S(2)}) async-start(bf16[8,8,32,128]{3,2,1,0:T(8,128)(2,1)} %get-tuple-element.19), calls=%async_computation.1 | async-start | bytes 1048576 | tf_op jit(solution)/shard_map/all_to_all | solution.py:30
  9.2 9.0 %all-gather = f32[256,256]{1,0:T(8,128)S(1)} all-gather(f32[64,256]{1,0:T(8,128)S(1)} %get-tuple-element.15), channel_id=2, replica_groups=mesh['param'=4,'ex'=8] {'param'}, dimensions={0}, use_global_device_ids=true | all-gather | bytes 327680 | tf_op jit(solution)/shard_map/all_gather | solution.py:442
  18.2 0.1 low_columns.1
  18.3 0.1 collective-permute-start
  18.4 1.2 %collective-permute-done = bf16[1,32,256]{2,1,0:T(8,128)(2,1)S(1)} collective-permute-done((bf16[1,32,256]{2,1,0:T(8,128)(2,1)S(1)}, bf16[1,32,256]{2,1,0:T(8,128)(2,1)S(1)}, u32[]{:S(2)}, u32[]{:S(2)}) %collective-permute-start) | collective-permute-done | bytes 16416 | tf_op jit(solution)/shard_map/ppermute | solution.py:298
  19.6 3.8 %collective-permute-start.3 = (bf16[2,32,256]{2,1,0:T(8,128)(2,1)S(1)}, bf16[2,32,256]{2,1,0:T(8,128)(2,1)S(1)}, u32[]{:S(2)}, u32[]{:S(2)}) collective-permute-start(bf16[2,32,256]{2,1,0:T(8,128)(2,1)S(1)} %constant_dynamic-update-slice_fusion.refs_0_), channel_id=1, source_target_pairs={{0,6},{1,7},{2,4},{3,5},{4,2},{5,3},{6,0},{7,1},{8,14},{9,15},{10,... | collective-permute-start | bytes 98312 | tf_op jit(solution)/shard_map/ppermute | solution.py:298
  23.4 0.0 collective-permute-start.2
  23.4 0.6 collective-permute-start.1
  23.9 0.0 copy-start
  23.9 1.2 %copy-done = bf16[2,8,32,1024]{3,2,1,0:T(8,128)(2,1)S(1)} copy-done((bf16[2,8,32,1024]{3,2,1,0:T(8,128)(2,1)S(1)}, bf16[2,8,32,1024]{3,2,1,0:T(8,128)(2,1)}, u32[]{:S(2)}) %copy-start) | copy-done | bytes 1048600
  25.2 1.8 %gradient_rows.1 = bf16[8,8,4096]{2,1,0:T(8,128)(2,1)} custom-call(bf16[2,8,32,1024]{3,2,1,0:T(8,128)(2,1)S(1)} %copy-done, bf16[256,128]{1,0:T(8,128)(2,1)S(1)} %get-tuple-element.17.low_ref), custom_call_target="tpu_custom_call" | custom-call | tf_op jit(solution)/shard_map/gradient_rows/pallas_call | solution.py:141
  27.0 0.0 collective-permute-done.3.refs_3_
  27.0 1.2 %collective-permute-done.2.refs_2_ = bf16[2,32,256]{2,1,0:T(8,128)(2,1)S(1)} collective-permute-done((bf16[2,32,256]{2,1,0:T(8,128)(2,1)S(1)}, bf16[2,32,256]{2,1,0:T(8,128)(2,1)S(1)}, u32[]{:S(2)}, u32[]{:S(2)}) %collective-permute-start.2) | collective-permute-done | bytes 32800 | tf_op jit(solution)/shard_map/ppermute | solution.py:298
  28.2 0.0 collective-permute-done.1.refs_1_
  28.2 0.0 all-to-all-done.1
  28.2 3.9 %all-to-all-start = ((bf16[8,8,4096]{2,1,0:T(8,128)(2,1)}), bf16[8,8,4096]{2,1,0:T(8,128)(2,1)S(1)}, u32[]{:S(2)}, u32[]{:S(2)}) async-start(bf16[8,8,4096]{2,1,0:T(8,128)(2,1)} %gradient_rows.1), calls=%async_computation | async-start | bytes 1048576 | tf_op jit(solution)/shard_map/all_to_all | solution.py:30
  32.1 0.0 copy-start.2
  32.1 0.0 copy-start.1
  32.1 11.5 %early_features.1.total_ref = f32[64,4096]{1,0:T(8,128)S(1)} custom-call(s32[1]{0:T(128)} %bitcast.6.offset_ref, bf16[64,32,128]{2,1,0:T(8,128)(2,1)S(1)} %bitcast.13, bf16[2,32,256]{2,1,0:T(8,128)(2,1)S(1)} %constant_dynamic-update-slice_fusion.refs_0_, bf16[2,32,256]{2,1,0:T(8,128)(2,1)S(1)} %collective-permute-done.1.refs_1_, ...), custom_call_target="tpu_custom_call" | custom-call | tf_op jit(solution)/shard_map/early_features/pallas_call | solution.py:232
  43.6 3.9 %all-to-all-done = bf16[8,8,4096]{2,1,0:T(8,128)(2,1)S(1)} async-done(((bf16[8,8,4096]{2,1,0:T(8,128)(2,1)}), bf16[8,8,4096]{2,1,0:T(8,128)(2,1)S(1)}, u32[]{:S(2)}, u32[]{:S(2)}) %all-to-all-start) | async-done | bytes 524320 | tf_op jit(solution)/shard_map/all_to_all | solution.py:30
  47.5 11.4 %late_features.1 = (f32[16,64,128]{2,1,0:T(8,128)S(1)}, f32[16,64,128]{2,1,0:T(8,128)S(1)}) custom-call(s32[1]{0:T(128)} %bitcast.1.core_ref, bf16[64,4096]{1,0:T(8,128)(2,1)S(1)} %bitcast.14, bf16[128,64,4096]{2,1,0:T(8,128)(2,1)} %bitcast.5.refs_4_.rows_ref, f32[64,4096]{1,0:T(8,128)S(1)} %early_features.1.total_ref), custom_call_target="tpu_custom_call" | custom-call | tf_op jit(solution)/shard_map/late_features/pallas_call | solution.py:271
  58.9 0.1 collective-permute-start.4
  59.0 1.9 %collective-permute-done.4 = f32[16,64,128]{2,1,0:T(8,128)S(1)} collective-permute-done((f32[16,64,128]{2,1,0:T(8,128)S(1)}, f32[16,64,128]{2,1,0:T(8,128)S(1)}, u32[]{:S(2)}, u32[]{:S(2)}) %collective-permute-start.4) | collective-permute-done | bytes 524320 | tf_op jit(solution)/shard_map/ppermute | solution.py:298
  60.9 0.8 add_convert_fusion
  61.7 3.6 %all-to-all-start.2 = ((bf16[16,64,128]{2,1,0:T(8,128)(2,1)}), bf16[16,64,128]{2,1,0:T(8,128)(2,1)S(1)}, u32[]{:S(2)}, u32[]{:S(2)}) async-start(bf16[16,64,128]{2,1,0:T(8,128)(2,1)} %add_convert_fusion), calls=%async_computation.2 | async-start | bytes 524288 | tf_op jit(solution)/shard_map/all_to_all | solution.py:30
  65.3 0.0 copy-done.2
  65.3 0.1 fusion.1
  65.4 0.1 pad_bitcast_fusion.row_ref
  65.5 10.9 %all-to-all-done.2.blocks_ref = bf16[16,64,128]{2,1,0:T(8,128)(2,1)S(1)} async-done(((bf16[16,64,128]{2,1,0:T(8,128)(2,1)}), bf16[16,64,128]{2,1,0:T(8,128)(2,1)S(1)}, u32[]{:S(2)}, u32[]{:S(2)}) %all-to-all-start.2) | async-done | bytes 262176 | tf_op jit(solution)/shard_map/all_to_all | solution.py:30
  76.3 0.3 packed_gram.1
  76.7 0.0 collective-permute-start.5
  76.7 1.2 %collective-permute-done.5 = f32[24,128]{1,0:T(8,128)S(1)} collective-permute-done((f32[24,128]{1,0:T(8,128)S(1)}, f32[24,128]{1,0:T(8,128)S(1)}, u32[]{:S(2)}, u32[]{:S(2)}) %collective-permute-start.5) | collective-permute-done | bytes 12320 | tf_op jit(solution)/shard_map/ppermute | solution.py:298
  77.9 12.4 %all_to_all.20.pieces_ref = f32[16,24,128]{2,1,0:T(8,128)S(1)} all-to-all(f32[16,24,128]{2,1,0:T(8,128)S(1)} %broadcast_in_dim.22), channel_id=1, replica_groups={{0,2,4,6,8,10,12,14,16,18,20,22,24,26,28,30},{1,3,5,7,9,11,13,15,17,19,..., dimensions={0} | all-to-all | bytes 393216 | tf_op jit(solution)/shard_map/all_to_all | solution.py:30
  90.3 0.0 copy-done.1
  90.3 4.9 %solve.1 = (f32[8,64]{1,0:T(8,128)}, f32[4,64]{1,0:T(4,128)}) custom-call(s32[1]{0:T(128)} %bitcast.slot_ref, f32[16,24,128]{2,1,0:T(8,128)S(1)} %all_to_all.20.pieces_ref, s32[1,64]{1,0:T(1,128)S(1)} %bitcast.16), custom_call_target="tpu_custom_call" | custom-call | tf_op jit(solution)/shard_map/solve/pallas_call | solution.py:397
  (5 shorter events, 0.0 us)
Async XLA Ops:
  2.9 25.3 %all-to-all-start.1 = ((bf16[8,8,32,128]{3,2,1,0:T(8,128)(2,1)}), bf16[8,8,32,128]{3,2,1,0:T(8,128)(2,1)S(1)}, u32[]{:S(2)}, u32[]{:S(2)}) async-start(bf16[8,8,32,128]{3,2,1,0:T(8,128)(2,1)} %get-tuple-element.19), calls=%async_computation.1 | async-start | bytes 1048576 | tf_op jit(solution)/shard_map/all_to_all | solution.py:30
  18.3 1.2 %collective-permute-start = (bf16[1,32,256]{2,1,0:T(8,128)(2,1)S(1)}, bf16[1,32,256]{2,1,0:T(8,128)(2,1)S(1)}, u32[]{:S(2)}, u32[]{:S(2)}) collective-permute-start(bf16[1,32,256]{2,1,0:T(8,128)(2,1)S(1)} %get-tuple-element.16), channel_id=1, source_target_pairs={{0,1},{1,0},{2,3},{3,2},{4,5},{5,4},{6,7},{7,6},{8,9},{9,8},{10,11... | collective-permute-start | bytes 49160 | tf_op jit(solution)/shard_map/ppermute | solution.py:298
  19.6 7.4 %collective-permute-start.3 = (bf16[2,32,256]{2,1,0:T(8,128)(2,1)S(1)}, bf16[2,32,256]{2,1,0:T(8,128)(2,1)S(1)}, u32[]{:S(2)}, u32[]{:S(2)}) collective-permute-start(bf16[2,32,256]{2,1,0:T(8,128)(2,1)S(1)} %constant_dynamic-update-slice_fusion.refs_0_), channel_id=1, source_target_pairs={{0,6},{1,7},{2,4},{3,5},{4,2},{5,3},{6,0},{7,1},{8,14},{9,15},{10,... | collective-permute-start | bytes 98312 | tf_op jit(solution)/shard_map/ppermute | solution.py:298
  23.4 4.8 %collective-permute-start.2 = (bf16[2,32,256]{2,1,0:T(8,128)(2,1)S(1)}, bf16[2,32,256]{2,1,0:T(8,128)(2,1)S(1)}, u32[]{:S(2)}, u32[]{:S(2)}) collective-permute-start(bf16[2,32,256]{2,1,0:T(8,128)(2,1)S(1)} %constant_dynamic-update-slice_fusion.refs_0_), channel_id=1, source_target_pairs={{0,4},{1,5},{2,6},{3,7},{4,0},{5,1},{6,2},{7,3},{8,12},{9,13},{10,... | collective-permute-start | bytes 98312 | tf_op jit(solution)/shard_map/ppermute | solution.py:298
  23.4 4.8 %collective-permute-start.1 = (bf16[2,32,256]{2,1,0:T(8,128)(2,1)S(1)}, bf16[2,32,256]{2,1,0:T(8,128)(2,1)S(1)}, u32[]{:S(2)}, u32[]{:S(2)}) collective-permute-start(bf16[2,32,256]{2,1,0:T(8,128)(2,1)S(1)} %constant_dynamic-update-slice_fusion.refs_0_), channel_id=1, source_target_pairs={{0,2},{1,3},{2,0},{3,1},{4,6},{5,7},{6,4},{7,5},{8,10},{9,11},{10,... | collective-permute-start | bytes 98312 | tf_op jit(solution)/shard_map/ppermute | solution.py:298
  23.9 1.2 %copy-start = (bf16[2,8,32,1024]{3,2,1,0:T(8,128)(2,1)S(1)}, bf16[2,8,32,1024]{3,2,1,0:T(8,128)(2,1)}, u32[]{:S(2)}) copy-start(bf16[2,8,32,1024]{3,2,1,0:T(8,128)(2,1)} %out_ref.1) | copy-start | bytes 3145732
  28.2 19.3 %all-to-all-start = ((bf16[8,8,4096]{2,1,0:T(8,128)(2,1)}), bf16[8,8,4096]{2,1,0:T(8,128)(2,1)S(1)}, u32[]{:S(2)}, u32[]{:S(2)}) async-start(bf16[8,8,4096]{2,1,0:T(8,128)(2,1)} %gradient_rows.1), calls=%async_computation | async-start | bytes 1048576 | tf_op jit(solution)/shard_map/all_to_all | solution.py:30
  32.1 33.2 %copy-start.2 = (s32[8]{0:T(128)S(1)}, s32[8]{0:T(128)}, u32[]{:S(2)}) copy-start(s32[8]{0:T(128)} %param.12) | copy-start | bytes 100
  32.1 58.2 %copy-start.1 = (s32[64]{0:T(128)S(1)}, s32[64]{0:T(128)}, u32[]{:S(2)}) copy-start(s32[64]{0:T(128)} %param.13) | copy-start | bytes 772
  58.9 2.0 %collective-permute-start.4 = (f32[16,64,128]{2,1,0:T(8,128)S(1)}, f32[16,64,128]{2,1,0:T(8,128)S(1)}, u32[]{:S(2)}, u32[]{:S(2)}) collective-permute-start(f32[16,64,128]{2,1,0:T(8,128)S(1)} %get-tuple-element.25), channel_id=1, source_target_pairs={{0,1},{1,0},{2,3},{3,2},{4,5},{5,4},{6,7},{7,6},{8,9},{9,8},{10,11... | collective-permute-start | bytes 1572872 | tf_op jit(solution)/shard_map/ppermute | solution.py:298
  61.7 14.7 %all-to-all-start.2 = ((bf16[16,64,128]{2,1,0:T(8,128)(2,1)}), bf16[16,64,128]{2,1,0:T(8,128)(2,1)S(1)}, u32[]{:S(2)}, u32[]{:S(2)}) async-start(bf16[16,64,128]{2,1,0:T(8,128)(2,1)} %add_convert_fusion), calls=%async_computation.2 | async-start | bytes 524288 | tf_op jit(solution)/shard_map/all_to_all | solution.py:30
  76.7 1.2 %collective-permute-start.5 = (f32[24,128]{1,0:T(8,128)S(1)}, f32[24,128]{1,0:T(8,128)S(1)}, u32[]{:S(2)}, u32[]{:S(2)}) collective-permute-start(f32[24,128]{1,0:T(8,128)S(1)} %packed_gram.1), channel_id=1, source_target_pairs={{0,1},{1,0},{2,3},{3,2},{4,5},{5,4},{6,7},{7,6},{8,9},{9,8},{10,11... | collective-permute-start | bytes 36872 | tf_op jit(solution)/shard_map/ppermute | solution.py:298

commit v8 on v7

--- a/solution.py
+++ b/solution.py
@@ -313,14 +313,15 @@
     body = jnp.concatenate([across[:quarter], across[quarter:], mixed[:quarter], mixed[quarter:]], axis=1)
     diagonal = jnp.sum(jnp.where(rows == cols, under, 0.0), axis=0, keepdims=True)
     last = row_ref[...] + jnp.concatenate([diagonal, jnp.zeros((1, 128 - HALF), jnp.float32)], axis=1)
-    piece = jnp.concatenate([body, jnp.broadcast_to(last, (8, 128))], axis=0)
-    out_ref[...] = piece
+    for i in range(quarter):
+        out_ref[:, i * 128 : (i + 1) * 128] = body[i : i + 1]
+    out_ref[:, quarter * 128 :] = last
 
 
 def packed_gram(blocks, row):
     return pl.pallas_call(
         packed_gram_kernel,
-        out_shape=jax.ShapeDtypeStruct((HALF // 2 + 8, 128), jnp.float32),
+        out_shape=jax.ShapeDtypeStruct((1, (HALF // 2 + 1) * 128), jnp.float32),
         compiler_params=pltpu.CompilerParams(vmem_limit_bytes=16 << 20),
         name="packed_gram",
     )(blocks, row)
@@ -346,7 +347,8 @@
 def solve_kernel(count, slot_ref, pieces_ref, ids_ref, scores_ref, domain_ref, work_ref):
     total = jnp.sum(pieces_ref[...], axis=0)
     if packs(count):
-        raw_gram, all_domains = unpack(total)
+        total = [total[:, i * 128 : (i + 1) * 128] for i in range(total.shape[1] // 128)]
+        raw_gram, all_domains = unpack(jnp.concatenate(total, axis=0))
     else:
         raw_gram, all_domains = total[:count], total[count : count + 1]
     rows = lax.broadcasted_iota(jnp.int32, (count, count), 0)

time: 95.7 us -> 94.6 us (0.989)
  blocking collectives: 21.4 us -> 20.1 us
    all_to_all x1, blocking collectives: 12.4 us -> 11.1 us  [swap(): lax.all_to_all(blocks, axes, split_axis=0, concat_axis=0, axis_index_grou...]
where the time goes in v8:
time: 94.6 us; the launch traced here: 94.1 us
  Pallas kernels  32.3 us (34%)
  waiting for transfers between devices  20.2 us (21%)
  blocking collectives  20.1 us (21%)
  starting transfers between devices  18.4 us (19%)
  local copies, waits for them, and re-layouts  1.39 us (1%)
    all_to_all x3, waiting for transfers between devices, swap(): lax.all_to_all(blocks, axes, split_axis=0, concat_axis=0, axis_index_grou...  14.7 us
    all_to_all x3, starting transfers between devices, swap(): lax.all_to_all(blocks, axes, split_axis=0, concat_axis=0, axis_index_grou...  13.8 us
    pallas_call x1, Pallas kernels, early_features(): pl.pallas_call(functools.partial(early_features_kernel, len(low)), out_sh...  11.5 us
    pallas_call x1, Pallas kernels, late_features_paired(): pl.pallas_call(late_features_paired_kernel, out_shape=(shape, shape), in_...  11.4 us
    all_to_all x1, blocking collectives, swap(): lax.all_to_all(blocks, axes, split_axis=0, concat_axis=0, axis_index_grou...  11.1 us
    all_gather x1, blocking collectives, local(): low_parts = lax.all_gather(partial_low, 'param')  8.99 us
    ppermute x6, waiting for transfers between devices, flip(): lax.ppermute(array, 'ex', [(i, i ^ bits) for i in range(lax.axis_size('ex...  5.42 us
    pallas_call x1, Pallas kernels, solve(): pl.pallas_call(functools.partial(solve_kernel, count), out_shape=(jax.Sha...  4.94 us
  transfers between devices with their start and end apart: 9, of which 6 were waited for; matrix products, arithmetic and copies ran while one was open for 0% of the time, Pallas kernels for 14%

profile of v8, /device:TPU:0, one launch (start us, length us, event | category | flops | bytes accessed | tf_op | source)
XLA Modules:
  0.0 94.1 jit_solution(14407882397656602781)
XLA Ops:
  0.6 2.2 %first_sums.1 = (f32[64,256]{1,0:T(8,128)S(1)}, bf16[8,8,32,128]{3,2,1,0:T(8,128)(2,1)}) custom-call(bf16[8,32,1024]{2,1,0:T(8,128)(2,1)} %refs_0_.1, bf16[2,8,32,1024]{3,2,1,0:T(8,128)(2,1)} %out_ref.1, bf16[2,16,1024]{2,1,0:T(8,128)(2,1)} %refs_2_.1, bf16[2,16,1024]{2,1,0:T(8,128)(2,1)} %bitcast.17), custom_call_target="tpu_custom_call" | custom-call | tf_op jit(solution)/shard_map/first_sums/pallas_call | solution.py:65
  2.9 6.3 %all-to-all-start.1 = ((bf16[8,8,32,128]{3,2,1,0:T(8,128)(2,1)}), bf16[8,8,32,128]{3,2,1,0:T(8,128)(2,1)S(1)}, u32[]{:S(2)}, u32[]{:S(2)}) async-start(bf16[8,8,32,128]{3,2,1,0:T(8,128)(2,1)} %get-tuple-element.19), calls=%async_computation.1 | async-start | bytes 1048576 | tf_op jit(solution)/shard_map/all_to_all | solution.py:30
  9.2 9.0 %all-gather = f32[256,256]{1,0:T(8,128)S(1)} all-gather(f32[64,256]{1,0:T(8,128)S(1)} %get-tuple-element.15), channel_id=2, replica_groups=mesh['param'=4,'ex'=8] {'param'}, dimensions={0}, use_global_device_ids=true | all-gather | bytes 327680 | tf_op jit(solution)/shard_map/all_gather | solution.py:444
  18.2 0.1 low_columns.1
  18.3 0.1 collective-permute-start
  18.4 1.2 %collective-permute-done = bf16[1,32,256]{2,1,0:T(8,128)(2,1)S(1)} collective-permute-done((bf16[1,32,256]{2,1,0:T(8,128)(2,1)S(1)}, bf16[1,32,256]{2,1,0:T(8,128)(2,1)S(1)}, u32[]{:S(2)}, u32[]{:S(2)}) %collective-permute-start) | collective-permute-done | bytes 16416 | tf_op jit(solution)/shard_map/ppermute | solution.py:298
  19.5 3.8 %collective-permute-start.3 = (bf16[2,32,256]{2,1,0:T(8,128)(2,1)S(1)}, bf16[2,32,256]{2,1,0:T(8,128)(2,1)S(1)}, u32[]{:S(2)}, u32[]{:S(2)}) collective-permute-start(bf16[2,32,256]{2,1,0:T(8,128)(2,1)S(1)} %constant_dynamic-update-slice_fusion.refs_0_), channel_id=1, source_target_pairs={{0,6},{1,7},{2,4},{3,5},{4,2},{5,3},{6,0},{7,1},{8,14},{9,15},{10,... | collective-permute-start | bytes 98312 | tf_op jit(solution)/shard_map/ppermute | solution.py:298
  23.4 0.0 collective-permute-start.2
  23.4 0.6 collective-permute-start.1
  23.9 0.0 copy-start
  23.9 1.2 %copy-done = bf16[2,8,32,1024]{3,2,1,0:T(8,128)(2,1)S(1)} copy-done((bf16[2,8,32,1024]{3,2,1,0:T(8,128)(2,1)S(1)}, bf16[2,8,32,1024]{3,2,1,0:T(8,128)(2,1)}, u32[]{:S(2)}) %copy-start) | copy-done | bytes 1048600
  25.2 1.8 %gradient_rows.1 = bf16[8,8,4096]{2,1,0:T(8,128)(2,1)} custom-call(bf16[2,8,32,1024]{3,2,1,0:T(8,128)(2,1)S(1)} %copy-done, bf16[256,128]{1,0:T(8,128)(2,1)S(1)} %get-tuple-element.17.low_ref), custom_call_target="tpu_custom_call" | custom-call | tf_op jit(solution)/shard_map/gradient_rows/pallas_call | solution.py:141
  27.0 0.0 collective-permute-done.3.refs_3_
  27.0 1.2 %collective-permute-done.2.refs_2_ = bf16[2,32,256]{2,1,0:T(8,128)(2,1)S(1)} collective-permute-done((bf16[2,32,256]{2,1,0:T(8,128)(2,1)S(1)}, bf16[2,32,256]{2,1,0:T(8,128)(2,1)S(1)}, u32[]{:S(2)}, u32[]{:S(2)}) %collective-permute-start.2) | collective-permute-done | bytes 32800 | tf_op jit(solution)/shard_map/ppermute | solution.py:298
  28.2 0.0 collective-permute-done.1.refs_1_
  28.2 0.0 all-to-all-done.1
  28.2 3.9 %all-to-all-start = ((bf16[8,8,4096]{2,1,0:T(8,128)(2,1)}), bf16[8,8,4096]{2,1,0:T(8,128)(2,1)S(1)}, u32[]{:S(2)}, u32[]{:S(2)}) async-start(bf16[8,8,4096]{2,1,0:T(8,128)(2,1)} %gradient_rows.1), calls=%async_computation | async-start | bytes 1048576 | tf_op jit(solution)/shard_map/all_to_all | solution.py:30
  32.1 0.0 copy-start.2
  32.1 0.0 copy-start.1
  32.1 11.5 %early_features.1.total_ref = f32[64,4096]{1,0:T(8,128)S(1)} custom-call(s32[1]{0:T(128)} %bitcast.6.offset_ref, bf16[64,32,128]{2,1,0:T(8,128)(2,1)S(1)} %bitcast.13, bf16[2,32,256]{2,1,0:T(8,128)(2,1)S(1)} %constant_dynamic-update-slice_fusion.refs_0_, bf16[2,32,256]{2,1,0:T(8,128)(2,1)S(1)} %collective-permute-done.1.refs_1_, ...), custom_call_target="tpu_custom_call" | custom-call | tf_op jit(solution)/shard_map/early_features/pallas_call | solution.py:232
  43.6 3.9 %all-to-all-done = bf16[8,8,4096]{2,1,0:T(8,128)(2,1)S(1)} async-done(((bf16[8,8,4096]{2,1,0:T(8,128)(2,1)}), bf16[8,8,4096]{2,1,0:T(8,128)(2,1)S(1)}, u32[]{:S(2)}, u32[]{:S(2)}) %all-to-all-start) | async-done | bytes 524320 | tf_op jit(solution)/shard_map/all_to_all | solution.py:30
  47.5 11.4 %late_features.1 = (f32[16,64,128]{2,1,0:T(8,128)S(1)}, f32[16,64,128]{2,1,0:T(8,128)S(1)}) custom-call(s32[1]{0:T(128)} %bitcast.1.core_ref, bf16[64,4096]{1,0:T(8,128)(2,1)S(1)} %bitcast.14, bf16[128,64,4096]{2,1,0:T(8,128)(2,1)} %bitcast.5.refs_4_.rows_ref, f32[64,4096]{1,0:T(8,128)S(1)} %early_features.1.total_ref), custom_call_target="tpu_custom_call" | custom-call | tf_op jit(solution)/shard_map/late_features/pallas_call | solution.py:271
  58.9 0.1 collective-permute-start.4
  59.0 1.9 %collective-permute-done.4 = f32[16,64,128]{2,1,0:T(8,128)S(1)} collective-permute-done((f32[16,64,128]{2,1,0:T(8,128)S(1)}, f32[16,64,128]{2,1,0:T(8,128)S(1)}, u32[]{:S(2)}, u32[]{:S(2)}) %collective-permute-start.4) | collective-permute-done | bytes 524320 | tf_op jit(solution)/shard_map/ppermute | solution.py:298
  60.9 0.8 add_convert_fusion
  61.7 3.6 %all-to-all-start.2 = ((bf16[16,64,128]{2,1,0:T(8,128)(2,1)}), bf16[16,64,128]{2,1,0:T(8,128)(2,1)S(1)}, u32[]{:S(2)}, u32[]{:S(2)}) async-start(bf16[16,64,128]{2,1,0:T(8,128)(2,1)} %add_convert_fusion), calls=%async_computation.2 | async-start | bytes 524288 | tf_op jit(solution)/shard_map/all_to_all | solution.py:30
  65.3 0.0 copy-done.2
  65.3 0.1 fusion.1
  65.4 0.1 pad_bitcast_fusion.row_ref
  65.4 10.9 %all-to-all-done.2.blocks_ref = bf16[16,64,128]{2,1,0:T(8,128)(2,1)S(1)} async-done(((bf16[16,64,128]{2,1,0:T(8,128)(2,1)}), bf16[16,64,128]{2,1,0:T(8,128)(2,1)S(1)}, u32[]{:S(2)}, u32[]{:S(2)}) %all-to-all-start.2) | async-done | bytes 262176 | tf_op jit(solution)/shard_map/all_to_all | solution.py:30
  76.3 0.3 packed_gram.1
  76.7 0.1 collective-permute-start.5
  76.8 1.2 %collective-permute-done.5 = f32[1,2176]{1,0:T(1,128)S(1)} collective-permute-done((f32[1,2176]{1,0:T(1,128)S(1)}, f32[1,2176]{1,0:T(1,128)S(1)}, u32[]{:S(2)}, u32[]{:S(2)}) %collective-permute-start.5) | collective-permute-done | bytes 8736 | tf_op jit(solution)/shard_map/ppermute | solution.py:298
  77.9 0.1 broadcast_in_dim.25
  78.0 11.1 %all_to_all.20.pieces_ref = f32[16,1,2176]{2,1,0:T(1,128)S(1)} all-to-all(f32[16,1,2176]{2,1,0:T(1,128)S(1)} %broadcast_in_dim.25), channel_id=1, replica_groups={{0,2,4,6,8,10,12,14,16,18,20,22,24,26,28,30},{1,3,5,7,9,11,13,15,17,19,..., dimensions={0} | all-to-all | bytes 278528 | tf_op jit(solution)/shard_map/all_to_all | solution.py:30
  89.2 0.0 copy-done.1
  89.2 4.9 %solve.1 = (f32[8,64]{1,0:T(8,128)}, f32[4,64]{1,0:T(4,128)}) custom-call(s32[1]{0:T(128)} %bitcast.slot_ref, f32[16,1,2176]{2,1,0:T(1,128)S(1)} %all_to_all.20.pieces_ref, s32[1,64]{1,0:T(1,128)S(1)} %bitcast.16), custom_call_target="tpu_custom_call" | custom-call | tf_op jit(solution)/shard_map/solve/pallas_call | solution.py:399
  (4 shorter events, 0.0 us)
Async XLA Ops:
  2.9 25.3 %all-to-all-start.1 = ((bf16[8,8,32,128]{3,2,1,0:T(8,128)(2,1)}), bf16[8,8,32,128]{3,2,1,0:T(8,128)(2,1)S(1)}, u32[]{:S(2)}, u32[]{:S(2)}) async-start(bf16[8,8,32,128]{3,2,1,0:T(8,128)(2,1)} %get-tuple-element.19), calls=%async_computation.1 | async-start | bytes 1048576 | tf_op jit(solution)/shard_map/all_to_all | solution.py:30
  18.3 1.2 %collective-permute-start = (bf16[1,32,256]{2,1,0:T(8,128)(2,1)S(1)}, bf16[1,32,256]{2,1,0:T(8,128)(2,1)S(1)}, u32[]{:S(2)}, u32[]{:S(2)}) collective-permute-start(bf16[1,32,256]{2,1,0:T(8,128)(2,1)S(1)} %get-tuple-element.16), channel_id=1, source_target_pairs={{0,1},{1,0},{2,3},{3,2},{4,5},{5,4},{6,7},{7,6},{8,9},{9,8},{10,11... | collective-permute-start | bytes 49160 | tf_op jit(solution)/shard_map/ppermute | solution.py:298
  19.5 7.4 %collective-permute-start.3 = (bf16[2,32,256]{2,1,0:T(8,128)(2,1)S(1)}, bf16[2,32,256]{2,1,0:T(8,128)(2,1)S(1)}, u32[]{:S(2)}, u32[]{:S(2)}) collective-permute-start(bf16[2,32,256]{2,1,0:T(8,128)(2,1)S(1)} %constant_dynamic-update-slice_fusion.refs_0_), channel_id=1, source_target_pairs={{0,6},{1,7},{2,4},{3,5},{4,2},{5,3},{6,0},{7,1},{8,14},{9,15},{10,... | collective-permute-start | bytes 98312 | tf_op jit(solution)/shard_map/ppermute | solution.py:298
  23.4 4.8 %collective-permute-start.2 = (bf16[2,32,256]{2,1,0:T(8,128)(2,1)S(1)}, bf16[2,32,256]{2,1,0:T(8,128)(2,1)S(1)}, u32[]{:S(2)}, u32[]{:S(2)}) collective-permute-start(bf16[2,32,256]{2,1,0:T(8,128)(2,1)S(1)} %constant_dynamic-update-slice_fusion.refs_0_), channel_id=1, source_target_pairs={{0,4},{1,5},{2,6},{3,7},{4,0},{5,1},{6,2},{7,3},{8,12},{9,13},{10,... | collective-permute-start | bytes 98312 | tf_op jit(solution)/shard_map/ppermute | solution.py:298
  23.4 4.8 %collective-permute-start.1 = (bf16[2,32,256]{2,1,0:T(8,128)(2,1)S(1)}, bf16[2,32,256]{2,1,0:T(8,128)(2,1)S(1)}, u32[]{:S(2)}, u32[]{:S(2)}) collective-permute-start(bf16[2,32,256]{2,1,0:T(8,128)(2,1)S(1)} %constant_dynamic-update-slice_fusion.refs_0_), channel_id=1, source_target_pairs={{0,2},{1,3},{2,0},{3,1},{4,6},{5,7},{6,4},{7,5},{8,10},{9,11},{10,... | collective-permute-start | bytes 98312 | tf_op jit(solution)/shard_map/ppermute | solution.py:298
  23.9 1.2 %copy-start = (bf16[2,8,32,1024]{3,2,1,0:T(8,128)(2,1)S(1)}, bf16[2,8,32,1024]{3,2,1,0:T(8,128)(2,1)}, u32[]{:S(2)}) copy-start(bf16[2,8,32,1024]{3,2,1,0:T(8,128)(2,1)} %out_ref.1) | copy-start | bytes 3145732
  28.2 19.3 %all-to-all-start = ((bf16[8,8,4096]{2,1,0:T(8,128)(2,1)}), bf16[8,8,4096]{2,1,0:T(8,128)(2,1)S(1)}, u32[]{:S(2)}, u32[]{:S(2)}) async-start(bf16[8,8,4096]{2,1,0:T(8,128)(2,1)} %gradient_rows.1), calls=%async_computation | async-start | bytes 1048576 | tf_op jit(solution)/shard_map/all_to_all | solution.py:30
  32.1 33.2 %copy-start.2 = (s32[8]{0:T(128)S(1)}, s32[8]{0:T(128)}, u32[]{:S(2)}) copy-start(s32[8]{0:T(128)} %param.12) | copy-start | bytes 100
  32.1 57.1 %copy-start.1 = (s32[64]{0:T(128)S(1)}, s32[64]{0:T(128)}, u32[]{:S(2)}) copy-start(s32[64]{0:T(128)} %param.13) | copy-start | bytes 772
  58.9 2.0 %collective-permute-start.4 = (f32[16,64,128]{2,1,0:T(8,128)S(1)}, f32[16,64,128]{2,1,0:T(8,128)S(1)}, u32[]{:S(2)}, u32[]{:S(2)}) collective-permute-start(f32[16,64,128]{2,1,0:T(8,128)S(1)} %get-tuple-element.25), channel_id=1, source_target_pairs={{0,1},{1,0},{2,3},{3,2},{4,5},{5,4},{6,7},{7,6},{8,9},{9,8},{10,11... | collective-permute-start | bytes 1572872 | tf_op jit(solution)/shard_map/ppermute | solution.py:298
  61.7 14.7 %all-to-all-start.2 = ((bf16[16,64,128]{2,1,0:T(8,128)(2,1)}), bf16[16,64,128]{2,1,0:T(8,128)(2,1)S(1)}, u32[]{:S(2)}, u32[]{:S(2)}) async-start(bf16[16,64,128]{2,1,0:T(8,128)(2,1)} %add_convert_fusion), calls=%async_computation.2 | async-start | bytes 524288 | tf_op jit(solution)/shard_map/all_to_all | solution.py:30
  76.7 1.2 %collective-permute-start.5 = (f32[1,2176]{1,0:T(1,128)S(1)}, f32[1,2176]{1,0:T(1,128)S(1)}, u32[]{:S(2)}, u32[]{:S(2)}) collective-permute-start(f32[1,2176]{1,0:T(1,128)S(1)} %packed_gram.1), channel_id=1, source_target_pairs={{0,1},{1,0},{2,3},{3,2},{4,5},{5,4},{6,7},{7,6},{8,9},{9,8},{10,11... | collective-permute-start | bytes 26120 | tf_op jit(solution)/shard_map/ppermute | solution.py:298

commit v9 on v8

--- a/solution.py
+++ b/solution.py
@@ -31,12 +31,12 @@
 
 
 def first_sums_kernel(blocked, *refs):
-    sources, low_ref, wire_ref = refs[:4], refs[4], refs[5 : 5 + blocked]
-    held, sems = refs[5 + blocked : -1], refs[-1]
+    sources, low_ref, out_ref, wire_ref = refs[:4], refs[4], refs[5], refs[6 : 6 + blocked]
+    act_ref, down_ref, up_ref, sems = refs[6 + blocked :]
+    held = (act_ref, out_ref, down_ref, up_ref)
     copies = [pltpu.make_async_copy(source, here, sems.at[i]) for i, (source, here) in enumerate(zip(sources, held))]
     for copy in copies:
         copy.start()
-    act_ref, out_ref, down_ref, up_ref = held
     examples, tokens, channels = act_ref.shape
     copies[0].wait()
     for wire in wire_ref:
@@ -57,21 +57,24 @@
 
 def first_sums(activations, output_gradients, down, up, blocks):
     examples, tokens, channels = activations.shape
-    out_shape = [jax.ShapeDtypeStruct((4 * down.shape[1], examples * tokens), jnp.float32)]
+    out_shape = [
+        jax.ShapeDtypeStruct((4 * down.shape[1], examples * tokens), jnp.float32),
+        jax.ShapeDtypeStruct(output_gradients.shape, output_gradients.dtype),
+    ]
     if channels // blocks % 128 == 0:
         out_shape.append(jax.ShapeDtypeStruct((blocks, examples, tokens, channels // blocks), activations.dtype))
     operands = (activations, output_gradients, down, up)
     kept = [pltpu.with_memory_space_constraint(operand, pltpu.HBM) for operand in operands]
-    low, *wire = pl.pallas_call(
-        functools.partial(first_sums_kernel, len(out_shape) - 1),
+    low, held, *wire = pl.pallas_call(
+        functools.partial(first_sums_kernel, len(out_shape) - 2),
         out_shape=out_shape,
         in_specs=[pl.BlockSpec(memory_space=pltpu.HBM)] * 4,
-        scratch_shapes=[pltpu.VMEM(operand.shape, operand.dtype) for operand in operands]
+        scratch_shapes=[pltpu.VMEM(operand.shape, operand.dtype) for operand in (activations, down, up)]
         + [pltpu.SemaphoreType.DMA((4,))],
         compiler_params=pltpu.CompilerParams(vmem_limit_bytes=16 << 20),
         name="first_sums",
     )(*kept)
-    return (wire[0] if wire else None), low
+    return (wire[0] if wire else None), low, held
 
 
 def spread(columns):
@@ -434,7 +437,7 @@
     channels = activations.shape[2]
     owned = channels // ex_size
 
-    wire, partial_low = first_sums(
+    wire, partial_low, held = first_sums(
         activations, output_gradients, down_projection_weight, adapter_up.swapaxes(1, 2), ex_size
     )
     if wire is None:
@@ -453,7 +456,7 @@
         queries = [swap(queries, "ex")]
         offset = jnp.int32(0)
 
-    wire = gradient_rows(output_gradients, rest, ex_size)
+    wire = gradient_rows(held, rest, ex_size)
     queries, wire = lax.optimization_barrier((queries, wire))
     grads = swap(wire, "ex").reshape(example_count, owned * 2 * rank)
     rows = projection.reshape(owned, 4 * rank, K)

time: 94.6 us -> 94.1 us (level)
  local copies, waits for them, and re-layouts: 1.39 us -> 0.17 us
  waiting for transfers between devices: 20.2 us -> 21.2 us
    ppermute x6, waiting for transfers between devices: 5.42 us -> 6.65 us  [flip(): lax.ppermute(array, 'ex', [(i, i ^ bits) for i in range(lax.axis_size('ex...]
    unnamed x7 -> x5, local copies, waits for them, and re-layouts: 1.24 us -> 0.02 us
where the time goes in v9:
time: 94.1 us; the launch traced here: 93.6 us
  Pallas kernels  32.3 us (34%)
  waiting for transfers between devices  21.2 us (23%)
  blocking collectives  20.1 us (21%)
  starting transfers between devices  18.1 us (19%)
    all_to_all x3, waiting for transfers between devices, swap(): lax.all_to_all(blocks, axes, split_axis=0, concat_axis=0, axis_index_grou...  14.5 us
    all_to_all x3, starting transfers between devices, swap(): lax.all_to_all(blocks, axes, split_axis=0, concat_axis=0, axis_index_grou...  13.5 us
    pallas_call x1, Pallas kernels, early_features(): pl.pallas_call(functools.partial(early_features_kernel, len(low)), out_sh...  11.5 us
    pallas_call x1, Pallas kernels, late_features_paired(): pl.pallas_call(late_features_paired_kernel, out_shape=(shape, shape), in_...  11.4 us
    all_to_all x1, blocking collectives, swap(): lax.all_to_all(blocks, axes, split_axis=0, concat_axis=0, axis_index_grou...  11.1 us
    all_gather x1, blocking collectives, local(): low_parts = lax.all_gather(partial_low, 'param')  8.99 us
    ppermute x6, waiting for transfers between devices, flip(): lax.ppermute(array, 'ex', [(i, i ^ bits) for i in range(lax.axis_size('ex...  6.65 us
    pallas_call x1, Pallas kernels, solve(): pl.pallas_call(functools.partial(solve_kernel, count), out_shape=(jax.Sha...  4.94 us
  transfers between devices with their start and end apart: 9, of which 6 were waited for; matrix products, arithmetic and copies ran while one was open for 0% of the time, Pallas kernels for 14%

profile of v9, /device:TPU:0, one launch (start us, length us, event | category | flops | bytes accessed | tf_op | source)
XLA Modules:
  0.0 93.6 jit_solution(16779184066991441198)
XLA Ops:
  0.6 2.2 %first_sums.1 = (f32[64,256]{1,0:T(8,128)S(1)}, bf16[2,8,32,1024]{3,2,1,0:T(8,128)(2,1)S(1)}, bf16[8,8,32,128]{3,2,1,0:T(8,128)(2,1)}) custom-call(bf16[8,32,1024]{2,1,0:T(8,128)(2,1)} %refs_0_.1, bf16[2,8,32,1024]{3,2,1,0:T(8,128)(2,1)} %refs_1_.1, bf16[2,16,1024]{2,1,0:T(8,128)(2,1)} %refs_2_.1, bf16[2,16,1024]{2,1,0:T(8,128)(2,1)} %bitcast.17), custom_call_target="tpu_custom_call" | custom-call | tf_op jit(solution)/shard_map/first_sums/pallas_call | solution.py:68
  2.9 6.3 %all-to-all-start.1 = ((bf16[8,8,32,128]{3,2,1,0:T(8,128)(2,1)}), bf16[8,8,32,128]{3,2,1,0:T(8,128)(2,1)S(1)}, u32[]{:S(2)}, u32[]{:S(2)}) async-start(bf16[8,8,32,128]{3,2,1,0:T(8,128)(2,1)} %get-tuple-element.21), calls=%async_computation.1 | async-start | bytes 1048576 | tf_op jit(solution)/shard_map/all_to_all | solution.py:30
  9.2 9.0 %all-gather = f32[256,256]{1,0:T(8,128)S(1)} all-gather(f32[64,256]{1,0:T(8,128)S(1)} %get-tuple-element.16), channel_id=2, replica_groups=mesh['param'=4,'ex'=8] {'param'}, dimensions={0}, use_global_device_ids=true | all-gather | bytes 327680 | tf_op jit(solution)/shard_map/all_gather | solution.py:447
  18.2 0.1 low_columns.1
  18.3 0.1 collective-permute-start
  18.4 1.2 %collective-permute-done = bf16[1,32,256]{2,1,0:T(8,128)(2,1)S(1)} collective-permute-done((bf16[1,32,256]{2,1,0:T(8,128)(2,1)S(1)}, bf16[1,32,256]{2,1,0:T(8,128)(2,1)S(1)}, u32[]{:S(2)}, u32[]{:S(2)}) %collective-permute-start) | collective-permute-done | bytes 16416 | tf_op jit(solution)/shard_map/ppermute | solution.py:301
  19.5 3.8 %collective-permute-start.3 = (bf16[2,32,256]{2,1,0:T(8,128)(2,1)S(1)}, bf16[2,32,256]{2,1,0:T(8,128)(2,1)S(1)}, u32[]{:S(2)}, u32[]{:S(2)}) collective-permute-start(bf16[2,32,256]{2,1,0:T(8,128)(2,1)S(1)} %constant_dynamic-update-slice_fusion.refs_0_), channel_id=1, source_target_pairs={{0,6},{1,7},{2,4},{3,5},{4,2},{5,3},{6,0},{7,1},{8,14},{9,15},{10,... | collective-permute-start | bytes 98312 | tf_op jit(solution)/shard_map/ppermute | solution.py:301
  23.4 0.0 collective-permute-start.2
  23.4 0.6 collective-permute-start.1
  23.9 1.8 %gradient_rows.1 = bf16[8,8,4096]{2,1,0:T(8,128)(2,1)} custom-call(bf16[2,8,32,1024]{3,2,1,0:T(8,128)(2,1)S(1)} %get-tuple-element.18.out_ref, bf16[256,128]{1,0:T(8,128)(2,1)S(1)} %get-tuple-element.19.low_ref), custom_call_target="tpu_custom_call" | custom-call | tf_op jit(solution)/shard_map/gradient_rows/pallas_call | solution.py:144
  25.7 0.0 collective-permute-done.3.refs_3_
  25.8 2.4 %collective-permute-done.2.refs_2_ = bf16[2,32,256]{2,1,0:T(8,128)(2,1)S(1)} collective-permute-done((bf16[2,32,256]{2,1,0:T(8,128)(2,1)S(1)}, bf16[2,32,256]{2,1,0:T(8,128)(2,1)S(1)}, u32[]{:S(2)}, u32[]{:S(2)}) %collective-permute-start.2) | collective-permute-done | bytes 32800 | tf_op jit(solution)/shard_map/ppermute | solution.py:301
  28.2 0.0 collective-permute-done.1.refs_1_
  28.2 0.0 all-to-all-done.1
  28.2 3.5 %all-to-all-start = ((bf16[8,8,4096]{2,1,0:T(8,128)(2,1)}), bf16[8,8,4096]{2,1,0:T(8,128)(2,1)S(1)}, u32[]{:S(2)}, u32[]{:S(2)}) async-start(bf16[8,8,4096]{2,1,0:T(8,128)(2,1)} %gradient_rows.1), calls=%async_computation | async-start | bytes 1048576 | tf_op jit(solution)/shard_map/all_to_all | solution.py:30
  31.7 0.0 copy-start.1
  31.7 0.0 copy-start
  31.7 11.5 %early_features.1.total_ref = f32[64,4096]{1,0:T(8,128)S(1)} custom-call(s32[1]{0:T(128)} %bitcast.6.offset_ref, bf16[64,32,128]{2,1,0:T(8,128)(2,1)S(1)} %bitcast.13, bf16[2,32,256]{2,1,0:T(8,128)(2,1)S(1)} %constant_dynamic-update-slice_fusion.refs_0_, bf16[2,32,256]{2,1,0:T(8,128)(2,1)S(1)} %collective-permute-done.1.refs_1_, ...), custom_call_target="tpu_custom_call" | custom-call | tf_op jit(solution)/shard_map/early_features/pallas_call | solution.py:235
  43.2 3.8 %all-to-all-done = bf16[8,8,4096]{2,1,0:T(8,128)(2,1)S(1)} async-done(((bf16[8,8,4096]{2,1,0:T(8,128)(2,1)}), bf16[8,8,4096]{2,1,0:T(8,128)(2,1)S(1)}, u32[]{:S(2)}, u32[]{:S(2)}) %all-to-all-start) | async-done | bytes 524320 | tf_op jit(solution)/shard_map/all_to_all | solution.py:30
  47.0 11.4 %late_features.1 = (f32[16,64,128]{2,1,0:T(8,128)S(1)}, f32[16,64,128]{2,1,0:T(8,128)S(1)}) custom-call(s32[1]{0:T(128)} %bitcast.1.core_ref, bf16[64,4096]{1,0:T(8,128)(2,1)S(1)} %bitcast.14, bf16[128,64,4096]{2,1,0:T(8,128)(2,1)} %bitcast.5.refs_4_.rows_ref, f32[64,4096]{1,0:T(8,128)S(1)} %early_features.1.total_ref), custom_call_target="tpu_custom_call" | custom-call | tf_op jit(solution)/shard_map/late_features/pallas_call | solution.py:274
  58.4 0.1 collective-permute-start.4
  58.5 1.9 %collective-permute-done.4 = f32[16,64,128]{2,1,0:T(8,128)S(1)} collective-permute-done((f32[16,64,128]{2,1,0:T(8,128)S(1)}, f32[16,64,128]{2,1,0:T(8,128)S(1)}, u32[]{:S(2)}, u32[]{:S(2)}) %collective-permute-start.4) | collective-permute-done | bytes 524320 | tf_op jit(solution)/shard_map/ppermute | solution.py:301
  60.4 0.8 add_convert_fusion
  61.2 3.7 %all-to-all-start.2 = ((bf16[16,64,128]{2,1,0:T(8,128)(2,1)}), bf16[16,64,128]{2,1,0:T(8,128)(2,1)S(1)}, u32[]{:S(2)}, u32[]{:S(2)}) async-start(bf16[16,64,128]{2,1,0:T(8,128)(2,1)} %add_convert_fusion), calls=%async_computation.2 | async-start | bytes 524288 | tf_op jit(solution)/shard_map/all_to_all | solution.py:30
  64.9 0.0 copy-done.1
  64.9 0.1 fusion.1
  65.0 0.1 pad_bitcast_fusion.row_ref
  65.1 10.7 %all-to-all-done.2.blocks_ref = bf16[16,64,128]{2,1,0:T(8,128)(2,1)S(1)} async-done(((bf16[16,64,128]{2,1,0:T(8,128)(2,1)}), bf16[16,64,128]{2,1,0:T(8,128)(2,1)S(1)}, u32[]{:S(2)}, u32[]{:S(2)}) %all-to-all-start.2) | async-done | bytes 262176 | tf_op jit(solution)/shard_map/all_to_all | solution.py:30
  75.8 0.3 packed_gram.1
  76.2 0.1 collective-permute-start.5
  76.3 1.2 %collective-permute-done.5 = f32[1,2176]{1,0:T(1,128)S(1)} collective-permute-done((f32[1,2176]{1,0:T(1,128)S(1)}, f32[1,2176]{1,0:T(1,128)S(1)}, u32[]{:S(2)}, u32[]{:S(2)}) %collective-permute-start.5) | collective-permute-done | bytes 8736 | tf_op jit(solution)/shard_map/ppermute | solution.py:301
  77.5 0.1 broadcast_in_dim.25
  77.5 11.1 %all_to_all.20.pieces_ref = f32[16,1,2176]{2,1,0:T(1,128)S(1)} all-to-all(f32[16,1,2176]{2,1,0:T(1,128)S(1)} %broadcast_in_dim.25), channel_id=1, replica_groups={{0,2,4,6,8,10,12,14,16,18,20,22,24,26,28,30},{1,3,5,7,9,11,13,15,17,19,..., dimensions={0} | all-to-all | bytes 278528 | tf_op jit(solution)/shard_map/all_to_all | solution.py:30
  88.7 0.0 copy-done
  88.7 4.9 %solve.1 = (f32[8,64]{1,0:T(8,128)}, f32[4,64]{1,0:T(4,128)}) custom-call(s32[1]{0:T(128)} %bitcast.slot_ref, f32[16,1,2176]{2,1,0:T(1,128)S(1)} %all_to_all.20.pieces_ref, s32[1,64]{1,0:T(1,128)S(1)} %bitcast.16), custom_call_target="tpu_custom_call" | custom-call | tf_op jit(solution)/shard_map/solve/pallas_call | solution.py:402
  (4 shorter events, 0.0 us)
Async XLA Ops:
  2.9 25.3 %all-to-all-start.1 = ((bf16[8,8,32,128]{3,2,1,0:T(8,128)(2,1)}), bf16[8,8,32,128]{3,2,1,0:T(8,128)(2,1)S(1)}, u32[]{:S(2)}, u32[]{:S(2)}) async-start(bf16[8,8,32,128]{3,2,1,0:T(8,128)(2,1)} %get-tuple-element.21), calls=%async_computation.1 | async-start | bytes 1048576 | tf_op jit(solution)/shard_map/all_to_all | solution.py:30
  18.3 1.2 %collective-permute-start = (bf16[1,32,256]{2,1,0:T(8,128)(2,1)S(1)}, bf16[1,32,256]{2,1,0:T(8,128)(2,1)S(1)}, u32[]{:S(2)}, u32[]{:S(2)}) collective-permute-start(bf16[1,32,256]{2,1,0:T(8,128)(2,1)S(1)} %get-tuple-element.17), channel_id=1, source_target_pairs={{0,1},{1,0},{2,3},{3,2},{4,5},{5,4},{6,7},{7,6},{8,9},{9,8},{10,11... | collective-permute-start | bytes 49160 | tf_op jit(solution)/shard_map/ppermute | solution.py:301
  19.5 6.2 %collective-permute-start.3 = (bf16[2,32,256]{2,1,0:T(8,128)(2,1)S(1)}, bf16[2,32,256]{2,1,0:T(8,128)(2,1)S(1)}, u32[]{:S(2)}, u32[]{:S(2)}) collective-permute-start(bf16[2,32,256]{2,1,0:T(8,128)(2,1)S(1)} %constant_dynamic-update-slice_fusion.refs_0_), channel_id=1, source_target_pairs={{0,6},{1,7},{2,4},{3,5},{4,2},{5,3},{6,0},{7,1},{8,14},{9,15},{10,... | collective-permute-start | bytes 98312 | tf_op jit(solution)/shard_map/ppermute | solution.py:301
  23.4 4.8 %collective-permute-start.2 = (bf16[2,32,256]{2,1,0:T(8,128)(2,1)S(1)}, bf16[2,32,256]{2,1,0:T(8,128)(2,1)S(1)}, u32[]{:S(2)}, u32[]{:S(2)}) collective-permute-start(bf16[2,32,256]{2,1,0:T(8,128)(2,1)S(1)} %constant_dynamic-update-slice_fusion.refs_0_), channel_id=1, source_target_pairs={{0,4},{1,5},{2,6},{3,7},{4,0},{5,1},{6,2},{7,3},{8,12},{9,13},{10,... | collective-permute-start | bytes 98312 | tf_op jit(solution)/shard_map/ppermute | solution.py:301
  23.4 4.8 %collective-permute-start.1 = (bf16[2,32,256]{2,1,0:T(8,128)(2,1)S(1)}, bf16[2,32,256]{2,1,0:T(8,128)(2,1)S(1)}, u32[]{:S(2)}, u32[]{:S(2)}) collective-permute-start(bf16[2,32,256]{2,1,0:T(8,128)(2,1)S(1)} %constant_dynamic-update-slice_fusion.refs_0_), channel_id=1, source_target_pairs={{0,2},{1,3},{2,0},{3,1},{4,6},{5,7},{6,4},{7,5},{8,10},{9,11},{10,... | collective-permute-start | bytes 98312 | tf_op jit(solution)/shard_map/ppermute | solution.py:301
  28.2 18.8 %all-to-all-start = ((bf16[8,8,4096]{2,1,0:T(8,128)(2,1)}), bf16[8,8,4096]{2,1,0:T(8,128)(2,1)S(1)}, u32[]{:S(2)}, u32[]{:S(2)}) async-start(bf16[8,8,4096]{2,1,0:T(8,128)(2,1)} %gradient_rows.1), calls=%async_computation | async-start | bytes 1048576 | tf_op jit(solution)/shard_map/all_to_all | solution.py:30
  31.7 33.2 %copy-start.1 = (s32[8]{0:T(128)S(1)}, s32[8]{0:T(128)}, u32[]{:S(2)}) copy-start(s32[8]{0:T(128)} %param.12) | copy-start | bytes 100
  31.7 57.0 %copy-start = (s32[64]{0:T(128)S(1)}, s32[64]{0:T(128)}, u32[]{:S(2)}) copy-start(s32[64]{0:T(128)} %param.13) | copy-start | bytes 772
  58.4 2.0 %collective-permute-start.4 = (f32[16,64,128]{2,1,0:T(8,128)S(1)}, f32[16,64,128]{2,1,0:T(8,128)S(1)}, u32[]{:S(2)}, u32[]{:S(2)}) collective-permute-start(f32[16,64,128]{2,1,0:T(8,128)S(1)} %get-tuple-element.27), channel_id=1, source_target_pairs={{0,1},{1,0},{2,3},{3,2},{4,5},{5,4},{6,7},{7,6},{8,9},{9,8},{10,11... | collective-permute-start | bytes 1572872 | tf_op jit(solution)/shard_map/ppermute | solution.py:301
  61.2 14.7 %all-to-all-start.2 = ((bf16[16,64,128]{2,1,0:T(8,128)(2,1)}), bf16[16,64,128]{2,1,0:T(8,128)(2,1)S(1)}, u32[]{:S(2)}, u32[]{:S(2)}) async-start(bf16[16,64,128]{2,1,0:T(8,128)(2,1)} %add_convert_fusion), calls=%async_computation.2 | async-start | bytes 524288 | tf_op jit(solution)/shard_map/all_to_all | solution.py:30
  76.2 1.2 %collective-permute-start.5 = (f32[1,2176]{1,0:T(1,128)S(1)}, f32[1,2176]{1,0:T(1,128)S(1)}, u32[]{:S(2)}, u32[]{:S(2)}) collective-permute-start(f32[1,2176]{1,0:T(1,128)S(1)} %packed_gram.1), channel_id=1, source_target_pairs={{0,1},{1,0},{2,3},{3,2},{4,5},{5,4},{6,7},{7,6},{8,9},{9,8},{10,11... | collective-permute-start | bytes 26120 | tf_op jit(solution)/shard_map/ppermute | solution.py:301

commit v10 on v9

--- a/solution.py
+++ b/solution.py
@@ -264,16 +264,16 @@
         even = acc_ref[:, 2 * pair * lanes : (2 * pair + 1) * lanes]
         odd = acc_ref[:, (2 * pair + 1) * lanes : (2 * pair + 2) * lanes]
         own_ref[pair] = jnp.where(first, even, odd)
-        other_ref[pair] = jnp.where(first, odd, even)
+        other_ref[pair] = jnp.where(first, odd, even).astype(other_ref.dtype)
 
 
 def late_features_paired(grads, rows, total, core, pairs):
     examples, columns = total.shape
     in_vmem = pl.BlockSpec(memory_space=pltpu.VMEM)
-    shape = jax.ShapeDtypeStruct((pairs, examples, columns // pairs // 2), jnp.float32)
+    shape = (pairs, examples, columns // pairs // 2)
     return pl.pallas_call(
         late_features_paired_kernel,
-        out_shape=(shape, shape),
+        out_shape=(jax.ShapeDtypeStruct(shape, jnp.float32), jax.ShapeDtypeStruct(shape, jnp.bfloat16)),
         in_specs=[pl.BlockSpec(memory_space=pltpu.SMEM), in_vmem, pl.BlockSpec(memory_space=pl.ANY), in_vmem],
         out_specs=(in_vmem, in_vmem),
         scratch_shapes=[pltpu.VMEM((examples, columns), jnp.float32)] + held_rows(rows),
@@ -469,7 +469,7 @@
         row = jnp.pad(domain_row, (HALF, 128 - HALF - example_count))[None]
         core = lax.rem(lax.axis_index("ex"), 2)
         own, other = late_features_paired(grads, rows, total, core, devices // 2)
-        own = (own + flip(other, 1)).astype(jnp.bfloat16)
+        own = (own + flip(other, 1).astype(single_float)).astype(jnp.bfloat16)
         piece = packed_gram(swap(own, EVERY, 2), row)
         piece = piece + flip(piece, 1)
         pieces = swap(jnp.broadcast_to(piece[None], (devices // 2, *piece.shape)), EVERY, 2)

time: 94.1 us -> 93.7 us (level)
  no operation moved by 1% of the time
where the time goes in v10:
time: 93.7 us; the launch traced here: 93.3 us
  Pallas kernels  32.3 us (34%)
  waiting for transfers between devices  20.8 us (22%)
  blocking collectives  20.1 us (21%)
  starting transfers between devices  18.1 us (19%)
    all_to_all x3, waiting for transfers between devices, swap(): lax.all_to_all(blocks, axes, split_axis=0, concat_axis=0, axis_index_grou...  14.5 us
    all_to_all x3, starting transfers between devices, swap(): lax.all_to_all(blocks, axes, split_axis=0, concat_axis=0, axis_index_grou...  13.5 us
    pallas_call x1, Pallas kernels, early_features(): pl.pallas_call(functools.partial(early_features_kernel, len(low)), out_sh...  11.5 us
    pallas_call x1, Pallas kernels, late_features_paired(): pl.pallas_call(late_features_paired_kernel, out_shape=(jax.ShapeDtypeStru...  11.4 us
    all_to_all x1, blocking collectives, swap(): lax.all_to_all(blocks, axes, split_axis=0, concat_axis=0, axis_index_grou...  11.1 us
    all_gather x1, blocking collectives, local(): low_parts = lax.all_gather(partial_low, 'param')  8.99 us
    ppermute x6, waiting for transfers between devices, flip(): lax.ppermute(array, 'ex', [(i, i ^ bits) for i in range(lax.axis_size('ex...  6.28 us
    pallas_call x1, Pallas kernels, solve(): pl.pallas_call(functools.partial(solve_kernel, count), out_shape=(jax.Sha...  4.94 us
  transfers between devices with their start and end apart: 9, of which 6 were waited for; matrix products, arithmetic and copies ran while one was open for 0% of the time, Pallas kernels for 14%

profile of v10, /device:TPU:0, one launch (start us, length us, event | category | flops | bytes accessed | tf_op | source)
XLA Modules:
  0.0 93.3 jit_solution(12590467624376448676)
XLA Ops:
  0.6 2.2 %first_sums.1 = (f32[64,256]{1,0:T(8,128)S(1)}, bf16[2,8,32,1024]{3,2,1,0:T(8,128)(2,1)S(1)}, bf16[8,8,32,128]{3,2,1,0:T(8,128)(2,1)}) custom-call(bf16[8,32,1024]{2,1,0:T(8,128)(2,1)} %refs_0_.1, bf16[2,8,32,1024]{3,2,1,0:T(8,128)(2,1)} %refs_1_.1, bf16[2,16,1024]{2,1,0:T(8,128)(2,1)} %refs_2_.1, bf16[2,16,1024]{2,1,0:T(8,128)(2,1)} %bitcast.17), custom_call_target="tpu_custom_call" | custom-call | tf_op jit(solution)/shard_map/first_sums/pallas_call | solution.py:68
  2.9 6.3 %all-to-all-start.1 = ((bf16[8,8,32,128]{3,2,1,0:T(8,128)(2,1)}), bf16[8,8,32,128]{3,2,1,0:T(8,128)(2,1)S(1)}, u32[]{:S(2)}, u32[]{:S(2)}) async-start(bf16[8,8,32,128]{3,2,1,0:T(8,128)(2,1)} %get-tuple-element.21), calls=%async_computation.1 | async-start | bytes 1048576 | tf_op jit(solution)/shard_map/all_to_all | solution.py:30
  9.2 9.0 %all-gather = f32[256,256]{1,0:T(8,128)S(1)} all-gather(f32[64,256]{1,0:T(8,128)S(1)} %get-tuple-element.16), channel_id=2, replica_groups=mesh['param'=4,'ex'=8] {'param'}, dimensions={0}, use_global_device_ids=true | all-gather | bytes 327680 | tf_op jit(solution)/shard_map/all_gather | solution.py:447
  18.2 0.1 low_columns.1
  18.3 0.1 collective-permute-start
  18.4 1.2 %collective-permute-done = bf16[1,32,256]{2,1,0:T(8,128)(2,1)S(1)} collective-permute-done((bf16[1,32,256]{2,1,0:T(8,128)(2,1)S(1)}, bf16[1,32,256]{2,1,0:T(8,128)(2,1)S(1)}, u32[]{:S(2)}, u32[]{:S(2)}) %collective-permute-start) | collective-permute-done | bytes 16416 | tf_op jit(solution)/shard_map/ppermute | solution.py:301
  19.5 3.8 %collective-permute-start.3 = (bf16[2,32,256]{2,1,0:T(8,128)(2,1)S(1)}, bf16[2,32,256]{2,1,0:T(8,128)(2,1)S(1)}, u32[]{:S(2)}, u32[]{:S(2)}) collective-permute-start(bf16[2,32,256]{2,1,0:T(8,128)(2,1)S(1)} %constant_dynamic-update-slice_fusion.refs_0_), channel_id=1, source_target_pairs={{0,6},{1,7},{2,4},{3,5},{4,2},{5,3},{6,0},{7,1},{8,14},{9,15},{10,... | collective-permute-start | bytes 98312 | tf_op jit(solution)/shard_map/ppermute | solution.py:301
  23.4 0.0 collective-permute-start.2
  23.4 0.6 collective-permute-start.1
  23.9 1.8 %gradient_rows.1 = bf16[8,8,4096]{2,1,0:T(8,128)(2,1)} custom-call(bf16[2,8,32,1024]{3,2,1,0:T(8,128)(2,1)S(1)} %get-tuple-element.18.out_ref, bf16[256,128]{1,0:T(8,128)(2,1)S(1)} %get-tuple-element.19.low_ref), custom_call_target="tpu_custom_call" | custom-call | tf_op jit(solution)/shard_map/gradient_rows/pallas_call | solution.py:144
  25.7 0.0 collective-permute-done.3.refs_3_
  25.8 2.4 %collective-permute-done.2.refs_2_ = bf16[2,32,256]{2,1,0:T(8,128)(2,1)S(1)} collective-permute-done((bf16[2,32,256]{2,1,0:T(8,128)(2,1)S(1)}, bf16[2,32,256]{2,1,0:T(8,128)(2,1)S(1)}, u32[]{:S(2)}, u32[]{:S(2)}) %collective-permute-start.2) | collective-permute-done | bytes 32800 | tf_op jit(solution)/shard_map/ppermute | solution.py:301
  28.2 0.0 collective-permute-done.1.refs_1_
  28.2 0.0 all-to-all-done.1
  28.2 3.5 %all-to-all-start = ((bf16[8,8,4096]{2,1,0:T(8,128)(2,1)}), bf16[8,8,4096]{2,1,0:T(8,128)(2,1)S(1)}, u32[]{:S(2)}, u32[]{:S(2)}) async-start(bf16[8,8,4096]{2,1,0:T(8,128)(2,1)} %gradient_rows.1), calls=%async_computation | async-start | bytes 1048576 | tf_op jit(solution)/shard_map/all_to_all | solution.py:30
  31.7 0.0 copy-start.1
  31.7 0.0 copy-start
  31.7 11.5 %early_features.1.total_ref = f32[64,4096]{1,0:T(8,128)S(1)} custom-call(s32[1]{0:T(128)} %bitcast.6.offset_ref, bf16[64,32,128]{2,1,0:T(8,128)(2,1)S(1)} %bitcast.13, bf16[2,32,256]{2,1,0:T(8,128)(2,1)S(1)} %constant_dynamic-update-slice_fusion.refs_0_, bf16[2,32,256]{2,1,0:T(8,128)(2,1)S(1)} %collective-permute-done.1.refs_1_, ...), custom_call_target="tpu_custom_call" | custom-call | tf_op jit(solution)/shard_map/early_features/pallas_call | solution.py:235
  43.2 3.8 %all-to-all-done = bf16[8,8,4096]{2,1,0:T(8,128)(2,1)S(1)} async-done(((bf16[8,8,4096]{2,1,0:T(8,128)(2,1)}), bf16[8,8,4096]{2,1,0:T(8,128)(2,1)S(1)}, u32[]{:S(2)}, u32[]{:S(2)}) %all-to-all-start) | async-done | bytes 524320 | tf_op jit(solution)/shard_map/all_to_all | solution.py:30
  47.0 11.4 %late_features.1 = (f32[16,64,128]{2,1,0:T(8,128)S(1)}, bf16[16,64,128]{2,1,0:T(8,128)(2,1)S(1)}) custom-call(s32[1]{0:T(128)} %bitcast.1.core_ref, bf16[64,4096]{1,0:T(8,128)(2,1)S(1)} %bitcast.14, bf16[128,64,4096]{2,1,0:T(8,128)(2,1)} %bitcast.5.refs_4_.rows_ref, f32[64,4096]{1,0:T(8,128)S(1)} %early_features.1.total_ref), custom_call_target="tpu_custom_call" | custom-call | tf_op jit(solution)/shard_map/late_features/pallas_call | solution.py:274
  58.4 0.1 collective-permute-start.4
  58.5 1.5 %collective-permute-done.4 = bf16[16,64,128]{2,1,0:T(8,128)(2,1)S(1)} collective-permute-done((bf16[16,64,128]{2,1,0:T(8,128)(2,1)S(1)}, bf16[16,64,128]{2,1,0:T(8,128)(2,1)S(1)}, u32[]{:S(2)}, u32[]{:S(2)}) %collective-permute-start.4) | collective-permute-done | bytes 262176 | tf_op jit(solution)/shard_map/ppermute | solution.py:301
  60.0 0.8 add_convert_fusion
  60.8 3.7 %all-to-all-start.2 = ((bf16[16,64,128]{2,1,0:T(8,128)(2,1)}), bf16[16,64,128]{2,1,0:T(8,128)(2,1)S(1)}, u32[]{:S(2)}, u32[]{:S(2)}) async-start(bf16[16,64,128]{2,1,0:T(8,128)(2,1)} %add_convert_fusion), calls=%async_computation.2 | async-start | bytes 524288 | tf_op jit(solution)/shard_map/all_to_all | solution.py:30
  64.5 0.0 copy-done.1
  64.5 0.1 fusion.1
  64.6 0.1 pad_bitcast_fusion.row_ref
  64.7 10.7 %all-to-all-done.2.blocks_ref = bf16[16,64,128]{2,1,0:T(8,128)(2,1)S(1)} async-done(((bf16[16,64,128]{2,1,0:T(8,128)(2,1)}), bf16[16,64,128]{2,1,0:T(8,128)(2,1)S(1)}, u32[]{:S(2)}, u32[]{:S(2)}) %all-to-all-start.2) | async-done | bytes 262176 | tf_op jit(solution)/shard_map/all_to_all | solution.py:30
  75.5 0.3 packed_gram.1
  75.8 0.1 collective-permute-start.5
  75.9 1.2 %collective-permute-done.5 = f32[1,2176]{1,0:T(1,128)S(1)} collective-permute-done((f32[1,2176]{1,0:T(1,128)S(1)}, f32[1,2176]{1,0:T(1,128)S(1)}, u32[]{:S(2)}, u32[]{:S(2)}) %collective-permute-start.5) | collective-permute-done | bytes 8736 | tf_op jit(solution)/shard_map/ppermute | solution.py:301
  77.1 0.1 broadcast_in_dim.25
  77.2 11.1 %all_to_all.20.pieces_ref = f32[16,1,2176]{2,1,0:T(1,128)S(1)} all-to-all(f32[16,1,2176]{2,1,0:T(1,128)S(1)} %broadcast_in_dim.25), channel_id=1, replica_groups={{0,2,4,6,8,10,12,14,16,18,20,22,24,26,28,30},{1,3,5,7,9,11,13,15,17,19,..., dimensions={0} | all-to-all | bytes 278528 | tf_op jit(solution)/shard_map/all_to_all | solution.py:30
  88.3 0.0 copy-done
  88.3 4.9 %solve.1 = (f32[8,64]{1,0:T(8,128)}, f32[4,64]{1,0:T(4,128)}) custom-call(s32[1]{0:T(128)} %bitcast.slot_ref, f32[16,1,2176]{2,1,0:T(1,128)S(1)} %all_to_all.20.pieces_ref, s32[1,64]{1,0:T(1,128)S(1)} %bitcast.16), custom_call_target="tpu_custom_call" | custom-call | tf_op jit(solution)/shard_map/solve/pallas_call | solution.py:402
  (4 shorter events, 0.0 us)
Async XLA Ops:
  2.9 25.3 %all-to-all-start.1 = ((bf16[8,8,32,128]{3,2,1,0:T(8,128)(2,1)}), bf16[8,8,32,128]{3,2,1,0:T(8,128)(2,1)S(1)}, u32[]{:S(2)}, u32[]{:S(2)}) async-start(bf16[8,8,32,128]{3,2,1,0:T(8,128)(2,1)} %get-tuple-element.21), calls=%async_computation.1 | async-start | bytes 1048576 | tf_op jit(solution)/shard_map/all_to_all | solution.py:30
  18.3 1.2 %collective-permute-start = (bf16[1,32,256]{2,1,0:T(8,128)(2,1)S(1)}, bf16[1,32,256]{2,1,0:T(8,128)(2,1)S(1)}, u32[]{:S(2)}, u32[]{:S(2)}) collective-permute-start(bf16[1,32,256]{2,1,0:T(8,128)(2,1)S(1)} %get-tuple-element.17), channel_id=1, source_target_pairs={{0,1},{1,0},{2,3},{3,2},{4,5},{5,4},{6,7},{7,6},{8,9},{9,8},{10,11... | collective-permute-start | bytes 49160 | tf_op jit(solution)/shard_map/ppermute | solution.py:301
  19.5 6.2 %collective-permute-start.3 = (bf16[2,32,256]{2,1,0:T(8,128)(2,1)S(1)}, bf16[2,32,256]{2,1,0:T(8,128)(2,1)S(1)}, u32[]{:S(2)}, u32[]{:S(2)}) collective-permute-start(bf16[2,32,256]{2,1,0:T(8,128)(2,1)S(1)} %constant_dynamic-update-slice_fusion.refs_0_), channel_id=1, source_target_pairs={{0,6},{1,7},{2,4},{3,5},{4,2},{5,3},{6,0},{7,1},{8,14},{9,15},{10,... | collective-permute-start | bytes 98312 | tf_op jit(solution)/shard_map/ppermute | solution.py:301
  23.4 4.8 %collective-permute-start.2 = (bf16[2,32,256]{2,1,0:T(8,128)(2,1)S(1)}, bf16[2,32,256]{2,1,0:T(8,128)(2,1)S(1)}, u32[]{:S(2)}, u32[]{:S(2)}) collective-permute-start(bf16[2,32,256]{2,1,0:T(8,128)(2,1)S(1)} %constant_dynamic-update-slice_fusion.refs_0_), channel_id=1, source_target_pairs={{0,4},{1,5},{2,6},{3,7},{4,0},{5,1},{6,2},{7,3},{8,12},{9,13},{10,... | collective-permute-start | bytes 98312 | tf_op jit(solution)/shard_map/ppermute | solution.py:301
  23.4 4.8 %collective-permute-start.1 = (bf16[2,32,256]{2,1,0:T(8,128)(2,1)S(1)}, bf16[2,32,256]{2,1,0:T(8,128)(2,1)S(1)}, u32[]{:S(2)}, u32[]{:S(2)}) collective-permute-start(bf16[2,32,256]{2,1,0:T(8,128)(2,1)S(1)} %constant_dynamic-update-slice_fusion.refs_0_), channel_id=1, source_target_pairs={{0,2},{1,3},{2,0},{3,1},{4,6},{5,7},{6,4},{7,5},{8,10},{9,11},{10,... | collective-permute-start | bytes 98312 | tf_op jit(solution)/shard_map/ppermute | solution.py:301
  28.2 18.8 %all-to-all-start = ((bf16[8,8,4096]{2,1,0:T(8,128)(2,1)}), bf16[8,8,4096]{2,1,0:T(8,128)(2,1)S(1)}, u32[]{:S(2)}, u32[]{:S(2)}) async-start(bf16[8,8,4096]{2,1,0:T(8,128)(2,1)} %gradient_rows.1), calls=%async_computation | async-start | bytes 1048576 | tf_op jit(solution)/shard_map/all_to_all | solution.py:30
  31.7 32.8 %copy-start.1 = (s32[8]{0:T(128)S(1)}, s32[8]{0:T(128)}, u32[]{:S(2)}) copy-start(s32[8]{0:T(128)} %param.12) | copy-start | bytes 100
  31.7 56.6 %copy-start = (s32[64]{0:T(128)S(1)}, s32[64]{0:T(128)}, u32[]{:S(2)}) copy-start(s32[64]{0:T(128)} %param.13) | copy-start | bytes 772
  58.4 1.6 %collective-permute-start.4 = (bf16[16,64,128]{2,1,0:T(8,128)(2,1)S(1)}, bf16[16,64,128]{2,1,0:T(8,128)(2,1)S(1)}, u32[]{:S(2)}, u32[]{:S(2)}) collective-permute-start(bf16[16,64,128]{2,1,0:T(8,128)(2,1)S(1)} %get-tuple-element.27), channel_id=1, source_target_pairs={{0,1},{1,0},{2,3},{3,2},{4,5},{5,4},{6,7},{7,6},{8,9},{9,8},{10,11... | collective-permute-start | bytes 786440 | tf_op jit(solution)/shard_map/ppermute | solution.py:301
  60.8 14.7 %all-to-all-start.2 = ((bf16[16,64,128]{2,1,0:T(8,128)(2,1)}), bf16[16,64,128]{2,1,0:T(8,128)(2,1)S(1)}, u32[]{:S(2)}, u32[]{:S(2)}) async-start(bf16[16,64,128]{2,1,0:T(8,128)(2,1)} %add_convert_fusion), calls=%async_computation.2 | async-start | bytes 524288 | tf_op jit(solution)/shard_map/all_to_all | solution.py:30
  75.8 1.2 %collective-permute-start.5 = (f32[1,2176]{1,0:T(1,128)S(1)}, f32[1,2176]{1,0:T(1,128)S(1)}, u32[]{:S(2)}, u32[]{:S(2)}) collective-permute-start(f32[1,2176]{1,0:T(1,128)S(1)} %packed_gram.1), channel_id=1, source_target_pairs={{0,1},{1,0},{2,3},{3,2},{4,5},{5,4},{6,7},{7,6},{8,9},{9,8},{10,11... | collective-permute-start | bytes 26120 | tf_op jit(solution)/shard_map/ppermute | solution.py:301
